TPU v7x, 32 devices: a whole 2x2x4 slice. The times are simulated.
32 devices in a mesh: lsec: 4 (over z), rsec: 8 (over y, x, core).
Axes of the slice: x: 2, y: 2, z: 4, core: 2. Of those that a mesh axis runs over, the one named last changes fastest.
Arguments:
- wavefunction: bfloat16 [4096, 4096], P('lsec', 'rsec'), may hold values from -6 to 6
- left_env: bfloat16 [16, 4096, 1024], P(None, 'lsec'), may hold values from -0.1875 to 0.1875
- right_env: bfloat16 [16, 4096, 512], P(None, 'rsec'), may hold values from -0.25 to 0.25
Outputs:
- hpsi: bfloat16 [4096, 4096], P('lsec', 'rsec')
All inputs are finite; a program needn't handle non-finite values.
Results may differ from a plain program's by a relative error of at most 0.0053.
Values may be sent and summed in bfloat16 or wider, within the bound.
No kernel may reach another device: no remote copies, remote signals or barrier semaphores. Data moves between devices by JAX's collectives and lax.ppermute only.
A program may use at most 128 MiB of HBM per device.

v0:
```python
import jax
import jax.numpy as jnp
from jax import lax
from jax.sharding import PartitionSpec as P

channel_shifts = (0, 1, -1, 0)


def shifted(value, axis, steps):
    count = lax.axis_size(axis)
    first, last = (max(0, -steps), min(count, count - steps))
    return lax.ppermute(value, axis, [(source, source + steps) for source in range(first, last)])


def contract(left_block, moved, right_block):
    partial_sum = jnp.dot(left_block, moved, preferred_element_type=jnp.float32).astype(
        jnp.bfloat16
    )
    return jnp.dot(partial_sum, right_block, preferred_element_type=jnp.float32)


def shards(wavefunction, left_env, right_env):
    count = left_env.shape[0]
    from_above = shifted(wavefunction, "lsec", -1)
    from_below = shifted(wavefunction, "lsec", 1)
    total = jnp.zeros(wavefunction.shape, jnp.float32)
    for channel in range(count):
        if channel_shifts[channel % 4] == 0:
            total = total + contract(left_env[channel], wavefunction, right_env[channel])
    upper = [c for c in range(count) if channel_shifts[c % 4] == 1]
    lower = [c for c in range(count) if channel_shifts[c % 4] == -1]
    upper_sum = jnp.zeros(wavefunction.shape, jnp.float32)
    for channel in upper:
        upper_sum = upper_sum + contract(left_env[channel], from_above, right_env[channel])
    lower_sum = jnp.zeros(wavefunction.shape, jnp.float32)
    for channel in lower:
        lower_sum = lower_sum + contract(left_env[channel], from_below, right_env[channel])
    upper_moved = shifted(upper_sum.astype(jnp.bfloat16), "rsec", -1)
    lower_moved = shifted(lower_sum.astype(jnp.bfloat16), "rsec", 1)
    total = total + upper_moved.astype(jnp.float32) + lower_moved.astype(jnp.float32)
    return total.astype(jnp.bfloat16)


def solution(mesh):
    in_specs = (P("lsec", "rsec"), P(None, "lsec", None), P(None, "rsec", None))
    out_specs = P("lsec", "rsec")
    return jax.shard_map(shards, mesh=mesh, in_specs=in_specs, out_specs=out_specs, check_vma=False)
```

profile of v0, /device:TPU:0, one launch (start us, length us, event | category | flops | bytes accessed | tf_op | source)
XLA Modules:
  0.0 106.3 jit_solution(2344801975065931339)
XLA Ops:
  0.0 0.0 copy-start
  0.0 6.1 %collective-permute-start.2 = (bf16[1024,512]{1,0:T(8,128)(2,1)}, bf16[1024,512]{1,0:T(8,128)(2,1)}, u32[]{:S(2)}, u32[]{:S(2)}) collective-permute-start(bf16[1024,512]{1,0:T(8,128)(2,1)} %param.3), channel_id=1, source_target_pairs={{0,8},{8,16},{16,24},{1,9},{9,17},{17,25},{2,10},{10,18},{18,26},{... | collective-permute-start | bytes 3145736 | tf_op jit(solution)/shard_map/ppermute | solution.py:12
  6.1 1.3 %collective-permute-start = (bf16[1024,512]{1,0:T(8,128)(2,1)}, bf16[1024,512]{1,0:T(8,128)(2,1)}, u32[]{:S(2)}, u32[]{:S(2)}) collective-permute-start(bf16[1024,512]{1,0:T(8,128)(2,1)} %param.3), channel_id=1, source_target_pairs={{8,0},{16,8},{24,16},{9,1},{17,9},{25,17},{10,2},{18,10},{26,18},{... | collective-permute-start | bytes 3145736 | tf_op jit(solution)/shard_map/ppermute | solution.py:12
  7.4 3.8 %fusion.115 = f32[1024,512]{1,0:T(8,128)S(1)} fusion(bf16[1024,512]{1,0:T(8,128)(2,1)} %param.3, bf16[16,1024,1024]{2,1,0:T(8,128)(2,1)} %param.4, bf16[16,512,512]{2,1,0:T(8,128)(2,1)} %param.5), kind=kOutput, calls=%fused_computation.73 | convolution fusion | flops 1611137024 | bytes 5767168 | tf_op jit(solution)/shard_map/dot_general | solution.py:19
  11.2 0.0 copy-done
  11.2 4.8 %fusion.118 = f32[1024,512]{1,0:T(8,128)} fusion(bf16[1024,512]{1,0:T(8,128)(2,1)S(1)} %copy-done, bf16[16,1024,1024]{2,1,0:T(8,128)(2,1)} %param.4, bf16[16,512,512]{2,1,0:T(8,128)(2,1)} %param.5), kind=kOutput, calls=%fused_computation.74 | convolution fusion | flops 1611137024 | bytes 5767168 | tf_op jit(solution)/shard_map/dot_general | solution.py:19
  16.0 4.8 %fusion.121 = f32[1024,512]{1,0:T(8,128)} fusion(bf16[1024,512]{1,0:T(8,128)(2,1)S(1)} %copy-done, bf16[16,1024,1024]{2,1,0:T(8,128)(2,1)} %param.4, bf16[16,512,512]{2,1,0:T(8,128)(2,1)} %param.5), kind=kOutput, calls=%fused_computation.75 | convolution fusion | flops 1611137024 | bytes 5767168 | tf_op jit(solution)/shard_map/dot_general | solution.py:19
  20.8 4.8 %fusion.124 = f32[1024,512]{1,0:T(8,128)} fusion(bf16[1024,512]{1,0:T(8,128)(2,1)S(1)} %copy-done, bf16[16,1024,1024]{2,1,0:T(8,128)(2,1)} %param.4, bf16[16,512,512]{2,1,0:T(8,128)(2,1)} %param.5), kind=kOutput, calls=%fused_computation.76 | convolution fusion | flops 1611137024 | bytes 5767168 | tf_op jit(solution)/shard_map/dot_general | solution.py:19
  25.6 7.4 %collective-permute-done = bf16[1024,512]{1,0:T(8,128)(2,1)} collective-permute-done((bf16[1024,512]{1,0:T(8,128)(2,1)}, bf16[1024,512]{1,0:T(8,128)(2,1)}, u32[]{:S(2)}, u32[]{:S(2)}) %collective-permute-start) | collective-permute-done | bytes 1048608 | tf_op jit(solution)/shard_map/ppermute | solution.py:12
  32.9 5.1 %fusion.106 = f32[1024,512]{1,0:T(8,128)} fusion(bf16[1024,512]{1,0:T(8,128)(2,1)} %collective-permute-done, bf16[16,1024,1024]{2,1,0:T(8,128)(2,1)} %param.4, bf16[16,512,512]{2,1,0:T(8,128)(2,1)} %param.5), kind=kOutput, calls=%fused_computation.70 | convolution fusion | flops 1611137024 | bytes 5767168 | tf_op jit(solution)/shard_map/dot_general | solution.py:19
  38.1 5.1 %fusion.109 = f32[1024,512]{1,0:T(8,128)} fusion(bf16[1024,512]{1,0:T(8,128)(2,1)} %collective-permute-done, bf16[16,1024,1024]{2,1,0:T(8,128)(2,1)} %param.4, bf16[16,512,512]{2,1,0:T(8,128)(2,1)} %param.5), kind=kOutput, calls=%fused_computation.71 | convolution fusion | flops 1611137024 | bytes 5767168 | tf_op jit(solution)/shard_map/dot_general | solution.py:19
  43.1 5.2 %fusion.112 = f32[1024,512]{1,0:T(8,128)} fusion(bf16[1024,512]{1,0:T(8,128)(2,1)} %collective-permute-done, bf16[16,1024,1024]{2,1,0:T(8,128)(2,1)} %param.4, bf16[16,512,512]{2,1,0:T(8,128)(2,1)} %param.5), kind=kOutput, calls=%fused_computation.72 | convolution fusion | flops 1611137024 | bytes 5767168 | tf_op jit(solution)/shard_map/dot_general | solution.py:19
  48.3 6.7 %add_convert_fusion.2 = bf16[1024,512]{1,0:T(8,128)(2,1)} fusion(f32[1024,512]{1,0:T(8,128)} %fusion.106, f32[1024,512]{1,0:T(8,128)} %fusion.112, f32[1024,512]{1,0:T(8,128)} %fusion.109, bf16[1024,512]{1,0:T(8,128)(2,1)} %collective-permute-done, bf16[16,1024,1024]{2,1,0:T(8,128)(2,1)} %param.4, bf16[16,512,512]{2,1,0:T(8,128)(2,1)} %param.5), kind=kOutput, calls=%fused_computation.38 | convolution fusion | flops 1613234176 | bytes 11010048 | tf_op jit(solution)/shard_map/dot_general | solution.py:19
  55.0 1.5 %collective-permute-start.1 = (bf16[1024,512]{1,0:T(8,128)(2,1)}, bf16[1024,512]{1,0:T(8,128)(2,1)}, u32[]{:S(2)}, u32[]{:S(2)}) collective-permute-start(bf16[1024,512]{1,0:T(8,128)(2,1)} %add_convert_fusion.2), channel_id=1, source_target_pairs={{1,0},{2,1},{3,2},{4,3},{5,4},{6,5},{7,6},{9,8},{10,9},{11,10},{12... | collective-permute-start | bytes 3145736 | tf_op jit(solution)/shard_map/ppermute | solution.py:12
  56.5 0.0 collective-permute-done.2
  56.5 5.1 %fusion.97 = f32[1024,512]{1,0:T(8,128)} fusion(bf16[1024,512]{1,0:T(8,128)(2,1)} %collective-permute-done.2, bf16[16,1024,1024]{2,1,0:T(8,128)(2,1)} %param.4, bf16[16,512,512]{2,1,0:T(8,128)(2,1)} %param.5), kind=kOutput, calls=%fused_computation.67 | convolution fusion | flops 1611137024 | bytes 5767168 | tf_op jit(solution)/shard_map/dot_general | solution.py:19
  61.6 5.1 %fusion.100 = f32[1024,512]{1,0:T(8,128)} fusion(bf16[1024,512]{1,0:T(8,128)(2,1)} %collective-permute-done.2, bf16[16,1024,1024]{2,1,0:T(8,128)(2,1)} %param.4, bf16[16,512,512]{2,1,0:T(8,128)(2,1)} %param.5), kind=kOutput, calls=%fused_computation.68 | convolution fusion | flops 1611137024 | bytes 5767168 | tf_op jit(solution)/shard_map/dot_general | solution.py:19
  66.7 5.1 %fusion.103 = f32[1024,512]{1,0:T(8,128)} fusion(bf16[1024,512]{1,0:T(8,128)(2,1)} %collective-permute-done.2, bf16[16,1024,1024]{2,1,0:T(8,128)(2,1)} %param.4, bf16[16,512,512]{2,1,0:T(8,128)(2,1)} %param.5), kind=kOutput, calls=%fused_computation.69 | convolution fusion | flops 1611137024 | bytes 5767168 | tf_op jit(solution)/shard_map/dot_general | solution.py:19
  71.8 6.7 %add_convert_fusion.1 = bf16[1024,512]{1,0:T(8,128)(2,1)} fusion(f32[1024,512]{1,0:T(8,128)} %fusion.97, f32[1024,512]{1,0:T(8,128)} %fusion.103, f32[1024,512]{1,0:T(8,128)} %fusion.100, bf16[1024,512]{1,0:T(8,128)(2,1)} %collective-permute-done.2, bf16[16,1024,1024]{2,1,0:T(8,128)(2,1)} %param.4, bf16[16,512,512]{2,1,0:T(8,128)(2,1)} %param.5), kind=kOutput, calls=%fused_computation.33 | convolution fusion | flops 1613234176 | bytes 11010048 | tf_op jit(solution)/shard_map/dot_general | solution.py:19
  78.6 4.0 %collective-permute-start.3 = (bf16[1024,512]{1,0:T(8,128)(2,1)}, bf16[1024,512]{1,0:T(8,128)(2,1)}, u32[]{:S(2)}, u32[]{:S(2)}) collective-permute-start(bf16[1024,512]{1,0:T(8,128)(2,1)} %add_convert_fusion.1), channel_id=1, source_target_pairs={{0,1},{1,2},{2,3},{3,4},{4,5},{5,6},{6,7},{8,9},{9,10},{10,11},{11... | collective-permute-start | bytes 3145736 | tf_op jit(solution)/shard_map/ppermute | solution.py:12
  82.6 4.8 %fusion.127 = f32[1024,512]{1,0:T(8,128)} fusion(bf16[1024,512]{1,0:T(8,128)(2,1)S(1)} %copy-done, bf16[16,1024,1024]{2,1,0:T(8,128)(2,1)} %param.4, bf16[16,512,512]{2,1,0:T(8,128)(2,1)} %param.5), kind=kOutput, calls=%fused_computation.77 | convolution fusion | flops 1611137024 | bytes 5767168 | tf_op jit(solution)/shard_map/dot_general | solution.py:19
  87.4 4.8 %fusion.130 = f32[1024,512]{1,0:T(8,128)} fusion(bf16[1024,512]{1,0:T(8,128)(2,1)S(1)} %copy-done, bf16[16,1024,1024]{2,1,0:T(8,128)(2,1)} %param.4, bf16[16,512,512]{2,1,0:T(8,128)(2,1)} %param.5), kind=kOutput, calls=%fused_computation.78 | convolution fusion | flops 1611137024 | bytes 5767168 | tf_op jit(solution)/shard_map/dot_general | solution.py:19
  92.2 4.8 %fusion.133 = f32[1024,512]{1,0:T(8,128)} fusion(bf16[1024,512]{1,0:T(8,128)(2,1)S(1)} %copy-done, bf16[16,1024,1024]{2,1,0:T(8,128)(2,1)} %param.4, bf16[16,512,512]{2,1,0:T(8,128)(2,1)} %param.5), kind=kOutput, calls=%fused_computation.79 | convolution fusion | flops 1611137024 | bytes 5767168 | tf_op jit(solution)/shard_map/dot_general | solution.py:19
  97.0 0.0 collective-permute-done.1
  97.0 0.0 collective-permute-done.3
  97.0 9.3 %add_convert_fusion = bf16[1024,512]{1,0:T(8,128)(2,1)} fusion(bf16[1024,512]{1,0:T(8,128)(2,1)} %collective-permute-done.3, bf16[1024,512]{1,0:T(8,128)(2,1)} %collective-permute-done.1, f32[1024,512]{1,0:T(8,128)S(1)} %fusion.115, f32[1024,512]{1,0:T(8,128)} %fusion.118, f32[1024,512]{1,0:T(8,128)} %fusion.121, f32[1024,512]{1,0:T(8,128)} %fusion.124, ...), kind=kOutput, calls=%fused_computation.32 | convolution fusion | flops 1617428480 | bytes 21495808 | tf_op jit(solution)/shard_map/dot_general | solution.py:19
Async XLA Ops:
  0.0 11.2 %copy-start = (bf16[1024,512]{1,0:T(8,128)(2,1)S(1)}, bf16[1024,512]{1,0:T(8,128)(2,1)}, u32[]{:S(2)}) copy-start(bf16[1024,512]{1,0:T(8,128)(2,1)} %param.3) | copy-start | bytes 3145732
  0.0 56.5 %collective-permute-start.2 = (bf16[1024,512]{1,0:T(8,128)(2,1)}, bf16[1024,512]{1,0:T(8,128)(2,1)}, u32[]{:S(2)}, u32[]{:S(2)}) collective-permute-start(bf16[1024,512]{1,0:T(8,128)(2,1)} %param.3), channel_id=1, source_target_pairs={{0,8},{8,16},{16,24},{1,9},{9,17},{17,25},{2,10},{10,18},{18,26},{... | collective-permute-start | bytes 3145736 | tf_op jit(solution)/shard_map/ppermute | solution.py:12
  6.1 26.8 %collective-permute-start = (bf16[1024,512]{1,0:T(8,128)(2,1)}, bf16[1024,512]{1,0:T(8,128)(2,1)}, u32[]{:S(2)}, u32[]{:S(2)}) collective-permute-start(bf16[1024,512]{1,0:T(8,128)(2,1)} %param.3), channel_id=1, source_target_pairs={{8,0},{16,8},{24,16},{9,1},{17,9},{25,17},{10,2},{18,10},{26,18},{... | collective-permute-start | bytes 3145736 | tf_op jit(solution)/shard_map/ppermute | solution.py:12
  55.0 42.0 %collective-permute-start.1 = (bf16[1024,512]{1,0:T(8,128)(2,1)}, bf16[1024,512]{1,0:T(8,128)(2,1)}, u32[]{:S(2)}, u32[]{:S(2)}) collective-permute-start(bf16[1024,512]{1,0:T(8,128)(2,1)} %add_convert_fusion.2), channel_id=1, source_target_pairs={{1,0},{2,1},{3,2},{4,3},{5,4},{6,5},{7,6},{9,8},{10,9},{11,10},{12... | collective-permute-start | bytes 3145736 | tf_op jit(solution)/shard_map/ppermute | solution.py:12
  78.6 18.4 %collective-permute-start.3 = (bf16[1024,512]{1,0:T(8,128)(2,1)}, bf16[1024,512]{1,0:T(8,128)(2,1)}, u32[]{:S(2)}, u32[]{:S(2)}) collective-permute-start(bf16[1024,512]{1,0:T(8,128)(2,1)} %add_convert_fusion.1), channel_id=1, source_target_pairs={{0,1},{1,2},{2,3},{3,4},{4,5},{5,6},{6,7},{8,9},{9,10},{10,11},{11... | collective-permute-start | bytes 3145736 | tf_op jit(solution)/shard_map/ppermute | solution.py:12
where the time goes:
time: 107 us; the launch traced here: 106 us
  matrix products  85.9 us (80%)
  starting transfers between devices  12.9 us (12%)
  waiting for transfers between devices  7.39 us (7%)
    dot_general x16, matrix products, contract(): return jnp.dot(partial_sum, right_block, preferred_element_type=jnp.float32)  85.9 us
    ppermute x4, starting transfers between devices, shifted(): lax.ppermute(value, axis, [(source, source + steps) for source in range(f...  12.9 us
    ppermute x4, waiting for transfers between devices, shifted(): lax.ppermute(value, axis, [(source, source + steps) for source in range(f...  7.39 us
  transfers between devices with their start and end apart: 4, of which 1 were waited for; matrix products, arithmetic and copies ran while one was open for 72% of the time, Pallas kernels for 0%

commit v1 on v0

v1 whole, which is shorter than its diff:
```python
import functools

import jax
import jax.numpy as jnp
from jax import lax
from jax.experimental import pallas as pl
from jax.experimental.pallas import tpu as pltpu
from jax.sharding import PartitionSpec as P

channel_shifts = (0, 1, -1, 0)
period = len(channel_shifts)
vmem_bytes = 57 << 20


def contract(left_block, block, right_block):
    partial = jnp.dot(left_block, block, preferred_element_type=jnp.float32)
    return jnp.dot(
        partial.astype(jnp.bfloat16), right_block, preferred_element_type=jnp.float32
    )


def local_channel(step):
    return period * (step // 2) + (period - 1) * (step % 2)


def cost(steps, rows, columns):
    macs = steps * (rows * rows * columns + rows * columns * columns)
    moved = 2 * steps * (rows * rows + columns * columns)
    return pl.CostEstimate(flops=2 * macs, bytes_accessed=moved, transcendentals=0)


def local_kernel(psi_ref, left_ref, right_ref, total_ref):
    term = contract(left_ref[0], psi_ref[...], right_ref[0])

    @pl.when(pl.program_id(0) == 0)
    def _():
        total_ref[...] = term

    @pl.when(pl.program_id(0) > 0)
    def _():
        total_ref[...] += term


def local_terms(psi, left_env, right_env, steps):
    rows, columns = psi.shape
    return pl.pallas_call(
        local_kernel,
        name="local_terms",
        grid=(steps,),
        in_specs=[
            pl.BlockSpec((rows, columns), lambda w: (0, 0)),
            pl.BlockSpec((1, rows, rows), lambda w: (local_channel(w), 0, 0)),
            pl.BlockSpec((1, columns, columns), lambda w: (local_channel(w), 0, 0)),
        ],
        out_specs=pl.BlockSpec((rows, columns), lambda w: (0, 0)),
        out_shape=jax.ShapeDtypeStruct((rows, columns), jnp.float32),
        compiler_params=pltpu.CompilerParams(vmem_limit_bytes=vmem_bytes),
        cost_estimate=cost(steps, rows, columns),
    )(psi, left_env, right_env)


def early_kernel(charged, psi_ref, left_ref, right_ref, after_ref, term_ref, total_ref):
    del charged, after_ref
    step = pl.program_id(0)
    term = contract(left_ref[0], psi_ref[...], right_ref[0])

    @pl.when(step == 0)
    def _():
        total_ref[...] = term

    @pl.when(step > 0)
    def _():
        total_ref[...] += term

    @pl.when(step == pl.num_programs(0) - 1)
    def _():
        term_ref[...] = total_ref[...].astype(term_ref.dtype)


def early_terms(charged, psi, left_env, right_env, after):
    rows, columns = psi.shape
    steps = left_env.shape[0] // period
    pick = lambda w, charged: (period * w + charged[0], 0, 0)
    return pl.pallas_call(
        early_kernel,
        name="early_terms",
        grid_spec=pltpu.PrefetchScalarGridSpec(
            num_scalar_prefetch=1,
            grid=(steps,),
            in_specs=[
                pl.BlockSpec((rows, columns), lambda w, charged: (0, 0)),
                pl.BlockSpec((1, rows, rows), pick),
                pl.BlockSpec((1, columns, columns), pick),
                pl.BlockSpec(memory_space=pl.ANY),
            ],
            out_specs=pl.BlockSpec((rows, columns), lambda w, charged: (0, 0)),
            scratch_shapes=[pltpu.VMEM((rows, columns), jnp.float32)],
        ),
        out_shape=jax.ShapeDtypeStruct((rows, columns), jnp.bfloat16),
        compiler_params=pltpu.CompilerParams(vmem_limit_bytes=vmem_bytes),
        cost_estimate=cost(steps, rows, columns),
    )(charged, psi, left_env, right_env, after)


def rest_kernel(first, local, charged, psi_ref, moved_ref, left_ref, own_ref, partner_ref,
                start_ref, after_ref, total_ref):
    del charged, after_ref
    step = pl.program_id(0)

    @pl.when(step == 0)
    def _():
        total_ref[...] = start_ref[...]

    @pl.when(step < local)
    def _():
        total_ref[...] += contract(left_ref[0], psi_ref[...], own_ref[0])

    @pl.when(step >= local)
    def _():
        total_ref[...] += contract(left_ref[0], moved_ref[...], partner_ref[0])


def rest_terms(charged, psi, moved, left_env, right_env, partner_env, start, after, first):
    rows, columns = psi.shape
    channels = left_env.shape[0]
    local, late = channels // 2 - first, channels // period

    def own(w, charged):
        return (local_channel(first + jnp.minimum(w, local - 1)), 0, 0)

    def partner(w, charged):
        return (period * jnp.maximum(w - local, 0) + charged[0], 0, 0)

    def left(w, charged):
        channel = jnp.where(w < local, own(w, charged)[0], partner(w, charged)[0])
        return (channel, 0, 0)

    whole = pl.BlockSpec((rows, columns), lambda w, charged: (0, 0))
    return pl.pallas_call(
        functools.partial(rest_kernel, first, local),
        name="rest_terms",
        grid_spec=pltpu.PrefetchScalarGridSpec(
            num_scalar_prefetch=1,
            grid=(local + late,),
            in_specs=[
                whole,
                whole,
                pl.BlockSpec((1, rows, rows), left),
                pl.BlockSpec((1, columns, columns), own),
                pl.BlockSpec((1, columns, columns), partner),
                whole,
                pl.BlockSpec(memory_space=pl.ANY),
            ],
            out_specs=whole,
        ),
        out_shape=jax.ShapeDtypeStruct((rows, columns), jnp.float32),
        compiler_params=pltpu.CompilerParams(vmem_limit_bytes=vmem_bytes),
        cost_estimate=cost(local + late, rows, columns),
    )(charged, psi, moved, left_env, right_env, partner_env, start, after)


def pairs(left_count, right_count):
    index = lambda i, j: i * right_count + j
    straight, crossed, partner, along = [], [], [], []
    for i in range(left_count):
        for j in range(right_count):
            step = 1 if j % 2 == 0 else -1
            partner.append((index(i, j + step), index(i, j)))
            if 0 <= i + step < left_count:
                straight.append((index(i + step, j), index(i, j)))
                crossed.append((index(i + step, j + step), index(i, j)))
            if 0 <= j - step < right_count:
                along.append((index(i, j), index(i, j - step)))
    return straight, crossed, partner, along


def shards(left_count, right_count, psi, left_env, right_env):
    axes = ("lsec", "rsec")
    straight, crossed, partner, along = pairs(left_count, right_count)
    charged = jnp.reshape(1 + lax.axis_index("rsec") % 2, (1,)).astype(jnp.int32)
    first = 5
    moved = lax.ppermute(psi, axes, straight)
    partner_env = lax.ppermute(right_env, axes, partner)
    total = local_terms(psi, left_env, right_env, first)
    moved, psi_after, total = lax.optimization_barrier((moved, psi, total))
    moved_across = lax.ppermute(psi_after, axes, crossed)
    early = early_terms(charged, moved, left_env, right_env, total)
    received = lax.ppermute(early, axes, along)
    total = rest_terms(
        charged, psi, moved_across, left_env, right_env, partner_env, total, early, first
    )
    return (total + received.astype(jnp.float32)).astype(jnp.bfloat16)


def solution(mesh):
    in_specs = (P("lsec", "rsec"), P(None, "lsec", None), P(None, "rsec", None))
    out_specs = P("lsec", "rsec")
    body = functools.partial(shards, mesh.shape["lsec"], mesh.shape["rsec"])
    return jax.shard_map(body, mesh=mesh, in_specs=in_specs, out_specs=out_specs, check_vma=False)
```

time: 107 us -> 62.1 us (0.58)
  the two profiles are of different devices: /device:TPU:0 before, /device:TPU:19 now
where the time goes in v1:
time: 62.1 us; the launch traced here: 61.9 us
  Pallas kernels  42.3 us (68%)
  starting transfers between devices  9.61 us (15%)
  waiting for transfers between devices  6.04 us (10%)
  other arithmetic  2.91 us (5%)
  local copies, waits for them, and re-layouts  0.96 us (2%)
    pallas_call x1, Pallas kernels, rest_terms(): pl.pallas_call(functools.partial(rest_kernel, first, local), name='rest_t...  17.8 us
    pallas_call x1, Pallas kernels, local_terms(): pl.pallas_call(local_kernel, name='local_terms', grid=(steps,), in_specs=...  13.4 us
    pallas_call x1, Pallas kernels, early_terms(): pl.pallas_call(early_kernel, name='early_terms', grid_spec=pltpu.Prefetch...  11.1 us
    ppermute x1, waiting for transfers between devices, shards(): received = lax.ppermute(early, axes, along)  6.03 us
    ppermute x1, starting transfers between devices, shards(): received = lax.ppermute(early, axes, along)  3.34 us
    ppermute x1, starting transfers between devices, shards(): moved = lax.ppermute(psi, axes, straight)  3.19 us
    convert_element_type x1, other arithmetic, shards(): return (total + received.astype(jnp.float32)).astype(jnp.bfloat16)  2.91 us
    ppermute x1, starting transfers between devices, shards(): moved_across = lax.ppermute(psi_after, axes, crossed)  2.4 us
  transfers between devices with their start and end apart: 4, of which 1 were waited for; matrix products, arithmetic and copies ran while one was open for 0% of the time, Pallas kernels for 68%

profile of v1, /device:TPU:19, one launch (start us, length us, event | category | flops | bytes accessed | tf_op | source)
XLA Modules:
  0.0 61.9 jit_solution(17054439204260136047)
XLA Ops:
  0.0 0.0 copy-start
  0.0 0.7 %collective-permute-start.2 = (bf16[16,512,512]{2,1,0:T(8,128)(2,1)}, bf16[16,512,512]{2,1,0:T(8,128)(2,1)}, u32[]{:S(2)}, u32[]{:S(2)}) collective-permute-start(bf16[16,512,512]{2,1,0:T(8,128)(2,1)} %own_ref.1), channel_id=1, source_target_pairs={{1,0},{0,1},{3,2},{2,3},{5,4},{4,5},{7,6},{6,7},{9,8},{8,9},{11,10... | collective-permute-start | bytes 25165832 | tf_op jit(solution)/shard_map/ppermute | solution.py:183
  0.7 3.2 %collective-permute-start = (bf16[1024,512]{1,0:T(8,128)(2,1)}, bf16[1024,512]{1,0:T(8,128)(2,1)S(1)}, u32[]{:S(2)}, u32[]{:S(2)}) collective-permute-start(bf16[1024,512]{1,0:T(8,128)(2,1)} %psi_ref.3), channel_id=1, source_target_pairs={{8,0},{10,2},{12,4},{14,6},{16,8},{1,9},{18,10},{3,11},{20,12},{5,... | collective-permute-start | bytes 3145736 | tf_op jit(solution)/shard_map/ppermute | solution.py:182
  3.9 13.4 %local_terms.1.after_ref.start_ref = f32[1024,512]{1,0:T(8,128)} custom-call(bf16[1024,512]{1,0:T(8,128)(2,1)} %psi_ref.3, bf16[16,1024,1024]{2,1,0:T(8,128)(2,1)} %left_ref.5, bf16[16,512,512]{2,1,0:T(8,128)(2,1)} %own_ref.1), custom_call_target="tpu_custom_call" | custom-call | flops 8053063680 | bytes 13107200 | tf_op jit(solution)/shard_map/local_terms/pallas_call | solution.py:46
  17.2 0.0 collective-permute-done.psi_ref
  17.2 0.0 copy-done
  17.3 0.0 copy-start.2
  17.3 2.4 %collective-permute-start.1 = (bf16[1024,512]{1,0:T(8,128)(2,1)S(1)}, bf16[1024,512]{1,0:T(8,128)(2,1)S(1)}, u32[]{:S(2)}, u32[]{:S(2)}) collective-permute-start(bf16[1024,512]{1,0:T(8,128)(2,1)S(1)} %copy-done), channel_id=1, source_target_pairs={{9,0},{11,2},{13,4},{15,6},{17,8},{0,9},{19,10},{2,11},{21,12},{4,... | collective-permute-start | bytes 3145736 | tf_op jit(solution)/shard_map/ppermute | solution.py:186
  19.7 0.0 copy-done.2
  19.7 11.1 %early_terms.1.after_ref = bf16[1024,512]{1,0:T(8,128)(2,1)} custom-call(s32[1]{0:T(128)} %bitcast.charged, bf16[1024,512]{1,0:T(8,128)(2,1)} %copy-done.2, bf16[16,1024,1024]{2,1,0:T(8,128)(2,1)} %left_ref.5, bf16[16,512,512]{2,1,0:T(8,128)(2,1)} %own_ref.1, f32[1024,512]{1,0:T(8,128)} %local_terms.1.after_ref.start_ref), custom_call_target="tpu_custom_call" | custom-call | flops 6442450944 | bytes 10485760 | tf_op jit(solution)/shard_map/early_terms/pallas_call | solution.py:84
  30.8 3.3 %collective-permute-start.3 = (bf16[1024,512]{1,0:T(8,128)(2,1)}, bf16[1024,512]{1,0:T(8,128)(2,1)S(1)}, u32[]{:S(2)}, u32[]{:S(2)}) collective-permute-start(bf16[1024,512]{1,0:T(8,128)(2,1)} %early_terms.1.after_ref), channel_id=1, source_target_pairs={{1,2},{2,1},{3,4},{4,3},{5,6},{6,5},{9,10},{10,9},{11,12},{12,11},... | collective-permute-start | bytes 3145736 | tf_op jit(solution)/shard_map/ppermute | solution.py:188
  34.2 0.0 collective-permute-done.1.moved_ref
  34.2 0.0 copy-start.1
  34.2 0.0 collective-permute-done.2.partner_ref
  34.2 0.9 %copy-done.1 = bf16[1024,512]{1,0:T(8,128)(2,1)} copy-done((bf16[1024,512]{1,0:T(8,128)(2,1)}, bf16[1024,512]{1,0:T(8,128)(2,1)S(1)}, u32[]{:S(2)}) %copy-start.1) | copy-done | bytes 1048600
  35.2 17.8 %rest_terms.1 = f32[1024,512]{1,0:T(8,128)} custom-call(s32[1]{0:T(128)} %bitcast.charged, bf16[1024,512]{1,0:T(8,128)(2,1)} %psi_ref.3, bf16[1024,512]{1,0:T(8,128)(2,1)} %copy-done.1, bf16[16,1024,1024]{2,1,0:T(8,128)(2,1)} %left_ref.5, bf16[16,512,512]{2,1,0:T(8,128)(2,1)} %own_ref.1, bf16[16,512,512]{2,1,0:T(8,128)(2,1)} %collective-permute-done.2.partner_ref, ...), custom_call_target="tpu_custom_call" | custom-call | flops 11274289152 | bytes 18350080 | tf_op jit(solution)/shard_map/rest_terms/pallas_call | solution.py:139
  52.9 6.0 %collective-permute-done.3 = bf16[1024,512]{1,0:T(8,128)(2,1)S(1)} collective-permute-done((bf16[1024,512]{1,0:T(8,128)(2,1)}, bf16[1024,512]{1,0:T(8,128)(2,1)S(1)}, u32[]{:S(2)}, u32[]{:S(2)}) %collective-permute-start.3) | collective-permute-done | bytes 1048608 | tf_op jit(solution)/shard_map/ppermute | solution.py:188
  59.0 2.9 %add_convert_fusion = bf16[1024,512]{1,0:T(8,128)(2,1)} fusion(f32[1024,512]{1,0:T(8,128)} %rest_terms.1, bf16[1024,512]{1,0:T(8,128)(2,1)S(1)} %collective-permute-done.3), kind=kLoop, calls=%fused_computation | loop fusion | flops 1572864 | bytes 4194304 | tf_op jit(solution)/shard_map/convert_element_type | solution.py:192
Async XLA Ops:
  0.0 17.3 %copy-start = (bf16[1024,512]{1,0:T(8,128)(2,1)S(1)}, bf16[1024,512]{1,0:T(8,128)(2,1)}, u32[]{:S(2)}) copy-start(bf16[1024,512]{1,0:T(8,128)(2,1)} %psi_ref.3) | copy-start | bytes 3145732
  0.0 34.2 %collective-permute-start.2 = (bf16[16,512,512]{2,1,0:T(8,128)(2,1)}, bf16[16,512,512]{2,1,0:T(8,128)(2,1)}, u32[]{:S(2)}, u32[]{:S(2)}) collective-permute-start(bf16[16,512,512]{2,1,0:T(8,128)(2,1)} %own_ref.1), channel_id=1, source_target_pairs={{1,0},{0,1},{3,2},{2,3},{5,4},{4,5},{7,6},{6,7},{9,8},{8,9},{11,10... | collective-permute-start | bytes 25165832 | tf_op jit(solution)/shard_map/ppermute | solution.py:183
  0.7 16.6 %collective-permute-start = (bf16[1024,512]{1,0:T(8,128)(2,1)}, bf16[1024,512]{1,0:T(8,128)(2,1)S(1)}, u32[]{:S(2)}, u32[]{:S(2)}) collective-permute-start(bf16[1024,512]{1,0:T(8,128)(2,1)} %psi_ref.3), channel_id=1, source_target_pairs={{8,0},{10,2},{12,4},{14,6},{16,8},{1,9},{18,10},{3,11},{20,12},{5,... | collective-permute-start | bytes 3145736 | tf_op jit(solution)/shard_map/ppermute | solution.py:182
  17.3 2.4 %copy-start.2 = (bf16[1024,512]{1,0:T(8,128)(2,1)}, bf16[1024,512]{1,0:T(8,128)(2,1)S(1)}, u32[]{:S(2)}) copy-start(bf16[1024,512]{1,0:T(8,128)(2,1)S(1)} %collective-permute-done.psi_ref) | copy-start | bytes 3145732
  17.3 16.9 %collective-permute-start.1 = (bf16[1024,512]{1,0:T(8,128)(2,1)S(1)}, bf16[1024,512]{1,0:T(8,128)(2,1)S(1)}, u32[]{:S(2)}, u32[]{:S(2)}) collective-permute-start(bf16[1024,512]{1,0:T(8,128)(2,1)S(1)} %copy-done), channel_id=1, source_target_pairs={{9,0},{11,2},{13,4},{15,6},{17,8},{0,9},{19,10},{2,11},{21,12},{4,... | collective-permute-start | bytes 3145736 | tf_op jit(solution)/shard_map/ppermute | solution.py:186
  30.8 28.2 %collective-permute-start.3 = (bf16[1024,512]{1,0:T(8,128)(2,1)}, bf16[1024,512]{1,0:T(8,128)(2,1)S(1)}, u32[]{:S(2)}, u32[]{:S(2)}) collective-permute-start(bf16[1024,512]{1,0:T(8,128)(2,1)} %early_terms.1.after_ref), channel_id=1, source_target_pairs={{1,2},{2,1},{3,4},{4,3},{5,6},{6,5},{9,10},{10,9},{11,12},{12,11},... | collective-permute-start | bytes 3145736 | tf_op jit(solution)/shard_map/ppermute | solution.py:188
  34.2 1.0 %copy-start.1 = (bf16[1024,512]{1,0:T(8,128)(2,1)}, bf16[1024,512]{1,0:T(8,128)(2,1)S(1)}, u32[]{:S(2)}) copy-start(bf16[1024,512]{1,0:T(8,128)(2,1)S(1)} %collective-permute-done.1.moved_ref) | copy-start | bytes 3145732

commit v2 on v1

v2 whole, which is shorter than its diff:
```python
import functools

import jax
import jax.numpy as jnp
from jax import lax
from jax.experimental import pallas as pl
from jax.experimental.pallas import tpu as pltpu
from jax.sharding import PartitionSpec as P


channel_shifts = (0, 1, -1, 0)
period = len(channel_shifts)
halves = 2
local_first = 6
vmem_bytes = 20 << 20
in_vmem = pl.BlockSpec(memory_space=pltpu.VMEM)
in_place = pl.BlockSpec(memory_space=pl.ANY)


def contract(left_block, block, right_block):
    partial = jnp.dot(left_block, block, preferred_element_type=jnp.float32)
    return jnp.dot(
        partial.astype(jnp.bfloat16), right_block, preferred_element_type=jnp.float32
    )


def local_channel(step):
    return period * (step // 2) + (period - 1) * (step % 2)


def cost(steps, rows, inner, columns):
    macs = steps * (rows * inner * columns + rows * columns * columns)
    moved = 2 * steps * (rows * inner + columns * columns)
    return pl.CostEstimate(flops=2 * macs, bytes_accessed=moved, transcendentals=0)


def params():
    return pltpu.CompilerParams(vmem_limit_bytes=vmem_bytes)


def half_rows(ref, half):
    rows = ref.shape[0] // halves
    return pl.ds(pl.multiple_of(half * rows, rows), rows)


def local_kernel(psi_ref, left_ref, right_ref, total_ref):
    rows = half_rows(total_ref, pl.program_id(1))
    old = jnp.where(pl.program_id(0) == 0, 0.0, total_ref[rows, :])
    total_ref[rows, :] = old + contract(left_ref[0], psi_ref[...], right_ref[0])


def local_terms(psi, left_env, right_env, steps):
    rows, columns = psi.shape
    return pl.pallas_call(
        local_kernel,
        name="local_terms",
        grid=(steps, halves),
        in_specs=[
            in_vmem,
            pl.BlockSpec((1, rows // halves, rows), lambda w, h: (local_channel(w), h, 0)),
            pl.BlockSpec((1, columns, columns), lambda w, h: (local_channel(w), 0, 0)),
        ],
        out_specs=in_vmem,
        out_shape=jax.ShapeDtypeStruct((rows, columns), jnp.float32),
        compiler_params=params(),
        cost_estimate=cost(steps, rows, rows, columns),
    )(psi, left_env, right_env)


def early_kernel(charged, psi_ref, left_ref, right_ref, after_ref, term_ref, total_ref):
    del charged, after_ref
    old = jnp.where(pl.program_id(0) == 0, 0.0, total_ref[...])
    total = old + contract(left_ref[0], psi_ref[...], right_ref[0])
    total_ref[...] = total
    term_ref[...] = total.astype(term_ref.dtype)


def early_terms(charged, psi, left_env, right_env, half, after):
    rows, columns = psi.shape
    steps = left_env.shape[0] // period
    part = rows // halves
    return pl.pallas_call(
        early_kernel,
        grid_spec=pltpu.PrefetchScalarGridSpec(
            num_scalar_prefetch=1,
            grid=(steps,),
            in_specs=[
                in_vmem,
                pl.BlockSpec((1, part, rows), lambda w, c: (period * w + c[0], half, 0)),
                pl.BlockSpec((1, columns, columns), lambda w, c: (period * w + c[0], 0, 0)),
                in_place,
            ],
            out_specs=in_vmem,
            scratch_shapes=[pltpu.VMEM((part, columns), jnp.float32)],
        ),
        out_shape=jax.ShapeDtypeStruct((part, columns), jnp.bfloat16),
        compiler_params=params(),
        cost_estimate=cost(steps, part, rows, columns),
    )(charged, psi, left_env, right_env, after)


def rest_kernel(local, charged, psi_ref, moved_ref, left_ref, own_ref, partner_ref,
                start_ref, after_ref, total_ref):
    del charged, after_ref, start_ref
    rows = half_rows(total_ref, pl.program_id(1))
    step = pl.program_id(0)

    @pl.when(step < local)
    def _():
        total_ref[rows, :] += contract(left_ref[0], psi_ref[...], own_ref[0])

    @pl.when(step >= local)
    def _():
        total_ref[rows, :] += contract(left_ref[0], moved_ref[...], partner_ref[0])


def rest_terms(charged, psi, moved, left_env, right_env, partner_env, start, after):
    rows, columns = psi.shape
    channels = left_env.shape[0]
    local, late = channels // 2 - local_first, channels // period

    def own(w):
        return local_channel(local_first + jnp.minimum(w, local - 1))

    def partner(w, charged):
        return period * jnp.maximum(w - local, 0) + charged[0]

    def left(w, h, charged):
        return (jnp.where(w < local, own(w), partner(w, charged)), h, 0)

    return pl.pallas_call(
        functools.partial(rest_kernel, local),
        name="rest_terms",
        grid_spec=pltpu.PrefetchScalarGridSpec(
            num_scalar_prefetch=1,
            grid=(local + late, halves),
            in_specs=[
                in_vmem,
                in_vmem,
                pl.BlockSpec((1, rows // halves, rows), left),
                pl.BlockSpec((1, columns, columns), lambda w, h, c: (own(w), 0, 0)),
                pl.BlockSpec((1, columns, columns), lambda w, h, c: (partner(w, c), 0, 0)),
                in_vmem,
                in_place,
            ],
            out_specs=in_vmem,
        ),
        out_shape=jax.ShapeDtypeStruct((rows, columns), jnp.float32),
        input_output_aliases={6: 0},
        compiler_params=params(),
        cost_estimate=cost(local + late, rows, rows, columns),
    )(charged, psi, moved, left_env, right_env, partner_env, start, after)


def finish_kernel(total_ref, first_ref, second_ref, out_ref):
    step = pl.program_id(0)
    rows = out_ref.shape[0]
    steps = pl.num_programs(0) // halves
    total = total_ref[pl.ds(pl.multiple_of(step * rows, rows), rows), :]
    part = pl.ds(pl.multiple_of(lax.rem(step, steps) * rows, rows), rows)

    @pl.when(step < steps)
    def _():
        out_ref[...] = (total + first_ref[part, :].astype(jnp.float32)).astype(out_ref.dtype)

    @pl.when(step >= steps)
    def _():
        out_ref[...] = (total + second_ref[part, :].astype(jnp.float32)).astype(out_ref.dtype)


def finish(total, first, second):
    rows, columns = total.shape
    return pl.pallas_call(
        finish_kernel,
        name="finish",
        grid=(2 * halves,),
        in_specs=[in_vmem, in_vmem, in_vmem],
        out_specs=pl.BlockSpec((rows // (2 * halves), columns), lambda w: (w, 0)),
        out_shape=jax.ShapeDtypeStruct((rows, columns), jnp.bfloat16),
        compiler_params=params(),
    )(total, first, second)


def pairs(left_count, right_count):
    index = lambda i, j: i * right_count + j
    straight, crossed, partner, along = [], [], [], []
    for i in range(left_count):
        for j in range(right_count):
            step = 1 if j % 2 == 0 else -1
            partner.append((index(i, j + step), index(i, j)))
            if 0 <= i + step < left_count:
                straight.append((index(i + step, j), index(i, j)))
                crossed.append((index(i + step, j + step), index(i, j)))
            if 0 <= j - step < right_count:
                along.append((index(i, j), index(i, j - step)))
    return straight, crossed, partner, along


def shards(left_count, right_count, psi, left_env, right_env):
    axes = ("lsec", "rsec")
    straight, crossed, partner, along = pairs(left_count, right_count)
    charged = jnp.reshape(1 + lax.axis_index("rsec") % 2, (1,)).astype(jnp.int32)
    left_env = pltpu.with_memory_space_constraint(left_env, pltpu.HBM)
    right_env = pltpu.with_memory_space_constraint(right_env, pltpu.HBM)
    moved = lax.ppermute(psi, axes, straight)
    partner_env = lax.ppermute(right_env, axes, partner)
    total = local_terms(psi, left_env, right_env, local_first)
    moved, total = lax.optimization_barrier((moved, total))
    first = early_terms(charged, moved, left_env, right_env, 0, total)
    psi_after, first, moved = lax.optimization_barrier((psi, first, moved))
    first_received = lax.ppermute(first, axes, along)
    moved_across = lax.ppermute(psi_after, axes, crossed)
    second = early_terms(charged, moved, left_env, right_env, 1, first)
    second_received = lax.ppermute(second, axes, along)
    total = rest_terms(
        charged, psi, moved_across, left_env, right_env, partner_env, total, second
    )
    return finish(total, first_received, second_received)


def solution(mesh):
    in_specs = (P("lsec", "rsec"), P(None, "lsec", None), P(None, "rsec", None))
    out_specs = P("lsec", "rsec")
    body = functools.partial(shards, mesh.shape["lsec"], mesh.shape["rsec"])
    return jax.shard_map(
        body, mesh=mesh, in_specs=in_specs, out_specs=out_specs, check_vma=False
    )
```

time: 62.1 us -> 60.6 us (0.976)
  the two profiles are of different devices: /device:TPU:19 before, /device:TPU:0 now
where the time goes in v2:
time: 60.6 us; the launch traced here: 60 us
  Pallas kernels  44.7 us (74%)
  starting transfers between devices  9.15 us (15%)
  waiting for transfers between devices  5.98 us (10%)
    pallas_call x1, Pallas kernels, rest_terms(): pl.pallas_call(functools.partial(rest_kernel, local), name='rest_terms',...  15.8 us
    pallas_call x1, Pallas kernels, local_terms(): pl.pallas_call(local_kernel, name='local_terms', grid=(steps, halves), in...  15.6 us
    pallas_call x2, Pallas kernels, early_terms(): pl.pallas_call(early_kernel, grid_spec=pltpu.PrefetchScalarGridSpec(num_s...  11.6 us
    ppermute x1, starting transfers between devices, shards(): moved_across = lax.ppermute(psi_after, axes, crossed)  5.99 us
    ppermute x1, waiting for transfers between devices, shards(): moved_across = lax.ppermute(psi_after, axes, crossed)  5.44 us
    pallas_call x1, Pallas kernels, finish(): pl.pallas_call(finish_kernel, name='finish', grid=(2 * halves,), in_specs...  1.69 us
    ppermute x1, starting transfers between devices, shards(): moved = lax.ppermute(psi, axes, straight)  1.28 us
  transfers between devices with their start and end apart: 5, of which 2 were waited for; matrix products, arithmetic and copies ran while one was open for 0% of the time, Pallas kernels for 72%

profile of v2, /device:TPU:0, one launch (start us, length us, event | category | flops | bytes accessed | tf_op | source)
XLA Modules:
  0.0 60.0 jit_solution(1747619882238167793)
XLA Ops:
  0.0 0.5 collective-permute-start.2
  0.5 1.3 %collective-permute-start = (bf16[1024,512]{1,0:T(8,128)(2,1)}, bf16[1024,512]{1,0:T(8,128)(2,1)S(1)}, u32[]{:S(2)}, u32[]{:S(2)}) collective-permute-start(bf16[1024,512]{1,0:T(8,128)(2,1)} %psi_ref.3), channel_id=1, source_target_pairs={{8,0},{10,2},{12,4},{14,6},{16,8},{1,9},{18,10},{3,11},{20,12},{5,... | collective-permute-start | bytes 3145736 | tf_op jit(solution)/shard_map/ppermute | solution.py:205
  1.8 15.6 %local_terms.1.after_ref.start_ref = f32[1024,512]{1,0:T(8,128)S(1)} custom-call(bf16[1024,512]{1,0:T(8,128)(2,1)} %psi_ref.3, bf16[16,1024,1024]{2,1,0:T(8,128)(2,1)} %left_ref.7, bf16[16,512,512]{2,1,0:T(8,128)(2,1)} %own_ref.1), custom_call_target="tpu_custom_call" | custom-call | flops 9663676416 | bytes 15728640 | tf_op jit(solution)/shard_map/local_terms/pallas_call | solution.py:54
  17.4 0.5 collective-permute-done.psi_ref
  17.9 5.8 %shard_map.37.after_ref = bf16[512,512]{1,0:T(8,128)(2,1)S(1)} custom-call(s32[1]{0:T(128)} %bitcast.charged, bf16[1024,512]{1,0:T(8,128)(2,1)S(1)} %collective-permute-done.psi_ref, bf16[16,1024,1024]{2,1,0:T(8,128)(2,1)} %left_ref.7, bf16[16,512,512]{2,1,0:T(8,128)(2,1)} %own_ref.1, f32[1024,512]{1,0:T(8,128)S(1)} %local_terms.1.after_ref.start_ref), custom_call_target="tpu_custom_call" | custom-call | flops 3221225472 | bytes 6291456 | tf_op jit(solution)/shard_map/pallas_call | solution.py:82
  23.8 6.0 %collective-permute-start.1 = (bf16[1024,512]{1,0:T(8,128)(2,1)}, bf16[1024,512]{1,0:T(8,128)(2,1)S(1)}, u32[]{:S(2)}, u32[]{:S(2)}) collective-permute-start(bf16[1024,512]{1,0:T(8,128)(2,1)} %psi_ref.3), channel_id=1, source_target_pairs={{9,0},{11,2},{13,4},{15,6},{17,8},{0,9},{19,10},{2,11},{21,12},{4,... | collective-permute-start | bytes 3145736 | tf_op jit(solution)/shard_map/ppermute | solution.py:212
  29.8 0.7 %collective-permute-start.3 = (bf16[512,512]{1,0:T(8,128)(2,1)S(1)}, bf16[512,512]{1,0:T(8,128)(2,1)S(1)}, u32[]{:S(2)}, u32[]{:S(2)}) collective-permute-start(bf16[512,512]{1,0:T(8,128)(2,1)S(1)} %shard_map.37.after_ref), channel_id=1, source_target_pairs={{1,2},{2,1},{3,4},{4,3},{5,6},{6,5},{9,10},{10,9},{11,12},{12,11},... | collective-permute-start | bytes 1572872 | tf_op jit(solution)/shard_map/ppermute | solution.py:211
  30.5 5.8 %shard_map.38.after_ref = bf16[512,512]{1,0:T(8,128)(2,1)S(1)} custom-call(s32[1]{0:T(128)} %bitcast.charged, bf16[1024,512]{1,0:T(8,128)(2,1)S(1)} %collective-permute-done.psi_ref, bf16[16,1024,1024]{2,1,0:T(8,128)(2,1)} %left_ref.7, bf16[16,512,512]{2,1,0:T(8,128)(2,1)} %own_ref.1, bf16[512,512]{1,0:T(8,128)(2,1)S(1)} %shard_map.37.after_ref), custom_call_target="tpu_custom_call" | custom-call | flops 3221225472 | bytes 6291456 | tf_op jit(solution)/shard_map/pallas_call | solution.py:82
  36.3 0.7 %collective-permute-start.4 = (bf16[512,512]{1,0:T(8,128)(2,1)S(1)}, bf16[512,512]{1,0:T(8,128)(2,1)S(1)}, u32[]{:S(2)}, u32[]{:S(2)}) collective-permute-start(bf16[512,512]{1,0:T(8,128)(2,1)S(1)} %shard_map.38.after_ref), channel_id=1, source_target_pairs={{1,2},{2,1},{3,4},{4,3},{5,6},{6,5},{9,10},{10,9},{11,12},{12,11},... | collective-permute-start | bytes 1572872 | tf_op jit(solution)/shard_map/ppermute | solution.py:214
  37.0 5.4 %collective-permute-done.1.moved_ref = bf16[1024,512]{1,0:T(8,128)(2,1)S(1)} collective-permute-done((bf16[1024,512]{1,0:T(8,128)(2,1)}, bf16[1024,512]{1,0:T(8,128)(2,1)S(1)}, u32[]{:S(2)}, u32[]{:S(2)}) %collective-permute-start.1) | collective-permute-done | bytes 1048608 | tf_op jit(solution)/shard_map/ppermute | solution.py:212
  42.4 0.0 collective-permute-done.2.partner_ref
  42.4 15.8 %rest_terms.1.total_ref = f32[1024,512]{1,0:T(8,128)S(1)} custom-call(s32[1]{0:T(128)} %bitcast.charged, bf16[1024,512]{1,0:T(8,128)(2,1)} %psi_ref.3, bf16[1024,512]{1,0:T(8,128)(2,1)S(1)} %collective-permute-done.1.moved_ref, bf16[16,1024,1024]{2,1,0:T(8,128)(2,1)} %left_ref.7, bf16[16,512,512]{2,1,0:T(8,128)(2,1)} %own_ref.1, ...), custom_call_target="tpu_custom_call", output_to_operand_aliasing={{}: (6, {})} | custom-call | flops 9663676416 | bytes 15728640 | tf_op jit(solution)/shard_map/rest_terms/pallas_call | solution.py:131
  58.2 0.0 collective-permute-done.4.second_ref
  58.3 0.0 collective-permute-done.3.first_ref
  58.3 1.7 %finish.1 = bf16[1024,512]{1,0:T(8,128)(2,1)} custom-call(f32[1024,512]{1,0:T(8,128)S(1)} %rest_terms.1.total_ref, bf16[512,512]{1,0:T(8,128)(2,1)S(1)} %collective-permute-done.3.first_ref, bf16[512,512]{1,0:T(8,128)(2,1)S(1)} %collective-permute-done.4.second_ref), custom_call_target="tpu_custom_call" | custom-call | tf_op jit(solution)/shard_map/finish/pallas_call | solution.py:173
Async XLA Ops:
  0.0 42.4 %collective-permute-start.2 = (bf16[16,512,512]{2,1,0:T(8,128)(2,1)}, bf16[16,512,512]{2,1,0:T(8,128)(2,1)}, u32[]{:S(2)}, u32[]{:S(2)}) collective-permute-start(bf16[16,512,512]{2,1,0:T(8,128)(2,1)} %own_ref.1), channel_id=1, source_target_pairs={{1,0},{0,1},{3,2},{2,3},{5,4},{4,5},{7,6},{6,7},{9,8},{8,9},{11,10... | collective-permute-start | bytes 25165832 | tf_op jit(solution)/shard_map/ppermute | solution.py:206
  0.5 17.4 %collective-permute-start = (bf16[1024,512]{1,0:T(8,128)(2,1)}, bf16[1024,512]{1,0:T(8,128)(2,1)S(1)}, u32[]{:S(2)}, u32[]{:S(2)}) collective-permute-start(bf16[1024,512]{1,0:T(8,128)(2,1)} %psi_ref.3), channel_id=1, source_target_pairs={{8,0},{10,2},{12,4},{14,6},{16,8},{1,9},{18,10},{3,11},{20,12},{5,... | collective-permute-start | bytes 3145736 | tf_op jit(solution)/shard_map/ppermute | solution.py:205
  23.8 18.7 %collective-permute-start.1 = (bf16[1024,512]{1,0:T(8,128)(2,1)}, bf16[1024,512]{1,0:T(8,128)(2,1)S(1)}, u32[]{:S(2)}, u32[]{:S(2)}) collective-permute-start(bf16[1024,512]{1,0:T(8,128)(2,1)} %psi_ref.3), channel_id=1, source_target_pairs={{9,0},{11,2},{13,4},{15,6},{17,8},{0,9},{19,10},{2,11},{21,12},{4,... | collective-permute-start | bytes 3145736 | tf_op jit(solution)/shard_map/ppermute | solution.py:212
  29.8 28.5 %collective-permute-start.3 = (bf16[512,512]{1,0:T(8,128)(2,1)S(1)}, bf16[512,512]{1,0:T(8,128)(2,1)S(1)}, u32[]{:S(2)}, u32[]{:S(2)}) collective-permute-start(bf16[512,512]{1,0:T(8,128)(2,1)S(1)} %shard_map.37.after_ref), channel_id=1, source_target_pairs={{1,2},{2,1},{3,4},{4,3},{5,6},{6,5},{9,10},{10,9},{11,12},{12,11},... | collective-permute-start | bytes 1572872 | tf_op jit(solution)/shard_map/ppermute | solution.py:211
  36.3 22.0 %collective-permute-start.4 = (bf16[512,512]{1,0:T(8,128)(2,1)S(1)}, bf16[512,512]{1,0:T(8,128)(2,1)S(1)}, u32[]{:S(2)}, u32[]{:S(2)}) collective-permute-start(bf16[512,512]{1,0:T(8,128)(2,1)S(1)} %shard_map.38.after_ref), channel_id=1, source_target_pairs={{1,2},{2,1},{3,4},{4,3},{5,6},{6,5},{9,10},{10,9},{11,12},{12,11},... | collective-permute-start | bytes 1572872 | tf_op jit(solution)/shard_map/ppermute | solution.py:214

commit v3 on v0

v3 whole, which is shorter than its diff:
```python
import functools

import jax
import jax.numpy as jnp
from jax import lax
from jax.experimental import pallas as pl
from jax.experimental.pallas import tpu as pltpu
from jax.sharding import PartitionSpec as P


channel_shifts = (0, 1, -1, 0)
period = len(channel_shifts)
local_first = 6
in_vmem = pl.BlockSpec(memory_space=pltpu.VMEM)
in_smem = pl.BlockSpec(memory_space=pltpu.SMEM)
in_hbm = pl.BlockSpec(memory_space=pl.ANY)


def contract(left_block, block, right_block):
    partial = jnp.dot(left_block, block, preferred_element_type=jnp.float32)
    return jnp.dot(
        partial.astype(jnp.bfloat16), right_block, preferred_element_type=jnp.float32
    )


def local_channel(step):
    return period * (step // 2) + (period - 1) * (step % 2)


def cost(steps, rows, inner, columns):
    macs = steps * (rows * inner * columns + rows * columns * columns)
    moved = 2 * steps * (rows * inner + columns * columns)
    return pl.CostEstimate(flops=2 * macs, bytes_accessed=moved, transcendentals=0)


class Fetch:
    def __init__(self, sems):
        self.sems, self.used = sems, 0

    def start(self, *pairs):
        copies = []
        for source, target in pairs:
            copies.append(pltpu.make_async_copy(source, target, self.sems.at[self.used]))
            self.used += 1
        for copy in copies:
            copy.start()
        return copies


def wait(copies):
    for copy in copies:
        copy.wait()


def half_blocks(left_ref, target_ref, charged, half):
    steps, part = target_ref.shape[:2]
    return [
        (left_ref.at[period * w + charged, pl.ds(half * part, part), :], target_ref.at[w])
        for w in range(steps)
    ]


def right_blocks(right_ref, target_ref, charged):
    return [
        (right_ref.at[period * w + charged], target_ref.at[w])
        for w in range(target_ref.shape[0])
    ]


def local_blocks(left_ref, right_ref, left_target, right_target, step, slot):
    channel = local_channel(step)
    return [
        (left_ref.at[channel], left_target.at[slot]),
        (right_ref.at[channel], right_target.at[slot]),
    ]


def local_kernel(charged_ref, psi_ref, left0_ref, right0_ref, left_ref, right_ref,
                 total_ref, next_left_ref, next_right_ref, lefts_ref, rights_ref, sems):
    charged = charged_ref[0]
    fetch = Fetch(sems)
    steps = lefts_ref.shape[0] + 1
    bring = lambda step: fetch.start(
        *local_blocks(left_ref, right_ref, lefts_ref, rights_ref, step, step - 1)
    )
    coming = {step: bring(step) for step in range(1, min(3, steps))}
    last = None
    for step in range(steps):
        if step:
            wait(coming[step])
        if step and step + 2 < steps:
            coming[step + 2] = bring(step + 2)
        if step == max(0, steps - 3):
            last = fetch.start(
                *half_blocks(left_ref, next_left_ref, charged, 0),
                *right_blocks(right_ref, next_right_ref, charged),
            )
        left = lefts_ref[step - 1] if step else left0_ref[...]
        right = rights_ref[step - 1] if step else right0_ref[...]
        term = contract(left, psi_ref[...], right)
        total_ref[...] = total_ref[...] + term if step else term
    wait(last)


def early_term(psi_ref, lefts_ref, rights_ref, term_ref, total_ref):
    steps = lefts_ref.shape[0]
    for step in range(steps):
        term = contract(lefts_ref[step], psi_ref[...], rights_ref[step])
        total = total_ref[...] + term if step else term
        if step + 1 < steps:
            total_ref[...] = total
        else:
            term_ref[...] = total.astype(term_ref.dtype)


def first_kernel(charged_ref, psi_ref, lefts_ref, rights_ref, left_ref, after_ref,
                 term_ref, next_left_ref, total_ref, sems):
    del after_ref
    coming = Fetch(sems).start(*half_blocks(left_ref, next_left_ref, charged_ref[0], 1))
    early_term(psi_ref, lefts_ref, rights_ref, term_ref, total_ref)
    wait(coming)


def second_kernel(psi_ref, lefts_ref, rights_ref, left_ref, right_ref, after_ref,
                  term_ref, next_left_ref, next_right_ref, total_ref, sems):
    del after_ref
    fetch, coming = Fetch(sems), []
    for slot in range(next_left_ref.shape[0]):
        coming += fetch.start(*local_blocks(
            left_ref, right_ref, next_left_ref, next_right_ref, local_first + slot, slot))
    early_term(psi_ref, lefts_ref, rights_ref, term_ref, total_ref)
    wait(coming)


def rest_kernel(charged_ref, psi_ref, lefts_ref, rights_ref, right_ref, start_ref, after_ref,
                total_ref, next_right_ref, sems):
    del after_ref
    coming = Fetch(sems).start(*right_blocks(right_ref, next_right_ref, charged_ref[0]))
    for step in range(lefts_ref.shape[0]):
        total = start_ref if step == 0 else total_ref
        total_ref[...] = total[...] + contract(lefts_ref[step], psi_ref[...], rights_ref[step])
    wait(coming)


def late_kernel(psi_ref, upper_ref, lower_ref, rights_ref, start_ref, received_ref,
                out_ref, total_ref, work_ref, ready_ref, sem):
    part = total_ref.shape[0]
    steps = rights_ref.shape[0]
    put = pltpu.make_async_copy(ready_ref, out_ref.at[pl.ds(0, part), :], sem)
    for half, lefts_ref in enumerate((upper_ref, lower_ref)):
        for step in range(steps):
            old = start_ref[half * part:(half + 1) * part, :] if step == 0 else work_ref[...]
            total = old + contract(lefts_ref[step], psi_ref[...], rights_ref[step])
            if step + 1 < steps:
                work_ref[...] = total
            elif half:
                total_ref[...] = total
            else:
                total = total + received_ref[...].astype(jnp.float32)
                ready_ref[...] = total.astype(ready_ref.dtype)
                put.start()
    put.wait()


def finish_kernel(total_ref, received_ref, start_ref, out_ref, ready_ref, sem):
    del start_ref
    part = total_ref.shape[0]
    total = total_ref[...] + received_ref[...].astype(jnp.float32)
    ready_ref[...] = total.astype(ready_ref.dtype)
    put = pltpu.make_async_copy(ready_ref, out_ref.at[pl.ds(part, part), :], sem)
    put.start()
    put.wait()


def pairs(left_count, right_count):
    index = lambda i, j: i * right_count + j
    straight, crossed, partner, along = [], [], [], []
    for i in range(left_count):
        for j in range(right_count):
            step = 1 if j % 2 == 0 else -1
            partner.append((index(i, j + step), index(i, j)))
            if 0 <= i + step < left_count:
                straight.append((index(i + step, j), index(i, j)))
                crossed.append((index(i + step, j + step), index(i, j)))
            if 0 <= j - step < right_count:
                along.append((index(i, j), index(i, j - step)))
    return straight, crossed, partner, along


def shards(left_count, right_count, psi, left_whole, right_whole):
    axes = ("lsec", "rsec")
    straight, crossed, partner, along = pairs(left_count, right_count)
    rows, columns = psi.shape
    channels = left_whole.shape[0]
    charged_count, local_rest = channels // period, channels // 2 - local_first
    part = rows // 2
    f32, bf16 = jnp.float32, jnp.bfloat16
    lefts = lambda count: pltpu.VMEM((count, rows, rows), bf16)
    halves = pltpu.VMEM((charged_count, part, rows), bf16)
    rights = lambda count: pltpu.VMEM((count, columns, columns), bf16)
    shape = lambda ref: jax.ShapeDtypeStruct(ref.shape, ref.dtype)
    sems = lambda count: pltpu.SemaphoreType.DMA((count,))

    def call(kernel, in_specs, outs, scratch, work, limit=20, aliases=None, out_specs=None):
        return pl.pallas_call(
            kernel,
            in_specs=in_specs,
            out_specs=out_specs or [in_vmem] * len(outs),
            out_shape=[shape(out) for out in outs],
            scratch_shapes=scratch,
            input_output_aliases=aliases or {},
            compiler_params=pltpu.CompilerParams(vmem_limit_bytes=limit << 20),
            cost_estimate=work,
        )

    charged = jnp.reshape(1 + lax.axis_index("rsec") % 2, (1,)).astype(jnp.int32)
    left_env = pltpu.with_memory_space_constraint(left_whole, pltpu.HBM)
    right_env = pltpu.with_memory_space_constraint(right_whole, pltpu.HBM)
    total_shape = pltpu.VMEM((rows, columns), f32)
    half_total = pltpu.VMEM((part, columns), f32)
    half_block = pltpu.VMEM((part, columns), bf16)

    moved = lax.ppermute(psi, axes, straight)
    partner_env = lax.ppermute(right_env, axes, partner)

    total, upper, own = call(
        local_kernel,
        [in_smem, in_vmem, in_vmem, in_vmem, in_hbm, in_hbm],
        [total_shape, halves, rights(charged_count)],
        [lefts(local_first - 1), rights(local_first - 1),
         sems(2 * (local_first - 1) + 2 * charged_count)],
        cost(local_first, rows, rows, columns),
    )(charged, psi, left_whole[0], right_whole[0], left_env, right_env)

    moved, total = lax.optimization_barrier((moved, total))
    first, lower = call(
        first_kernel,
        [in_smem, in_vmem, in_vmem, in_vmem, in_hbm, in_hbm],
        [half_block, halves],
        [half_total, sems(charged_count)],
        cost(charged_count, part, rows, columns),
    )(charged, moved, upper, own, left_env, total)

    psi_after, first, moved = lax.optimization_barrier((psi, first, moved))
    first_received = lax.ppermute(first, axes, along)
    moved_across = lax.ppermute(psi_after, axes, crossed)
    second, rest_left, rest_right = call(
        second_kernel,
        [in_vmem, in_vmem, in_vmem, in_hbm, in_hbm, in_hbm],
        [half_block, lefts(local_rest), rights(local_rest)],
        [half_total, sems(2 * local_rest)],
        cost(charged_count, part, rows, columns),
    )(moved, lower, own, left_env, right_env, first)
    second_received = lax.ppermute(second, axes, along)

    total, across = call(
        rest_kernel,
        [in_smem, in_vmem, in_vmem, in_vmem, in_hbm, in_vmem, in_hbm],
        [total_shape, rights(charged_count)],
        [sems(charged_count)],
        cost(local_rest, rows, rows, columns),
        aliases={5: 0},
    )(charged, psi, rest_left, rest_right, partner_env, total, second)
    moved_across, total = lax.optimization_barrier((moved_across, total))
    out, total = call(
        late_kernel,
        [in_vmem] * 6,
        [pltpu.VMEM((rows, columns), bf16), half_total],
        [half_total, half_block, pltpu.SemaphoreType.DMA],
        cost(charged_count, rows, rows, columns),
        out_specs=[in_hbm, in_vmem],
    )(moved_across, upper, lower, across, total, first_received)
    (out,) = call(
        finish_kernel,
        [in_vmem, in_vmem, in_hbm],
        [pltpu.VMEM((rows, columns), bf16)],
        [half_block, pltpu.SemaphoreType.DMA],
        None,
        aliases={2: 0},
        out_specs=[in_hbm],
    )(total, second_received, out)
    return out


def solution(mesh):
    in_specs = (P("lsec", "rsec"), P(None, "lsec", None), P(None, "rsec", None))
    out_specs = P("lsec", "rsec")
    body = functools.partial(shards, mesh.shape["lsec"], mesh.shape["rsec"])
    return jax.shard_map(
        body, mesh=mesh, in_specs=in_specs, out_specs=out_specs, check_vma=False
    )
```

time: 107 us -> 54.4 us (0.51)
  the two profiles are of different devices: /device:TPU:0 before, /device:TPU:4 now
where the time goes in v3:
time: 54.4 us; the launch traced here: 54.1 us
  Pallas kernels  31.9 us (59%)
  starting transfers between devices  11.7 us (22%)
  waiting for transfers between devices  7.45 us (14%)
  local copies, waits for them, and re-layouts  2.85 us (5%)
    pallas_call x1, Pallas kernels, shards(): call(local_kernel, [in_smem, in_vmem, in_vmem, in_vmem, in_hbm, in_hbm],...  10.9 us
    pallas_call x1, Pallas kernels, shards(): call(late_kernel, [in_vmem] * 6, [pltpu.VMEM((rows, columns), bf16), half...  6.83 us
    pallas_call x1, Pallas kernels, shards(): call(first_kernel, [in_smem, in_vmem, in_vmem, in_vmem, in_hbm, in_hbm],...  5.06 us
    ppermute x1, starting transfers between devices, shards(): second_received = lax.ppermute(second, axes, along)  4.72 us
    pallas_call x1, Pallas kernels, shards(): call(second_kernel, [in_vmem, in_vmem, in_vmem, in_hbm, in_hbm, in_hbm],...  4.67 us
    ppermute x1, starting transfers between devices, shards(): moved_across = lax.ppermute(psi_after, axes, crossed)  3.59 us
    pallas_call x1, Pallas kernels, shards(): call(rest_kernel, [in_smem, in_vmem, in_vmem, in_vmem, in_hbm, in_vmem, i...  3.5 us
    ppermute x1, waiting for transfers between devices, shards(): second_received = lax.ppermute(second, axes, along)  3.5 us
  transfers between devices with their start and end apart: 5, of which 3 were waited for; matrix products, arithmetic and copies ran while one was open for 5% of the time, Pallas kernels for 57%

profile of v3, /device:TPU:4, one launch (start us, length us, event | category | flops | bytes accessed | tf_op | source)
XLA Modules:
  0.0 54.1 jit_solution(7391760895384539012)
XLA Ops:
  0.0 0.0 copy-start
  0.0 0.0 collective-permute-start.2
  0.0 1.4 %collective-permute-start = (bf16[1024,512]{1,0:T(8,128)(2,1)}, bf16[1024,512]{1,0:T(8,128)(2,1)S(1)}, u32[]{:S(2)}, u32[]{:S(2)}) collective-permute-start(bf16[1024,512]{1,0:T(8,128)(2,1)} %psi_ref.3), channel_id=1, source_target_pairs={{8,0},{10,2},{12,4},{14,6},{16,8},{1,9},{18,10},{3,11},{20,12},{5,... | collective-permute-start | bytes 3145736 | tf_op jit(solution)/shard_map/ppermute | solution.py:223
  1.4 1.8 %slice_bitcast_fusion.left0_ref = bf16[1024,1024]{1,0:T(8,128)(2,1)S(1)} fusion(bf16[16,1024,1024]{2,1,0:T(8,128)(2,1)} %left_ref.5), kind=kLoop, calls=%fused_computation | loop fusion | bytes 4194304 | tf_op jit(solution)/shard_map/squeeze | solution.py:233
  3.2 1.1 %slice_bitcast_fusion.1.right0_ref = bf16[512,512]{1,0:T(8,128)(2,1)S(1)} fusion(bf16[16,512,512]{2,1,0:T(8,128)(2,1)} %right_ref.3), kind=kLoop, calls=%fused_computation.1 | loop fusion | bytes 1048576 | tf_op jit(solution)/shard_map/squeeze | solution.py:233
  4.3 0.0 copy-done
  4.3 10.9 %shard_map.37 = (f32[1024,512]{1,0:T(8,128)S(1)}, bf16[4,512,1024]{2,1,0:T(8,128)(2,1)S(1)}, bf16[4,512,512]{2,1,0:T(8,128)(2,1)S(1)}) custom-call(s32[1]{0:T(128)} %bitcast.charged_ref, bf16[1024,512]{1,0:T(8,128)(2,1)S(1)} %copy-done, bf16[1024,1024]{1,0:T(8,128)(2,1)S(1)} %slice_bitcast_fusion.left0_ref, ...), custom_call_target="tpu_custom_call" | custom-call | flops 9663676416 | bytes 15728640 | tf_op jit(solution)/shard_map/pallas_call | solution.py:226
  15.2 1.8 %collective-permute-done.psi_ref = bf16[1024,512]{1,0:T(8,128)(2,1)S(1)} collective-permute-done((bf16[1024,512]{1,0:T(8,128)(2,1)}, bf16[1024,512]{1,0:T(8,128)(2,1)S(1)}, u32[]{:S(2)}, u32[]{:S(2)}) %collective-permute-start) | collective-permute-done | bytes 1048608 | tf_op jit(solution)/shard_map/ppermute | solution.py:223
  17.0 5.1 %shard_map.38 = (bf16[512,512]{1,0:T(8,128)(2,1)S(1)}, bf16[4,512,1024]{2,1,0:T(8,128)(2,1)S(1)}) custom-call(s32[1]{0:T(128)} %bitcast.charged_ref, bf16[1024,512]{1,0:T(8,128)(2,1)S(1)} %collective-permute-done.psi_ref, bf16[4,512,1024]{2,1,0:T(8,128)(2,1)S(1)} %get-tuple-element.26.lefts_ref.upper_ref, ...), custom_call_target="tpu_custom_call" | custom-call | flops 3221225472 | bytes 6291456 | tf_op jit(solution)/shard_map/pallas_call | solution.py:236
  22.1 3.6 %collective-permute-start.1 = (bf16[1024,512]{1,0:T(8,128)(2,1)S(1)}, bf16[1024,512]{1,0:T(8,128)(2,1)S(1)}, u32[]{:S(2)}, u32[]{:S(2)}) collective-permute-start(bf16[1024,512]{1,0:T(8,128)(2,1)S(1)} %copy-done), channel_id=1, source_target_pairs={{9,0},{11,2},{13,4},{15,6},{17,8},{0,9},{19,10},{2,11},{21,12},{4,... | collective-permute-start | bytes 3145736 | tf_op jit(solution)/shard_map/ppermute | solution.py:246
  25.7 1.9 %collective-permute-start.3 = (bf16[512,512]{1,0:T(8,128)(2,1)S(1)}, bf16[512,512]{1,0:T(8,128)(2,1)S(1)}, u32[]{:S(2)}, u32[]{:S(2)}) collective-permute-start(bf16[512,512]{1,0:T(8,128)(2,1)S(1)} %get-tuple-element.33.after_ref), channel_id=1, source_target_pairs={{1,2},{2,1},{3,4},{4,3},{5,6},{6,5},{9,10},{10,9},{11,12},{12,11},... | collective-permute-start | bytes 1572872 | tf_op jit(solution)/shard_map/ppermute | solution.py:245
  27.6 4.7 %shard_map.39 = (bf16[512,512]{1,0:T(8,128)(2,1)S(1)}, bf16[2,1024,1024]{2,1,0:T(8,128)(2,1)S(1)}, bf16[2,512,512]{2,1,0:T(8,128)(2,1)S(1)}) custom-call(bf16[1024,512]{1,0:T(8,128)(2,1)S(1)} %collective-permute-done.psi_ref, bf16[4,512,1024]{2,1,0:T(8,128)(2,1)S(1)} %get-tuple-element.32.lefts_ref.lower_ref, ...), custom_call_target="tpu_custom_call" | custom-call | flops 3221225472 | bytes 6291456 | tf_op jit(solution)/shard_map/pallas_call | solution.py:247
  32.3 4.7 %collective-permute-start.4 = (bf16[512,512]{1,0:T(8,128)(2,1)S(1)}, bf16[512,512]{1,0:T(8,128)(2,1)S(1)}, u32[]{:S(2)}, u32[]{:S(2)}) collective-permute-start(bf16[512,512]{1,0:T(8,128)(2,1)S(1)} %get-tuple-element.36.after_ref), channel_id=1, source_target_pairs={{1,2},{2,1},{3,4},{4,3},{5,6},{6,5},{9,10},{10,9},{11,12},{12,11},... | collective-permute-start | bytes 1572872 | tf_op jit(solution)/shard_map/ppermute | solution.py:254
  37.0 0.0 collective-permute-done.2.right_ref
  37.1 3.5 %shard_map.40 = (f32[1024,512]{1,0:T(8,128)S(1)}, bf16[4,512,512]{2,1,0:T(8,128)(2,1)S(1)}) custom-call(s32[1]{0:T(128)} %bitcast.charged_ref, bf16[1024,512]{1,0:T(8,128)(2,1)S(1)} %copy-done, bf16[2,1024,1024]{2,1,0:T(8,128)(2,1)S(1)} %get-tuple-element.34.lefts_ref, ...), custom_call_target="tpu_custom_call", output_to_operand_aliasing={{0}: (5, {})} | custom-call | flops 3221225472 | bytes 5242880 | tf_op jit(solution)/shard_map/pallas_call | solution.py:256
  40.6 0.0 collective-permute-done.1.psi_ref
  40.6 2.1 %collective-permute-done.3.received_ref = bf16[512,512]{1,0:T(8,128)(2,1)S(1)} collective-permute-done((bf16[512,512]{1,0:T(8,128)(2,1)S(1)}, bf16[512,512]{1,0:T(8,128)(2,1)S(1)}, u32[]{:S(2)}, u32[]{:S(2)}) %collective-permute-start.3) | collective-permute-done | bytes 524320 | tf_op jit(solution)/shard_map/ppermute | solution.py:245
  42.7 6.8 %shard_map.41 = (bf16[1024,512]{1,0:T(8,128)(2,1)}, f32[512,512]{1,0:T(8,128)S(1)}) custom-call(bf16[1024,512]{1,0:T(8,128)(2,1)S(1)} %collective-permute-done.1.psi_ref, bf16[4,512,1024]{2,1,0:T(8,128)(2,1)S(1)} %get-tuple-element.26.lefts_ref.upper_ref, bf16[4,512,1024]{2,1,0:T(8,128)(2,1)S(1)} %get-tuple-element.32.lefts_ref.lower_ref, ...), custom_call_target="tpu_custom_call" | custom-call | flops 6442450944 | bytes 10485760 | tf_op jit(solution)/shard_map/pallas_call | solution.py:265
  49.6 3.5 %collective-permute-done.4.received_ref = bf16[512,512]{1,0:T(8,128)(2,1)S(1)} collective-permute-done((bf16[512,512]{1,0:T(8,128)(2,1)S(1)}, bf16[512,512]{1,0:T(8,128)(2,1)S(1)}, u32[]{:S(2)}, u32[]{:S(2)}) %collective-permute-start.4) | collective-permute-done | bytes 524320 | tf_op jit(solution)/shard_map/ppermute | solution.py:254
  53.1 0.9 %shard_map.42 = bf16[1024,512]{1,0:T(8,128)(2,1)} custom-call(f32[512,512]{1,0:T(8,128)S(1)} %get-tuple-element.41.total_ref, bf16[512,512]{1,0:T(8,128)(2,1)S(1)} %collective-permute-done.4.received_ref, bf16[1024,512]{1,0:T(8,128)(2,1)} %get-tuple-element.42.start_ref), custom_call_target="tpu_custom_call", output_to_operand_aliasing={{}: (2, {})} | custom-call | tf_op jit(solution)/shard_map/pallas_call | solution.py:273
Async XLA Ops:
  0.0 4.3 %copy-start = (bf16[1024,512]{1,0:T(8,128)(2,1)S(1)}, bf16[1024,512]{1,0:T(8,128)(2,1)}, u32[]{:S(2)}) copy-start(bf16[1024,512]{1,0:T(8,128)(2,1)} %psi_ref.3) | copy-start | bytes 3145732
  0.0 37.0 %collective-permute-start.2 = (bf16[16,512,512]{2,1,0:T(8,128)(2,1)}, bf16[16,512,512]{2,1,0:T(8,128)(2,1)}, u32[]{:S(2)}, u32[]{:S(2)}) collective-permute-start(bf16[16,512,512]{2,1,0:T(8,128)(2,1)} %right_ref.3), channel_id=1, source_target_pairs={{1,0},{0,1},{3,2},{2,3},{5,4},{4,5},{7,6},{6,7},{9,8},{8,9},{11,10... | collective-permute-start | bytes 25165832 | tf_op jit(solution)/shard_map/ppermute | solution.py:224
  0.0 17.0 %collective-permute-start = (bf16[1024,512]{1,0:T(8,128)(2,1)}, bf16[1024,512]{1,0:T(8,128)(2,1)S(1)}, u32[]{:S(2)}, u32[]{:S(2)}) collective-permute-start(bf16[1024,512]{1,0:T(8,128)(2,1)} %psi_ref.3), channel_id=1, source_target_pairs={{8,0},{10,2},{12,4},{14,6},{16,8},{1,9},{18,10},{3,11},{20,12},{5,... | collective-permute-start | bytes 3145736 | tf_op jit(solution)/shard_map/ppermute | solution.py:223
  22.1 18.5 %collective-permute-start.1 = (bf16[1024,512]{1,0:T(8,128)(2,1)S(1)}, bf16[1024,512]{1,0:T(8,128)(2,1)S(1)}, u32[]{:S(2)}, u32[]{:S(2)}) collective-permute-start(bf16[1024,512]{1,0:T(8,128)(2,1)S(1)} %copy-done), channel_id=1, source_target_pairs={{9,0},{11,2},{13,4},{15,6},{17,8},{0,9},{19,10},{2,11},{21,12},{4,... | collective-permute-start | bytes 3145736 | tf_op jit(solution)/shard_map/ppermute | solution.py:246
  25.7 17.0 %collective-permute-start.3 = (bf16[512,512]{1,0:T(8,128)(2,1)S(1)}, bf16[512,512]{1,0:T(8,128)(2,1)S(1)}, u32[]{:S(2)}, u32[]{:S(2)}) collective-permute-start(bf16[512,512]{1,0:T(8,128)(2,1)S(1)} %get-tuple-element.33.after_ref), channel_id=1, source_target_pairs={{1,2},{2,1},{3,4},{4,3},{5,6},{6,5},{9,10},{10,9},{11,12},{12,11},... | collective-permute-start | bytes 1572872 | tf_op jit(solution)/shard_map/ppermute | solution.py:245
  32.3 20.8 %collective-permute-start.4 = (bf16[512,512]{1,0:T(8,128)(2,1)S(1)}, bf16[512,512]{1,0:T(8,128)(2,1)S(1)}, u32[]{:S(2)}, u32[]{:S(2)}) collective-permute-start(bf16[512,512]{1,0:T(8,128)(2,1)S(1)} %get-tuple-element.36.after_ref), channel_id=1, source_target_pairs={{1,2},{2,1},{3,4},{4,3},{5,6},{6,5},{9,10},{10,9},{11,12},{12,11},... | collective-permute-start | bytes 1572872 | tf_op jit(solution)/shard_map/ppermute | solution.py:254

commit v4 on v3

--- a/solution.py
+++ b/solution.py
@@ -10,7 +10,7 @@
 
 channel_shifts = (0, 1, -1, 0)
 period = len(channel_shifts)
-local_first = 6
+local_first = 5
 in_vmem = pl.BlockSpec(memory_space=pltpu.VMEM)
 in_smem = pl.BlockSpec(memory_space=pltpu.SMEM)
 in_hbm = pl.BlockSpec(memory_space=pl.ANY)
@@ -75,30 +75,35 @@
     ]
 
 
-def local_kernel(charged_ref, psi_ref, left0_ref, right0_ref, left_ref, right_ref,
-                 total_ref, next_left_ref, next_right_ref, lefts_ref, rights_ref, sems):
+def local_kernel(charged_ref, whole_ref, left_ref, right_ref, total_ref, psi_ref, next_left_ref,
+                 next_right_ref, give_ref, lefts_ref, rights_ref, sems):
     charged = charged_ref[0]
     fetch = Fetch(sems)
-    steps = lefts_ref.shape[0] + 1
+    steps = lefts_ref.shape[0]
+    part = total_ref.shape[0] // 2
+    halves = (pl.ds(0, part), pl.ds(part, part))
+    tops = fetch.start((whole_ref, psi_ref))
+    tops += fetch.start((left_ref.at[0, halves[0], :], lefts_ref.at[0, halves[0], :]))
+    tops += fetch.start((right_ref.at[0], rights_ref.at[0]))
+    bottom = fetch.start((left_ref.at[0, halves[1], :], lefts_ref.at[0, halves[1], :]))
     bring = lambda step: fetch.start(
-        *local_blocks(left_ref, right_ref, lefts_ref, rights_ref, step, step - 1)
+        *local_blocks(left_ref, right_ref, lefts_ref, rights_ref, step, step)
     )
     coming = {step: bring(step) for step in range(1, min(3, steps))}
-    last = None
-    for step in range(steps):
-        if step:
-            wait(coming[step])
-        if step and step + 2 < steps:
+    for half, copies in zip(halves, (tops, bottom)):
+        wait(copies)
+        total_ref[half, :] = contract(lefts_ref[0, half, :], psi_ref[...], rights_ref[0])
+    last = []
+    for step in range(1, steps):
+        wait(coming[step])
+        if step + 2 < steps:
             coming[step + 2] = bring(step + 2)
-        if step == max(0, steps - 3):
-            last = fetch.start(
-                *half_blocks(left_ref, next_left_ref, charged, 0),
-                *right_blocks(right_ref, next_right_ref, charged),
-            )
-        left = lefts_ref[step - 1] if step else left0_ref[...]
-        right = rights_ref[step - 1] if step else right0_ref[...]
-        term = contract(left, psi_ref[...], right)
-        total_ref[...] = total_ref[...] + term if step else term
+        if step == max(1, steps - 3):
+            last += fetch.start(*half_blocks(left_ref, next_left_ref, charged, 0))
+        if step == max(1, steps - 2):
+            last += fetch.start(*right_blocks(right_ref, next_right_ref, charged))
+            last += fetch.start(*right_blocks(right_ref, give_ref, period - 1 - charged))
+        total_ref[...] += contract(lefts_ref[step], psi_ref[...], rights_ref[step])
     wait(last)
 
 
@@ -124,22 +129,26 @@
 def second_kernel(psi_ref, lefts_ref, rights_ref, left_ref, right_ref, after_ref,
                   term_ref, next_left_ref, next_right_ref, total_ref, sems):
     del after_ref
-    fetch, coming = Fetch(sems), []
-    for slot in range(next_left_ref.shape[0]):
-        coming += fetch.start(*local_blocks(
-            left_ref, right_ref, next_left_ref, next_right_ref, local_first + slot, slot))
+    coming = Fetch(sems).start(*local_blocks(
+        left_ref, right_ref, next_left_ref, next_right_ref, local_first, 0))
     early_term(psi_ref, lefts_ref, rights_ref, term_ref, total_ref)
     wait(coming)
 
 
-def rest_kernel(charged_ref, psi_ref, lefts_ref, rights_ref, right_ref, start_ref, after_ref,
-                total_ref, next_right_ref, sems):
+def rest_kernel(psi_ref, left0_ref, right0_ref, left_ref, right_ref, start_ref, after_ref,
+                total_ref, lefts_ref, rights_ref, sems):
     del after_ref
-    coming = Fetch(sems).start(*right_blocks(right_ref, next_right_ref, charged_ref[0]))
-    for step in range(lefts_ref.shape[0]):
-        total = start_ref if step == 0 else total_ref
-        total_ref[...] = total[...] + contract(lefts_ref[step], psi_ref[...], rights_ref[step])
-    wait(coming)
+    fetch = Fetch(sems)
+    count = lefts_ref.shape[0]
+    coming = [
+        fetch.start(*local_blocks(
+            left_ref, right_ref, lefts_ref, rights_ref, local_first + 1 + slot, slot))
+        for slot in range(count)
+    ]
+    total_ref[...] = start_ref[...] + contract(left0_ref[0], psi_ref[...], right0_ref[0])
+    for slot in range(count):
+        wait(coming[slot])
+        total_ref[...] += contract(lefts_ref[slot], psi_ref[...], rights_ref[slot])
 
 
 def late_kernel(psi_ref, upper_ref, lower_ref, rights_ref, start_ref, received_ref,
@@ -182,7 +191,7 @@
             if 0 <= i + step < left_count:
                 straight.append((index(i + step, j), index(i, j)))
                 crossed.append((index(i + step, j + step), index(i, j)))
-            if 0 <= j - step < right_count:
+            if 0 <= j - step < right_count and 0 <= i + step < left_count:
                 along.append((index(i, j), index(i, j - step)))
     return straight, crossed, partner, along
 
@@ -221,17 +230,19 @@
     half_block = pltpu.VMEM((part, columns), bf16)
 
     moved = lax.ppermute(psi, axes, straight)
-    partner_env = lax.ppermute(right_env, axes, partner)
-
-    total, upper, own = call(
+
+    total, kept, upper, own, give = call(
         local_kernel,
-        [in_smem, in_vmem, in_vmem, in_vmem, in_hbm, in_hbm],
-        [total_shape, halves, rights(charged_count)],
-        [lefts(local_first - 1), rights(local_first - 1),
-         sems(2 * (local_first - 1) + 2 * charged_count)],
+        [in_smem, in_hbm, in_hbm, in_hbm],
+        [total_shape, pltpu.VMEM((rows, columns), bf16), halves, rights(charged_count), rights(charged_count)],
+        [lefts(local_first), rights(local_first),
+         sems(2 * local_first + 2 + 3 * charged_count)],
         cost(local_first, rows, rows, columns),
-    )(charged, psi, left_whole[0], right_whole[0], left_env, right_env)
-
+    )(charged, psi, left_env, right_env)
+
+    psi_after, total = lax.optimization_barrier((psi, total))
+    moved_across = lax.ppermute(psi_after, axes, crossed)
+    across = lax.ppermute(give, axes, partner)
     moved, total = lax.optimization_barrier((moved, total))
     first, lower = call(
         first_kernel,
@@ -240,27 +251,25 @@
         [half_total, sems(charged_count)],
         cost(charged_count, part, rows, columns),
     )(charged, moved, upper, own, left_env, total)
-
-    psi_after, first, moved = lax.optimization_barrier((psi, first, moved))
     first_received = lax.ppermute(first, axes, along)
-    moved_across = lax.ppermute(psi_after, axes, crossed)
+
     second, rest_left, rest_right = call(
         second_kernel,
         [in_vmem, in_vmem, in_vmem, in_hbm, in_hbm, in_hbm],
-        [half_block, lefts(local_rest), rights(local_rest)],
-        [half_total, sems(2 * local_rest)],
+        [half_block, lefts(1), rights(1)],
+        [half_total, sems(2)],
         cost(charged_count, part, rows, columns),
     )(moved, lower, own, left_env, right_env, first)
     second_received = lax.ppermute(second, axes, along)
 
-    total, across = call(
+    (total,) = call(
         rest_kernel,
-        [in_smem, in_vmem, in_vmem, in_vmem, in_hbm, in_vmem, in_hbm],
-        [total_shape, rights(charged_count)],
-        [sems(charged_count)],
+        [in_vmem, in_vmem, in_vmem, in_hbm, in_hbm, in_vmem, in_hbm],
+        [total_shape],
+        [lefts(local_rest - 1), rights(local_rest - 1), sems(2 * local_rest - 2)],
         cost(local_rest, rows, rows, columns),
         aliases={5: 0},
-    )(charged, psi, rest_left, rest_right, partner_env, total, second)
+    )(kept, rest_left, rest_right, left_env, right_env, total, second)
     moved_across, total = lax.optimization_barrier((moved_across, total))
     out, total = call(
         late_kernel,

time: 54.4 us -> 52 us (0.956)
  the two profiles are of different devices: /device:TPU:4 before, /device:TPU:11 now
where the time goes in v4:
time: 52 us; the launch traced here: 51.8 us
  Pallas kernels  32.4 us (62%)
  starting transfers between devices  12.4 us (24%)
  waiting for transfers between devices  5.41 us (10%)
  local copies, waits for them, and re-layouts  1.22 us (2%)
    pallas_call x1, Pallas kernels, shards(): call(local_kernel, [in_smem, in_hbm, in_hbm, in_hbm], [total_shape, pltpu...  10.8 us
    pallas_call x1, Pallas kernels, shards(): call(late_kernel, [in_vmem] * 6, [pltpu.VMEM((rows, columns), bf16), half...  6.83 us
    pallas_call x1, Pallas kernels, shards(): call(rest_kernel, [in_vmem, in_vmem, in_vmem, in_hbm, in_hbm, in_vmem, in...  5.42 us
    pallas_call x1, Pallas kernels, shards(): call(first_kernel, [in_smem, in_vmem, in_vmem, in_vmem, in_hbm, in_hbm],...  5.07 us
    ppermute x1, waiting for transfers between devices, shards(): second_received = lax.ppermute(second, axes, along)  4.39 us
    ppermute x1, starting transfers between devices, shards(): first_received = lax.ppermute(first, axes, along)  4.09 us
    pallas_call x1, Pallas kernels, shards(): call(second_kernel, [in_vmem, in_vmem, in_vmem, in_hbm, in_hbm, in_hbm],...  3.44 us
    ppermute x1, starting transfers between devices, shards(): moved = lax.ppermute(psi, axes, straight)  3.19 us
  transfers between devices with their start and end apart: 5, of which 2 were waited for; matrix products, arithmetic and copies ran while one was open for 0% of the time, Pallas kernels for 61%

profile of v4, /device:TPU:11, one launch (start us, length us, event | category | flops | bytes accessed | tf_op | source)
XLA Modules:
  0.0 51.8 jit_solution(16904263187398408640)
XLA Ops:
  0.0 3.2 %collective-permute-start.1 = (bf16[1024,512]{1,0:T(8,128)(2,1)}, bf16[1024,512]{1,0:T(8,128)(2,1)S(1)}, u32[]{:S(2)}, u32[]{:S(2)}) collective-permute-start(bf16[1024,512]{1,0:T(8,128)(2,1)} %whole_ref.1), channel_id=1, source_target_pairs={{8,0},{10,2},{12,4},{14,6},{16,8},{1,9},{18,10},{3,11},{20,12},{5,... | collective-permute-start | bytes 3145736 | tf_op jit(solution)/shard_map/ppermute | solution.py:232
  3.2 0.0 copy-start
  3.2 1.2 %copy-done = bf16[1024,512]{1,0:T(8,128)(2,1)S(1)} copy-done((bf16[1024,512]{1,0:T(8,128)(2,1)S(1)}, bf16[1024,512]{1,0:T(8,128)(2,1)}, u32[]{:S(2)}) %copy-start) | copy-done | bytes 1048600
  4.4 10.8 %shard_map.37 = (f32[1024,512]{1,0:T(8,128)S(1)}, bf16[1024,512]{1,0:T(8,128)(2,1)S(1)}, bf16[4,512,1024]{2,1,0:T(8,128)(2,1)S(1)}, bf16[4,512,512]{2,1,0:T(8,128)(2,1)S(1)}, bf16[4,512,512]{2,1,0:T(8,128)(2,1)S(1)}) custom-call(s32[1]{0:T(128)} %bitcast.charged_ref, bf16[1024,512]{1,0:T(8,128)(2,1)S(1)} %copy-done, bf16[16,1024,1024]{2,1,0:T(8,128)(2,1)} %left_ref.7, ...), custom_call_target="tpu_custom_call" | custom-call | flops 8053063680 | bytes 13107200 | tf_op jit(solution)/shard_map/pallas_call | solution.py:234
  15.2 0.1 collective-permute-start.2
  15.3 2.5 %collective-permute-start = (bf16[1024,512]{1,0:T(8,128)(2,1)S(1)}, bf16[1024,512]{1,0:T(8,128)(2,1)S(1)}, u32[]{:S(2)}, u32[]{:S(2)}) collective-permute-start(bf16[1024,512]{1,0:T(8,128)(2,1)S(1)} %copy-done), channel_id=1, source_target_pairs={{9,0},{11,2},{13,4},{15,6},{17,8},{0,9},{19,10},{2,11},{21,12},{4,... | collective-permute-start | bytes 3145736 | tf_op jit(solution)/shard_map/ppermute | solution.py:244
  17.8 0.0 collective-permute-done.1.psi_ref
  17.9 5.1 %shard_map.38 = (bf16[512,512]{1,0:T(8,128)(2,1)S(1)}, bf16[4,512,1024]{2,1,0:T(8,128)(2,1)S(1)}) custom-call(s32[1]{0:T(128)} %bitcast.charged_ref, bf16[1024,512]{1,0:T(8,128)(2,1)S(1)} %collective-permute-done.1.psi_ref, bf16[4,512,1024]{2,1,0:T(8,128)(2,1)S(1)} %get-tuple-element.28.lefts_ref.upper_ref, ...), custom_call_target="tpu_custom_call" | custom-call | flops 3221225472 | bytes 6291456 | tf_op jit(solution)/shard_map/pallas_call | solution.py:247
  22.9 4.1 %collective-permute-start.3 = (bf16[512,512]{1,0:T(8,128)(2,1)S(1)}, bf16[512,512]{1,0:T(8,128)(2,1)S(1)}, u32[]{:S(2)}, u32[]{:S(2)}) collective-permute-start(bf16[512,512]{1,0:T(8,128)(2,1)S(1)} %get-tuple-element.32.after_ref), channel_id=1, source_target_pairs={{2,1},{4,3},{6,5},{9,10},{10,9},{11,12},{12,11},{13,14},{14,13},{1... | collective-permute-start | bytes 1572872 | tf_op jit(solution)/shard_map/ppermute | solution.py:254
  27.0 3.4 %shard_map.39 = (bf16[512,512]{1,0:T(8,128)(2,1)S(1)}, bf16[1,1024,1024]{2,1,0:T(8,128)(2,1)S(1)}, bf16[1,512,512]{2,1,0:T(8,128)(2,1)S(1)}) custom-call(bf16[1024,512]{1,0:T(8,128)(2,1)S(1)} %collective-permute-done.1.psi_ref, bf16[4,512,1024]{2,1,0:T(8,128)(2,1)S(1)} %get-tuple-element.31.lefts_ref.lower_ref, ...), custom_call_target="tpu_custom_call" | custom-call | flops 3221225472 | bytes 6291456 | tf_op jit(solution)/shard_map/pallas_call | solution.py:256
  30.5 2.5 %collective-permute-start.4 = (bf16[512,512]{1,0:T(8,128)(2,1)S(1)}, bf16[512,512]{1,0:T(8,128)(2,1)S(1)}, u32[]{:S(2)}, u32[]{:S(2)}) collective-permute-start(bf16[512,512]{1,0:T(8,128)(2,1)S(1)} %get-tuple-element.35.after_ref), channel_id=1, source_target_pairs={{2,1},{4,3},{6,5},{9,10},{10,9},{11,12},{12,11},{13,14},{14,13},{1... | collective-permute-start | bytes 1572872 | tf_op jit(solution)/shard_map/ppermute | solution.py:263
  33.0 5.4 %shard_map.40.start_ref = f32[1024,512]{1,0:T(8,128)S(1)} custom-call(bf16[1024,512]{1,0:T(8,128)(2,1)S(1)} %get-tuple-element.25.psi_ref, bf16[1,1024,1024]{2,1,0:T(8,128)(2,1)S(1)} %get-tuple-element.33.left0_ref, bf16[1,512,512]{2,1,0:T(8,128)(2,1)S(1)} %get-tuple-element.34.right0_ref, ...), custom_call_target="tpu_custom_call", output_to_operand_aliasing={{}: (5, {})} | custom-call | flops 4831838208 | bytes 7864320 | tf_op jit(solution)/shard_map/pallas_call | solution.py:265
  38.5 0.0 collective-permute-done.psi_ref
  38.5 1.0 %collective-permute-done.3.received_ref = bf16[512,512]{1,0:T(8,128)(2,1)S(1)} collective-permute-done((bf16[512,512]{1,0:T(8,128)(2,1)S(1)}, bf16[512,512]{1,0:T(8,128)(2,1)S(1)}, u32[]{:S(2)}, u32[]{:S(2)}) %collective-permute-start.3) | collective-permute-done | bytes 524320 | tf_op jit(solution)/shard_map/ppermute | solution.py:254
  39.5 0.0 collective-permute-done.2.rights_ref
  39.5 6.8 %shard_map.41 = (bf16[1024,512]{1,0:T(8,128)(2,1)}, f32[512,512]{1,0:T(8,128)S(1)}) custom-call(bf16[1024,512]{1,0:T(8,128)(2,1)S(1)} %collective-permute-done.psi_ref, bf16[4,512,1024]{2,1,0:T(8,128)(2,1)S(1)} %get-tuple-element.28.lefts_ref.upper_ref, bf16[4,512,1024]{2,1,0:T(8,128)(2,1)S(1)} %get-tuple-element.31.lefts_ref.lower_ref, ...), custom_call_target="tpu_custom_call" | custom-call | flops 6442450944 | bytes 10485760 | tf_op jit(solution)/shard_map/pallas_call | solution.py:274
  46.3 4.4 %collective-permute-done.4.received_ref = bf16[512,512]{1,0:T(8,128)(2,1)S(1)} collective-permute-done((bf16[512,512]{1,0:T(8,128)(2,1)S(1)}, bf16[512,512]{1,0:T(8,128)(2,1)S(1)}, u32[]{:S(2)}, u32[]{:S(2)}) %collective-permute-start.4) | collective-permute-done | bytes 524320 | tf_op jit(solution)/shard_map/ppermute | solution.py:263
  50.7 0.9 %shard_map.42 = bf16[1024,512]{1,0:T(8,128)(2,1)} custom-call(f32[512,512]{1,0:T(8,128)S(1)} %get-tuple-element.39.total_ref, bf16[512,512]{1,0:T(8,128)(2,1)S(1)} %collective-permute-done.4.received_ref, bf16[1024,512]{1,0:T(8,128)(2,1)} %get-tuple-element.40.start_ref), custom_call_target="tpu_custom_call", output_to_operand_aliasing={{}: (2, {})} | custom-call | tf_op jit(solution)/shard_map/pallas_call | solution.py:282
Async XLA Ops:
  0.0 17.8 %collective-permute-start.1 = (bf16[1024,512]{1,0:T(8,128)(2,1)}, bf16[1024,512]{1,0:T(8,128)(2,1)S(1)}, u32[]{:S(2)}, u32[]{:S(2)}) collective-permute-start(bf16[1024,512]{1,0:T(8,128)(2,1)} %whole_ref.1), channel_id=1, source_target_pairs={{8,0},{10,2},{12,4},{14,6},{16,8},{1,9},{18,10},{3,11},{20,12},{5,... | collective-permute-start | bytes 3145736 | tf_op jit(solution)/shard_map/ppermute | solution.py:232
  3.2 1.2 %copy-start = (bf16[1024,512]{1,0:T(8,128)(2,1)S(1)}, bf16[1024,512]{1,0:T(8,128)(2,1)}, u32[]{:S(2)}) copy-start(bf16[1024,512]{1,0:T(8,128)(2,1)} %whole_ref.1) | copy-start | bytes 3145732
  15.2 24.3 %collective-permute-start.2 = (bf16[4,512,512]{2,1,0:T(8,128)(2,1)S(1)}, bf16[4,512,512]{2,1,0:T(8,128)(2,1)S(1)}, u32[]{:S(2)}, u32[]{:S(2)}) collective-permute-start(bf16[4,512,512]{2,1,0:T(8,128)(2,1)S(1)} %get-tuple-element.37), channel_id=1, source_target_pairs={{1,0},{0,1},{3,2},{2,3},{5,4},{4,5},{7,6},{6,7},{9,8},{8,9},{11,10... | collective-permute-start | bytes 6291464 | tf_op jit(solution)/shard_map/ppermute | solution.py:245
  15.3 23.2 %collective-permute-start = (bf16[1024,512]{1,0:T(8,128)(2,1)S(1)}, bf16[1024,512]{1,0:T(8,128)(2,1)S(1)}, u32[]{:S(2)}, u32[]{:S(2)}) collective-permute-start(bf16[1024,512]{1,0:T(8,128)(2,1)S(1)} %copy-done), channel_id=1, source_target_pairs={{9,0},{11,2},{13,4},{15,6},{17,8},{0,9},{19,10},{2,11},{21,12},{4,... | collective-permute-start | bytes 3145736 | tf_op jit(solution)/shard_map/ppermute | solution.py:244
  22.9 16.6 %collective-permute-start.3 = (bf16[512,512]{1,0:T(8,128)(2,1)S(1)}, bf16[512,512]{1,0:T(8,128)(2,1)S(1)}, u32[]{:S(2)}, u32[]{:S(2)}) collective-permute-start(bf16[512,512]{1,0:T(8,128)(2,1)S(1)} %get-tuple-element.32.after_ref), channel_id=1, source_target_pairs={{2,1},{4,3},{6,5},{9,10},{10,9},{11,12},{12,11},{13,14},{14,13},{1... | collective-permute-start | bytes 1572872 | tf_op jit(solution)/shard_map/ppermute | solution.py:254
  30.5 20.2 %collective-permute-start.4 = (bf16[512,512]{1,0:T(8,128)(2,1)S(1)}, bf16[512,512]{1,0:T(8,128)(2,1)S(1)}, u32[]{:S(2)}, u32[]{:S(2)}) collective-permute-start(bf16[512,512]{1,0:T(8,128)(2,1)S(1)} %get-tuple-element.35.after_ref), channel_id=1, source_target_pairs={{2,1},{4,3},{6,5},{9,10},{10,9},{11,12},{12,11},{13,14},{14,13},{1... | collective-permute-start | bytes 1572872 | tf_op jit(solution)/shard_map/ppermute | solution.py:263

commit v5 on v4

--- a/solution.py
+++ b/solution.py
@@ -76,34 +76,26 @@
 
 
 def local_kernel(charged_ref, whole_ref, left_ref, right_ref, total_ref, psi_ref, next_left_ref,
-                 next_right_ref, give_ref, lefts_ref, rights_ref, sems):
+                 lower_ref, next_right_ref, give_ref, lefts_ref, rights_ref, sems):
     charged = charged_ref[0]
     fetch = Fetch(sems)
     steps = lefts_ref.shape[0]
-    part = total_ref.shape[0] // 2
-    halves = (pl.ds(0, part), pl.ds(part, part))
-    tops = fetch.start((whole_ref, psi_ref))
-    tops += fetch.start((left_ref.at[0, halves[0], :], lefts_ref.at[0, halves[0], :]))
-    tops += fetch.start((right_ref.at[0], rights_ref.at[0]))
-    bottom = fetch.start((left_ref.at[0, halves[1], :], lefts_ref.at[0, halves[1], :]))
     bring = lambda step: fetch.start(
         *local_blocks(left_ref, right_ref, lefts_ref, rights_ref, step, step)
     )
-    coming = {step: bring(step) for step in range(1, min(3, steps))}
-    for half, copies in zip(halves, (tops, bottom)):
-        wait(copies)
-        total_ref[half, :] = contract(lefts_ref[0, half, :], psi_ref[...], rights_ref[0])
+    coming = {0: fetch.start((whole_ref, psi_ref)) + bring(0)}
     last = []
-    for step in range(1, steps):
+    for step in range(steps):
         wait(coming[step])
-        if step + 2 < steps:
-            coming[step + 2] = bring(step + 2)
-        if step == max(1, steps - 3):
+        for more in range(1, steps) if step == 0 else ():
+            coming[more] = bring(more)
+        if step == 1:
+            last += fetch.start(*right_blocks(right_ref, next_right_ref, charged))
             last += fetch.start(*half_blocks(left_ref, next_left_ref, charged, 0))
-        if step == max(1, steps - 2):
-            last += fetch.start(*right_blocks(right_ref, next_right_ref, charged))
+            last += fetch.start(*half_blocks(left_ref, lower_ref, charged, 1))
             last += fetch.start(*right_blocks(right_ref, give_ref, period - 1 - charged))
-        total_ref[...] += contract(lefts_ref[step], psi_ref[...], rights_ref[step])
+        term = contract(lefts_ref[step], psi_ref[...], rights_ref[step])
+        total_ref[...] = total_ref[...] + term if step else term
     wait(last)
 
 
@@ -118,12 +110,9 @@
             term_ref[...] = total.astype(term_ref.dtype)
 
 
-def first_kernel(charged_ref, psi_ref, lefts_ref, rights_ref, left_ref, after_ref,
-                 term_ref, next_left_ref, total_ref, sems):
+def first_kernel(psi_ref, lefts_ref, rights_ref, after_ref, term_ref, total_ref):
     del after_ref
-    coming = Fetch(sems).start(*half_blocks(left_ref, next_left_ref, charged_ref[0], 1))
     early_term(psi_ref, lefts_ref, rights_ref, term_ref, total_ref)
-    wait(coming)
 
 
 def second_kernel(psi_ref, lefts_ref, rights_ref, left_ref, right_ref, after_ref,
@@ -181,7 +170,7 @@
     put.wait()
 
 
-def pairs(left_count, right_count):
+def routes(left_count, right_count):
     index = lambda i, j: i * right_count + j
     straight, crossed, partner, along = [], [], [], []
     for i in range(left_count):
@@ -198,7 +187,7 @@
 
 def shards(left_count, right_count, psi, left_whole, right_whole):
     axes = ("lsec", "rsec")
-    straight, crossed, partner, along = pairs(left_count, right_count)
+    straight, crossed, partner, along = routes(left_count, right_count)
     rows, columns = psi.shape
     channels = left_whole.shape[0]
     charged_count, local_rest = channels // period, channels // 2 - local_first
@@ -231,26 +220,24 @@
 
     moved = lax.ppermute(psi, axes, straight)
 
-    total, kept, upper, own, give = call(
+    total, kept, upper, lower, own, give = call(
         local_kernel,
         [in_smem, in_hbm, in_hbm, in_hbm],
-        [total_shape, pltpu.VMEM((rows, columns), bf16), halves, rights(charged_count), rights(charged_count)],
+        [total_shape, pltpu.VMEM((rows, columns), bf16), halves, halves, rights(charged_count), rights(charged_count)],
         [lefts(local_first), rights(local_first),
-         sems(2 * local_first + 2 + 3 * charged_count)],
+         sems(2 * local_first + 1 + 4 * charged_count)],
         cost(local_first, rows, rows, columns),
-    )(charged, psi, left_env, right_env)
-
-    psi_after, total = lax.optimization_barrier((psi, total))
-    moved_across = lax.ppermute(psi_after, axes, crossed)
-    across = lax.ppermute(give, axes, partner)
+    )(charged, pltpu.with_memory_space_constraint(psi, pltpu.HBM), left_env, right_env)
+
+    moved_across = lax.ppermute(kept, axes, crossed)
     moved, total = lax.optimization_barrier((moved, total))
-    first, lower = call(
+    (first,) = call(
         first_kernel,
-        [in_smem, in_vmem, in_vmem, in_vmem, in_hbm, in_hbm],
-        [half_block, halves],
-        [half_total, sems(charged_count)],
+        [in_vmem, in_vmem, in_vmem, in_hbm],
+        [half_block],
+        [half_total],
         cost(charged_count, part, rows, columns),
-    )(charged, moved, upper, own, left_env, total)
+    )(moved, upper, own, total)
     first_received = lax.ppermute(first, axes, along)
 
     second, rest_left, rest_right = call(
@@ -261,6 +248,7 @@
         cost(charged_count, part, rows, columns),
     )(moved, lower, own, left_env, right_env, first)
     second_received = lax.ppermute(second, axes, along)
+    across = lax.ppermute(give, axes, partner)
 
     (total,) = call(
         rest_kernel,

time: 52 us -> 49.5 us (0.952)
  the two profiles are of different devices: /device:TPU:11 before, /device:TPU:19 now
where the time goes in v5:
time: 49.5 us; the launch traced here: 49.3 us
  Pallas kernels  31.3 us (63%)
  starting transfers between devices  12.3 us (25%)
  waiting for transfers between devices  5.38 us (11%)
    pallas_call x1, Pallas kernels, shards(): call(local_kernel, [in_smem, in_hbm, in_hbm, in_hbm], [total_shape, pltpu...  11.2 us
    pallas_call x1, Pallas kernels, shards(): call(late_kernel, [in_vmem] * 6, [pltpu.VMEM((rows, columns), bf16), half...  6.91 us
    pallas_call x1, Pallas kernels, shards(): call(rest_kernel, [in_vmem, in_vmem, in_vmem, in_hbm, in_hbm, in_vmem, in...  5.43 us
    ppermute x1, waiting for transfers between devices, shards(): second_received = lax.ppermute(second, axes, along)  4.31 us
    ppermute x1, starting transfers between devices, shards(): first_received = lax.ppermute(first, axes, along)  4.02 us
    pallas_call x1, Pallas kernels, shards(): call(second_kernel, [in_vmem, in_vmem, in_vmem, in_hbm, in_hbm, in_hbm],...  3.46 us
    pallas_call x1, Pallas kernels, shards(): call(first_kernel, [in_vmem, in_vmem, in_vmem, in_hbm], [half_block], [ha...  3.43 us
    ppermute x1, starting transfers between devices, shards(): moved = lax.ppermute(psi, axes, straight)  3.19 us
  transfers between devices with their start and end apart: 5, of which 2 were waited for; matrix products, arithmetic and copies ran while one was open for 0% of the time, Pallas kernels for 62%

profile of v5, /device:TPU:19, one launch (start us, length us, event | category | flops | bytes accessed | tf_op | source)
XLA Modules:
  0.0 49.3 jit_solution(11121842353755623041)
XLA Ops:
  0.0 3.2 %collective-permute-start.1 = (bf16[1024,512]{1,0:T(8,128)(2,1)}, bf16[1024,512]{1,0:T(8,128)(2,1)S(1)}, u32[]{:S(2)}, u32[]{:S(2)}) collective-permute-start(bf16[1024,512]{1,0:T(8,128)(2,1)} %whole_ref.1), channel_id=1, source_target_pairs={{8,0},{10,2},{12,4},{14,6},{16,8},{1,9},{18,10},{3,11},{20,12},{5,... | collective-permute-start | bytes 3145736 | tf_op jit(solution)/shard_map/ppermute | solution.py:221
  3.2 11.2 %shard_map.37 = (f32[1024,512]{1,0:T(8,128)S(1)}, bf16[1024,512]{1,0:T(8,128)(2,1)S(1)}, bf16[4,512,1024]{2,1,0:T(8,128)(2,1)S(1)}, bf16[4,512,1024]{2,1,0:T(8,1...) custom-call(s32[1]{0:T(128)} %bitcast.charged_ref, bf16[1024,512]{1,0:T(8,128)(2,1)} %whole_ref.1, ...), custom_call_target="tpu_custom_call" | custom-call | flops 8053063680 | bytes 13107200 | tf_op jit(solution)/shard_map/pallas_call | solution.py:223
  14.4 0.1 collective-permute-start.2
  14.5 2.4 %collective-permute-start = (bf16[1024,512]{1,0:T(8,128)(2,1)S(1)}, bf16[1024,512]{1,0:T(8,128)(2,1)S(1)}, u32[]{:S(2)}, u32[]{:S(2)}) collective-permute-start(bf16[1024,512]{1,0:T(8,128)(2,1)S(1)} %get-tuple-element.20.psi_ref), channel_id=1, source_target_pairs={{9,0},{11,2},{13,4},{15,6},{17,8},{0,9},{19,10},{2,11},{21,12},{4,... | collective-permute-start | bytes 3145736 | tf_op jit(solution)/shard_map/ppermute | solution.py:232
  17.0 0.0 collective-permute-done.1.psi_ref
  17.0 3.4 %shard_map.38.after_ref = bf16[512,512]{1,0:T(8,128)(2,1)S(1)} custom-call(bf16[1024,512]{1,0:T(8,128)(2,1)S(1)} %collective-permute-done.1.psi_ref, bf16[4,512,1024]{2,1,0:T(8,128)(2,1)S(1)} %get-tuple-element.25.lefts_ref.upper_ref, bf16[4,512,512]{2,1,0:T(8,128)(2,1)S(1)} %get-tuple-element.24.rights_ref, ...), custom_call_target="tpu_custom_call" | custom-call | flops 3221225472 | bytes 6291456 | tf_op jit(solution)/shard_map/pallas_call | solution.py:234
  20.4 4.0 %collective-permute-start.3 = (bf16[512,512]{1,0:T(8,128)(2,1)S(1)}, bf16[512,512]{1,0:T(8,128)(2,1)S(1)}, u32[]{:S(2)}, u32[]{:S(2)}) collective-permute-start(bf16[512,512]{1,0:T(8,128)(2,1)S(1)} %shard_map.38.after_ref), channel_id=1, source_target_pairs={{2,1},{4,3},{6,5},{9,10},{10,9},{11,12},{12,11},{13,14},{14,13},{1... | collective-permute-start | bytes 1572872 | tf_op jit(solution)/shard_map/ppermute | solution.py:241
  24.5 3.5 %shard_map.39 = (bf16[512,512]{1,0:T(8,128)(2,1)S(1)}, bf16[1,1024,1024]{2,1,0:T(8,128)(2,1)S(1)}, bf16[1,512,512]{2,1,0:T(8,128)(2,1)S(1)}) custom-call(bf16[1024,512]{1,0:T(8,128)(2,1)S(1)} %collective-permute-done.1.psi_ref, bf16[4,512,1024]{2,1,0:T(8,128)(2,1)S(1)} %get-tuple-element.23.lefts_ref.lower_ref, ...), custom_call_target="tpu_custom_call" | custom-call | flops 3221225472 | bytes 6291456 | tf_op jit(solution)/shard_map/pallas_call | solution.py:243
  27.9 2.6 %collective-permute-start.4 = (bf16[512,512]{1,0:T(8,128)(2,1)S(1)}, bf16[512,512]{1,0:T(8,128)(2,1)S(1)}, u32[]{:S(2)}, u32[]{:S(2)}) collective-permute-start(bf16[512,512]{1,0:T(8,128)(2,1)S(1)} %get-tuple-element.29.after_ref), channel_id=1, source_target_pairs={{2,1},{4,3},{6,5},{9,10},{10,9},{11,12},{12,11},{13,14},{14,13},{1... | collective-permute-start | bytes 1572872 | tf_op jit(solution)/shard_map/ppermute | solution.py:250
  30.5 5.4 %shard_map.40.start_ref = f32[1024,512]{1,0:T(8,128)S(1)} custom-call(bf16[1024,512]{1,0:T(8,128)(2,1)S(1)} %get-tuple-element.20.psi_ref, bf16[1,1024,1024]{2,1,0:T(8,128)(2,1)S(1)} %get-tuple-element.27.left0_ref, bf16[1,512,512]{2,1,0:T(8,128)(2,1)S(1)} %get-tuple-element.28.right0_ref, ...), custom_call_target="tpu_custom_call", output_to_operand_aliasing={{}: (5, {})} | custom-call | flops 4831838208 | bytes 7864320 | tf_op jit(solution)/shard_map/pallas_call | solution.py:253
  36.0 0.0 collective-permute-done.psi_ref
  36.0 1.1 %collective-permute-done.3.received_ref = bf16[512,512]{1,0:T(8,128)(2,1)S(1)} collective-permute-done((bf16[512,512]{1,0:T(8,128)(2,1)S(1)}, bf16[512,512]{1,0:T(8,128)(2,1)S(1)}, u32[]{:S(2)}, u32[]{:S(2)}) %collective-permute-start.3) | collective-permute-done | bytes 524320 | tf_op jit(solution)/shard_map/ppermute | solution.py:241
  37.1 0.0 collective-permute-done.2.rights_ref
  37.1 6.9 %shard_map.41 = (bf16[1024,512]{1,0:T(8,128)(2,1)}, f32[512,512]{1,0:T(8,128)S(1)}) custom-call(bf16[1024,512]{1,0:T(8,128)(2,1)S(1)} %collective-permute-done.psi_ref, bf16[4,512,1024]{2,1,0:T(8,128)(2,1)S(1)} %get-tuple-element.25.lefts_ref.upper_ref, bf16[4,512,1024]{2,1,0:T(8,128)(2,1)S(1)} %get-tuple-element.23.lefts_ref.lower_ref, ...), custom_call_target="tpu_custom_call" | custom-call | flops 6442450944 | bytes 10485760 | tf_op jit(solution)/shard_map/pallas_call | solution.py:262
  44.0 4.3 %collective-permute-done.4.received_ref = bf16[512,512]{1,0:T(8,128)(2,1)S(1)} collective-permute-done((bf16[512,512]{1,0:T(8,128)(2,1)S(1)}, bf16[512,512]{1,0:T(8,128)(2,1)S(1)}, u32[]{:S(2)}, u32[]{:S(2)}) %collective-permute-start.4) | collective-permute-done | bytes 524320 | tf_op jit(solution)/shard_map/ppermute | solution.py:250
  48.3 0.9 %shard_map.42 = bf16[1024,512]{1,0:T(8,128)(2,1)} custom-call(f32[512,512]{1,0:T(8,128)S(1)} %get-tuple-element.33.total_ref, bf16[512,512]{1,0:T(8,128)(2,1)S(1)} %collective-permute-done.4.received_ref, bf16[1024,512]{1,0:T(8,128)(2,1)} %get-tuple-element.34.start_ref), custom_call_target="tpu_custom_call", output_to_operand_aliasing={{}: (2, {})} | custom-call | tf_op jit(solution)/shard_map/pallas_call | solution.py:270
Async XLA Ops:
  0.0 17.0 %collective-permute-start.1 = (bf16[1024,512]{1,0:T(8,128)(2,1)}, bf16[1024,512]{1,0:T(8,128)(2,1)S(1)}, u32[]{:S(2)}, u32[]{:S(2)}) collective-permute-start(bf16[1024,512]{1,0:T(8,128)(2,1)} %whole_ref.1), channel_id=1, source_target_pairs={{8,0},{10,2},{12,4},{14,6},{16,8},{1,9},{18,10},{3,11},{20,12},{5,... | collective-permute-start | bytes 3145736 | tf_op jit(solution)/shard_map/ppermute | solution.py:221
  14.4 22.6 %collective-permute-start.2 = (bf16[4,512,512]{2,1,0:T(8,128)(2,1)S(1)}, bf16[4,512,512]{2,1,0:T(8,128)(2,1)S(1)}, u32[]{:S(2)}, u32[]{:S(2)}) collective-permute-start(bf16[4,512,512]{2,1,0:T(8,128)(2,1)S(1)} %get-tuple-element.31), channel_id=1, source_target_pairs={{1,0},{0,1},{3,2},{2,3},{5,4},{4,5},{7,6},{6,7},{9,8},{8,9},{11,10... | collective-permute-start | bytes 6291464 | tf_op jit(solution)/shard_map/ppermute | solution.py:251
  14.5 21.5 %collective-permute-start = (bf16[1024,512]{1,0:T(8,128)(2,1)S(1)}, bf16[1024,512]{1,0:T(8,128)(2,1)S(1)}, u32[]{:S(2)}, u32[]{:S(2)}) collective-permute-start(bf16[1024,512]{1,0:T(8,128)(2,1)S(1)} %get-tuple-element.20.psi_ref), channel_id=1, source_target_pairs={{9,0},{11,2},{13,4},{15,6},{17,8},{0,9},{19,10},{2,11},{21,12},{4,... | collective-permute-start | bytes 3145736 | tf_op jit(solution)/shard_map/ppermute | solution.py:232
  20.4 16.6 %collective-permute-start.3 = (bf16[512,512]{1,0:T(8,128)(2,1)S(1)}, bf16[512,512]{1,0:T(8,128)(2,1)S(1)}, u32[]{:S(2)}, u32[]{:S(2)}) collective-permute-start(bf16[512,512]{1,0:T(8,128)(2,1)S(1)} %shard_map.38.after_ref), channel_id=1, source_target_pairs={{2,1},{4,3},{6,5},{9,10},{10,9},{11,12},{12,11},{13,14},{14,13},{1... | collective-permute-start | bytes 1572872 | tf_op jit(solution)/shard_map/ppermute | solution.py:241
  27.9 20.4 %collective-permute-start.4 = (bf16[512,512]{1,0:T(8,128)(2,1)S(1)}, bf16[512,512]{1,0:T(8,128)(2,1)S(1)}, u32[]{:S(2)}, u32[]{:S(2)}) collective-permute-start(bf16[512,512]{1,0:T(8,128)(2,1)S(1)} %get-tuple-element.29.after_ref), channel_id=1, source_target_pairs={{2,1},{4,3},{6,5},{9,10},{10,9},{11,12},{12,11},{13,14},{14,13},{1... | collective-permute-start | bytes 1572872 | tf_op jit(solution)/shard_map/ppermute | solution.py:250

commit v6 on v5

--- a/solution.py
+++ b/solution.py
@@ -11,6 +11,7 @@
 channel_shifts = (0, 1, -1, 0)
 period = len(channel_shifts)
 local_first = 5
+first_eighths = 3
 in_vmem = pl.BlockSpec(memory_space=pltpu.VMEM)
 in_smem = pl.BlockSpec(memory_space=pltpu.SMEM)
 in_hbm = pl.BlockSpec(memory_space=pl.ANY)
@@ -52,11 +53,11 @@
         copy.wait()
 
 
-def half_blocks(left_ref, target_ref, charged, half):
-    steps, part = target_ref.shape[:2]
+def row_blocks(left_ref, target_ref, charged, first_row):
+    steps, count = target_ref.shape[:2]
+    rows = pl.ds(first_row, count)
     return [
-        (left_ref.at[period * w + charged, pl.ds(half * part, part), :], target_ref.at[w])
-        for w in range(steps)
+        (left_ref.at[period * w + charged, rows, :], target_ref.at[w]) for w in range(steps)
     ]
 
 
@@ -84,18 +85,26 @@
         *local_blocks(left_ref, right_ref, lefts_ref, rights_ref, step, step)
     )
     coming = {0: fetch.start((whole_ref, psi_ref)) + bring(0)}
+    extra = [
+        row_blocks(left_ref, next_left_ref, charged, 0),
+        row_blocks(left_ref, lower_ref, charged, next_left_ref.shape[1]),
+        right_blocks(right_ref, next_right_ref, charged),
+        right_blocks(right_ref, give_ref, period - 1 - charged),
+    ]
     last = []
     for step in range(steps):
-        wait(coming[step])
-        for more in range(1, steps) if step == 0 else ():
-            coming[more] = bring(more)
-        if step == 1:
-            last += fetch.start(*right_blocks(right_ref, next_right_ref, charged))
-            last += fetch.start(*half_blocks(left_ref, next_left_ref, charged, 0))
-            last += fetch.start(*half_blocks(left_ref, lower_ref, charged, 1))
-            last += fetch.start(*right_blocks(right_ref, give_ref, period - 1 - charged))
+        if step % 2 or step == 0:
+            for near in range(step, min(step + 1 + (step > 0), steps)):
+                wait(coming[near])
+            begin = step + 1 + (step > 0)
+            for far in range(begin, min(begin + 2, steps)):
+                coming[far] = bring(far)
+        if step > 1 and extra:
+            last += fetch.start(*extra.pop(0), *extra.pop(0))
         term = contract(lefts_ref[step], psi_ref[...], rights_ref[step])
         total_ref[...] = total_ref[...] + term if step else term
+    for blocks in extra:
+        last += fetch.start(*blocks)
     wait(last)
 
 
@@ -135,39 +144,47 @@
         for slot in range(count)
     ]
     total_ref[...] = start_ref[...] + contract(left0_ref[0], psi_ref[...], right0_ref[0])
+    wait(sum(coming, []))
     for slot in range(count):
-        wait(coming[slot])
         total_ref[...] += contract(lefts_ref[slot], psi_ref[...], rights_ref[slot])
 
 
 def late_kernel(psi_ref, upper_ref, lower_ref, rights_ref, start_ref, received_ref,
                 out_ref, total_ref, work_ref, ready_ref, sem):
-    part = total_ref.shape[0]
     steps = rights_ref.shape[0]
-    put = pltpu.make_async_copy(ready_ref, out_ref.at[pl.ds(0, part), :], sem)
-    for half, lefts_ref in enumerate((upper_ref, lower_ref)):
-        for step in range(steps):
-            old = start_ref[half * part:(half + 1) * part, :] if step == 0 else work_ref[...]
-            total = old + contract(lefts_ref[step], psi_ref[...], rights_ref[step])
-            if step + 1 < steps:
-                work_ref[...] = total
-            elif half:
-                total_ref[...] = total
-            else:
-                total = total + received_ref[...].astype(jnp.float32)
-                ready_ref[...] = total.astype(ready_ref.dtype)
-                put.start()
+    count = work_ref.shape[0]
+    put = pltpu.make_async_copy(ready_ref, out_ref.at[pl.ds(0, count), :], sem)
+    for step in range(steps):
+        old = work_ref[...] if step else start_ref[:count, :]
+        total = old + contract(upper_ref[step], psi_ref[...], rights_ref[step])
+        if step + 1 < steps:
+            work_ref[...] = total
+        else:
+            total = total + received_ref[...].astype(jnp.float32)
+            ready_ref[...] = total.astype(ready_ref.dtype)
+    put.start()
+    for step in range(steps):
+        old = total_ref[...] if step else start_ref[count:, :]
+        total_ref[...] = old + contract(lower_ref[step], psi_ref[...], rights_ref[step])
     put.wait()
 
 
-def finish_kernel(total_ref, received_ref, start_ref, out_ref, ready_ref, sem):
+def finish_kernel(total_ref, received_ref, start_ref, out_ref, ready_ref, sems):
     del start_ref
-    part = total_ref.shape[0]
-    total = total_ref[...] + received_ref[...].astype(jnp.float32)
-    ready_ref[...] = total.astype(ready_ref.dtype)
-    put = pltpu.make_async_copy(ready_ref, out_ref.at[pl.ds(part, part), :], sem)
-    put.start()
-    put.wait()
+    count = total_ref.shape[0]
+    first_row, part = out_ref.shape[0] - count, count // 2
+    puts = []
+    for half in range(2):
+        rows = slice(half * part, (half + 1) * part)
+        total = total_ref[rows, :] + received_ref[rows, :].astype(jnp.float32)
+        ready_ref[rows, :] = total.astype(ready_ref.dtype)
+        puts.append(pltpu.make_async_copy(
+            ready_ref.at[pl.ds(half * part, part), :],
+            out_ref.at[pl.ds(first_row + half * part, part), :],
+            sems.at[half],
+        ))
+        puts[-1].start()
+    wait(puts)
 
 
 def routes(left_count, right_count):
@@ -191,10 +208,11 @@
     rows, columns = psi.shape
     channels = left_whole.shape[0]
     charged_count, local_rest = channels // period, channels // 2 - local_first
-    part = rows // 2
+    above = rows * first_eighths // 8
+    below = rows - above
     f32, bf16 = jnp.float32, jnp.bfloat16
     lefts = lambda count: pltpu.VMEM((count, rows, rows), bf16)
-    halves = pltpu.VMEM((charged_count, part, rows), bf16)
+    row_parts = [pltpu.VMEM((charged_count, count, rows), bf16) for count in (above, below)]
     rights = lambda count: pltpu.VMEM((count, columns, columns), bf16)
     shape = lambda ref: jax.ShapeDtypeStruct(ref.shape, ref.dtype)
     sems = lambda count: pltpu.SemaphoreType.DMA((count,))
@@ -215,15 +233,16 @@
     left_env = pltpu.with_memory_space_constraint(left_whole, pltpu.HBM)
     right_env = pltpu.with_memory_space_constraint(right_whole, pltpu.HBM)
     total_shape = pltpu.VMEM((rows, columns), f32)
-    half_total = pltpu.VMEM((part, columns), f32)
-    half_block = pltpu.VMEM((part, columns), bf16)
+    totals = [pltpu.VMEM((count, columns), f32) for count in (above, below)]
+    blocks = [pltpu.VMEM((count, columns), bf16) for count in (above, below)]
 
     moved = lax.ppermute(psi, axes, straight)
 
     total, kept, upper, lower, own, give = call(
         local_kernel,
         [in_smem, in_hbm, in_hbm, in_hbm],
-        [total_shape, pltpu.VMEM((rows, columns), bf16), halves, halves, rights(charged_count), rights(charged_count)],
+        [total_shape, pltpu.VMEM((rows, columns), bf16), *row_parts, rights(charged_count),
+         rights(charged_count)],
         [lefts(local_first), rights(local_first),
          sems(2 * local_first + 1 + 4 * charged_count)],
         cost(local_first, rows, rows, columns),
@@ -234,18 +253,18 @@
     (first,) = call(
         first_kernel,
         [in_vmem, in_vmem, in_vmem, in_hbm],
-        [half_block],
-        [half_total],
-        cost(charged_count, part, rows, columns),
+        [blocks[0]],
+        [totals[0]],
+        cost(charged_count, above, rows, columns),
     )(moved, upper, own, total)
     first_received = lax.ppermute(first, axes, along)
 
     second, rest_left, rest_right = call(
         second_kernel,
         [in_vmem, in_vmem, in_vmem, in_hbm, in_hbm, in_hbm],
-        [half_block, lefts(1), rights(1)],
-        [half_total, sems(2)],
-        cost(charged_count, part, rows, columns),
+        [blocks[1], lefts(1), rights(1)],
+        [totals[1], sems(2)],
+        cost(charged_count, below, rows, columns),
     )(moved, lower, own, left_env, right_env, first)
     second_received = lax.ppermute(second, axes, along)
     across = lax.ppermute(give, axes, partner)
@@ -262,8 +281,8 @@
     out, total = call(
         late_kernel,
         [in_vmem] * 6,
-        [pltpu.VMEM((rows, columns), bf16), half_total],
-        [half_total, half_block, pltpu.SemaphoreType.DMA],
+        [pltpu.VMEM((rows, columns), bf16), totals[1]],
+        [totals[0], blocks[0], pltpu.SemaphoreType.DMA],
         cost(charged_count, rows, rows, columns),
         out_specs=[in_hbm, in_vmem],
     )(moved_across, upper, lower, across, total, first_received)
@@ -271,7 +290,7 @@
         finish_kernel,
         [in_vmem, in_vmem, in_hbm],
         [pltpu.VMEM((rows, columns), bf16)],
-        [half_block, pltpu.SemaphoreType.DMA],
+        [blocks[1], sems(2)],
         None,
         aliases={2: 0},
         out_specs=[in_hbm],

time: 49.5 us -> 49.7 us (level)
  the two profiles are of different devices: /device:TPU:19 before, /device:TPU:11 now
where the time goes in v6:
time: 49.7 us; the launch traced here: 49.5 us
  Pallas kernels  32.8 us (66%)
  starting transfers between devices  12.4 us (25%)
  waiting for transfers between devices  4.05 us (8%)
    pallas_call x1, Pallas kernels, shards(): call(local_kernel, [in_smem, in_hbm, in_hbm, in_hbm], [total_shape, pltpu...  11.6 us
    pallas_call x1, Pallas kernels, shards(): call(late_kernel, [in_vmem] * 6, [pltpu.VMEM((rows, columns), bf16), tota...  7.25 us
    pallas_call x1, Pallas kernels, shards(): call(rest_kernel, [in_vmem, in_vmem, in_vmem, in_hbm, in_hbm, in_vmem, in...  5.93 us
    pallas_call x1, Pallas kernels, shards(): call(second_kernel, [in_vmem, in_vmem, in_vmem, in_hbm, in_hbm, in_hbm],...  4.28 us
    ppermute x1, starting transfers between devices, shards(): first_received = lax.ppermute(first, axes, along)  4.09 us
    ppermute x1, waiting for transfers between devices, shards(): second_received = lax.ppermute(second, axes, along)  4.04 us
    ppermute x1, starting transfers between devices, shards(): moved = lax.ppermute(psi, axes, straight)  3.19 us
    pallas_call x1, Pallas kernels, shards(): call(first_kernel, [in_vmem, in_vmem, in_vmem, in_hbm], [blocks[0]], [tot...  2.82 us
  transfers between devices with their start and end apart: 5, of which 1 were waited for; matrix products, arithmetic and copies ran while one was open for 0% of the time, Pallas kernels for 64%

profile of v6, /device:TPU:11, one launch (start us, length us, event | category | flops | bytes accessed | tf_op | source)
XLA Modules:
  0.0 49.5 jit_solution(5307475990144601347)
XLA Ops:
  0.0 3.2 %collective-permute-start.1 = (bf16[1024,512]{1,0:T(8,128)(2,1)}, bf16[1024,512]{1,0:T(8,128)(2,1)S(1)}, u32[]{:S(2)}, u32[]{:S(2)}) collective-permute-start(bf16[1024,512]{1,0:T(8,128)(2,1)} %whole_ref.1), channel_id=1, source_target_pairs={{8,0},{10,2},{12,4},{14,6},{16,8},{1,9},{18,10},{3,11},{20,12},{5,... | collective-permute-start | bytes 3145736 | tf_op jit(solution)/shard_map/ppermute | solution.py:239
  3.2 11.6 %shard_map.37 = (f32[1024,512]{1,0:T(8,128)S(1)}, bf16[1024,512]{1,0:T(8,128)(2,1)S(1)}, bf16[4,384,1024]{2,1,0:T(8,128)(2,1)S(1)}, bf16[4,640,1024]{2,1,0:T(8,1...) custom-call(s32[1]{0:T(128)} %bitcast.charged_ref, bf16[1024,512]{1,0:T(8,128)(2,1)} %whole_ref.1, ...), custom_call_target="tpu_custom_call" | custom-call | flops 8053063680 | bytes 13107200 | tf_op jit(solution)/shard_map/pallas_call | solution.py:241
  14.8 0.1 collective-permute-start.2
  14.9 2.5 %collective-permute-start = (bf16[1024,512]{1,0:T(8,128)(2,1)S(1)}, bf16[1024,512]{1,0:T(8,128)(2,1)S(1)}, u32[]{:S(2)}, u32[]{:S(2)}) collective-permute-start(bf16[1024,512]{1,0:T(8,128)(2,1)S(1)} %get-tuple-element.20.psi_ref), channel_id=1, source_target_pairs={{9,0},{11,2},{13,4},{15,6},{17,8},{0,9},{19,10},{2,11},{21,12},{4,... | collective-permute-start | bytes 3145736 | tf_op jit(solution)/shard_map/ppermute | solution.py:251
  17.4 0.0 collective-permute-done.1.psi_ref
  17.4 2.8 %shard_map.38.after_ref = bf16[384,512]{1,0:T(8,128)(2,1)S(1)} custom-call(bf16[1024,512]{1,0:T(8,128)(2,1)S(1)} %collective-permute-done.1.psi_ref, bf16[4,384,1024]{2,1,0:T(8,128)(2,1)S(1)} %get-tuple-element.25.lefts_ref.upper_ref, bf16[4,512,512]{2,1,0:T(8,128)(2,1)S(1)} %get-tuple-element.24.rights_ref, ...), custom_call_target="tpu_custom_call" | custom-call | flops 2415919104 | bytes 5242880 | tf_op jit(solution)/shard_map/pallas_call | solution.py:253
  20.3 4.1 %collective-permute-start.3 = (bf16[384,512]{1,0:T(8,128)(2,1)S(1)}, bf16[384,512]{1,0:T(8,128)(2,1)S(1)}, u32[]{:S(2)}, u32[]{:S(2)}) collective-permute-start(bf16[384,512]{1,0:T(8,128)(2,1)S(1)} %shard_map.38.after_ref), channel_id=1, source_target_pairs={{2,1},{4,3},{6,5},{9,10},{10,9},{11,12},{12,11},{13,14},{14,13},{1... | collective-permute-start | bytes 1179656 | tf_op jit(solution)/shard_map/ppermute | solution.py:260
  24.4 4.3 %shard_map.39 = (bf16[640,512]{1,0:T(8,128)(2,1)S(1)}, bf16[1,1024,1024]{2,1,0:T(8,128)(2,1)S(1)}, bf16[1,512,512]{2,1,0:T(8,128)(2,1)S(1)}) custom-call(bf16[1024,512]{1,0:T(8,128)(2,1)S(1)} %collective-permute-done.1.psi_ref, bf16[4,640,1024]{2,1,0:T(8,128)(2,1)S(1)} %get-tuple-element.23.lefts_ref.lower_ref, ...), custom_call_target="tpu_custom_call" | custom-call | flops 4026531840 | bytes 7340032 | tf_op jit(solution)/shard_map/pallas_call | solution.py:262
  28.6 2.6 %collective-permute-start.4 = (bf16[640,512]{1,0:T(8,128)(2,1)S(1)}, bf16[640,512]{1,0:T(8,128)(2,1)S(1)}, u32[]{:S(2)}, u32[]{:S(2)}) collective-permute-start(bf16[640,512]{1,0:T(8,128)(2,1)S(1)} %get-tuple-element.29.after_ref), channel_id=1, source_target_pairs={{2,1},{4,3},{6,5},{9,10},{10,9},{11,12},{12,11},{13,14},{14,13},{1... | collective-permute-start | bytes 1966088 | tf_op jit(solution)/shard_map/ppermute | solution.py:269
  31.2 5.9 %shard_map.40.start_ref = f32[1024,512]{1,0:T(8,128)S(1)} custom-call(bf16[1024,512]{1,0:T(8,128)(2,1)S(1)} %get-tuple-element.20.psi_ref, bf16[1,1024,1024]{2,1,0:T(8,128)(2,1)S(1)} %get-tuple-element.27.left0_ref, bf16[1,512,512]{2,1,0:T(8,128)(2,1)S(1)} %get-tuple-element.28.right0_ref, ...), custom_call_target="tpu_custom_call", output_to_operand_aliasing={{}: (5, {})} | custom-call | flops 4831838208 | bytes 7864320 | tf_op jit(solution)/shard_map/pallas_call | solution.py:272
  37.1 0.0 collective-permute-done.psi_ref
  37.1 0.0 collective-permute-done.3.received_ref
  37.2 0.0 collective-permute-done.2.rights_ref
  37.2 7.3 %shard_map.41 = (bf16[1024,512]{1,0:T(8,128)(2,1)}, f32[640,512]{1,0:T(8,128)S(1)}) custom-call(bf16[1024,512]{1,0:T(8,128)(2,1)S(1)} %collective-permute-done.psi_ref, bf16[4,384,1024]{2,1,0:T(8,128)(2,1)S(1)} %get-tuple-element.25.lefts_ref.upper_ref, bf16[4,640,1024]{2,1,0:T(8,128)(2,1)S(1)} %get-tuple-element.23.lefts_ref.lower_ref, ...), custom_call_target="tpu_custom_call" | custom-call | flops 6442450944 | bytes 10485760 | tf_op jit(solution)/shard_map/pallas_call | solution.py:281
  44.4 4.0 %collective-permute-done.4.received_ref = bf16[640,512]{1,0:T(8,128)(2,1)S(1)} collective-permute-done((bf16[640,512]{1,0:T(8,128)(2,1)S(1)}, bf16[640,512]{1,0:T(8,128)(2,1)S(1)}, u32[]{:S(2)}, u32[]{:S(2)}) %collective-permute-start.4) | collective-permute-done | bytes 655392 | tf_op jit(solution)/shard_map/ppermute | solution.py:269
  48.5 0.9 %shard_map.42 = bf16[1024,512]{1,0:T(8,128)(2,1)} custom-call(f32[640,512]{1,0:T(8,128)S(1)} %get-tuple-element.33.total_ref, bf16[640,512]{1,0:T(8,128)(2,1)S(1)} %collective-permute-done.4.received_ref, bf16[1024,512]{1,0:T(8,128)(2,1)} %get-tuple-element.34.start_ref), custom_call_target="tpu_custom_call", output_to_operand_aliasing={{}: (2, {})} | custom-call | tf_op jit(solution)/shard_map/pallas_call | solution.py:289
Async XLA Ops:
  0.0 17.4 %collective-permute-start.1 = (bf16[1024,512]{1,0:T(8,128)(2,1)}, bf16[1024,512]{1,0:T(8,128)(2,1)S(1)}, u32[]{:S(2)}, u32[]{:S(2)}) collective-permute-start(bf16[1024,512]{1,0:T(8,128)(2,1)} %whole_ref.1), channel_id=1, source_target_pairs={{8,0},{10,2},{12,4},{14,6},{16,8},{1,9},{18,10},{3,11},{20,12},{5,... | collective-permute-start | bytes 3145736 | tf_op jit(solution)/shard_map/ppermute | solution.py:239
  14.8 22.3 %collective-permute-start.2 = (bf16[4,512,512]{2,1,0:T(8,128)(2,1)S(1)}, bf16[4,512,512]{2,1,0:T(8,128)(2,1)S(1)}, u32[]{:S(2)}, u32[]{:S(2)}) collective-permute-start(bf16[4,512,512]{2,1,0:T(8,128)(2,1)S(1)} %get-tuple-element.31), channel_id=1, source_target_pairs={{1,0},{0,1},{3,2},{2,3},{5,4},{4,5},{7,6},{6,7},{9,8},{8,9},{11,10... | collective-permute-start | bytes 6291464 | tf_op jit(solution)/shard_map/ppermute | solution.py:270
  14.9 22.2 %collective-permute-start = (bf16[1024,512]{1,0:T(8,128)(2,1)S(1)}, bf16[1024,512]{1,0:T(8,128)(2,1)S(1)}, u32[]{:S(2)}, u32[]{:S(2)}) collective-permute-start(bf16[1024,512]{1,0:T(8,128)(2,1)S(1)} %get-tuple-element.20.psi_ref), channel_id=1, source_target_pairs={{9,0},{11,2},{13,4},{15,6},{17,8},{0,9},{19,10},{2,11},{21,12},{4,... | collective-permute-start | bytes 3145736 | tf_op jit(solution)/shard_map/ppermute | solution.py:251
  20.3 16.9 %collective-permute-start.3 = (bf16[384,512]{1,0:T(8,128)(2,1)S(1)}, bf16[384,512]{1,0:T(8,128)(2,1)S(1)}, u32[]{:S(2)}, u32[]{:S(2)}) collective-permute-start(bf16[384,512]{1,0:T(8,128)(2,1)S(1)} %shard_map.38.after_ref), channel_id=1, source_target_pairs={{2,1},{4,3},{6,5},{9,10},{10,9},{11,12},{12,11},{13,14},{14,13},{1... | collective-permute-start | bytes 1179656 | tf_op jit(solution)/shard_map/ppermute | solution.py:260
  28.6 19.8 %collective-permute-start.4 = (bf16[640,512]{1,0:T(8,128)(2,1)S(1)}, bf16[640,512]{1,0:T(8,128)(2,1)S(1)}, u32[]{:S(2)}, u32[]{:S(2)}) collective-permute-start(bf16[640,512]{1,0:T(8,128)(2,1)S(1)} %get-tuple-element.29.after_ref), channel_id=1, source_target_pairs={{2,1},{4,3},{6,5},{9,10},{10,9},{11,12},{12,11},{13,14},{14,13},{1... | collective-permute-start | bytes 1966088 | tf_op jit(solution)/shard_map/ppermute | solution.py:269

commit v7 on v5

--- a/solution.py
+++ b/solution.py
@@ -124,8 +124,8 @@
     wait(coming)
 
 
-def rest_kernel(psi_ref, left0_ref, right0_ref, left_ref, right_ref, start_ref, after_ref,
-                total_ref, lefts_ref, rights_ref, sems):
+def tail_kernel(psi_ref, moved_ref, left0_ref, right0_ref, upper_ref, lower_ref, across_ref,
+                left_ref, right_ref, start_ref, after_ref, total_ref, lefts_ref, rights_ref, sems):
     del after_ref
     fetch = Fetch(sems)
     count = lefts_ref.shape[0]
@@ -138,56 +138,55 @@
     for slot in range(count):
         wait(coming[slot])
         total_ref[...] += contract(lefts_ref[slot], psi_ref[...], rights_ref[slot])
-
-
-def late_kernel(psi_ref, upper_ref, lower_ref, rights_ref, start_ref, received_ref,
-                out_ref, total_ref, work_ref, ready_ref, sem):
-    part = total_ref.shape[0]
-    steps = rights_ref.shape[0]
-    put = pltpu.make_async_copy(ready_ref, out_ref.at[pl.ds(0, part), :], sem)
-    for half, lefts_ref in enumerate((upper_ref, lower_ref)):
-        for step in range(steps):
-            old = start_ref[half * part:(half + 1) * part, :] if step == 0 else work_ref[...]
-            total = old + contract(lefts_ref[step], psi_ref[...], rights_ref[step])
-            if step + 1 < steps:
-                work_ref[...] = total
-            elif half:
-                total_ref[...] = total
-            else:
-                total = total + received_ref[...].astype(jnp.float32)
-                ready_ref[...] = total.astype(ready_ref.dtype)
-                put.start()
-    put.wait()
-
-
-def finish_kernel(total_ref, received_ref, start_ref, out_ref, ready_ref, sem):
-    del start_ref
-    part = total_ref.shape[0]
-    total = total_ref[...] + received_ref[...].astype(jnp.float32)
-    ready_ref[...] = total.astype(ready_ref.dtype)
-    put = pltpu.make_async_copy(ready_ref, out_ref.at[pl.ds(part, part), :], sem)
-    put.start()
-    put.wait()
+    part = upper_ref.shape[1]
+    for step in range(across_ref.shape[0]):
+        for rows, side_ref in ((slice(0, part), upper_ref), (slice(part, None), lower_ref)):
+            total_ref[rows, :] += contract(side_ref[step], moved_ref[...], across_ref[step])
+
+
+def finish_kernel(right_count, total_ref, first_ref, relay_ref, second_ref, out_ref, ready_ref,
+                  sems):
+    part = first_ref.shape[0]
+    sector = lax.axis_index("rsec")
+    middle = right_count // 2
+    inner = (sector == middle - 1) | (sector == middle)
+    relayed = inner | (sector == 0) | (sector == right_count - 1)
+    first = jnp.where(relayed, relay_ref[...], first_ref[...])
+    puts = []
+    for half, received in enumerate((first, second_ref[...])):
+        rows = pl.ds(half * part, part)
+        total = total_ref[rows, :] + received.astype(jnp.float32)
+        ready_ref[rows, :] = total.astype(ready_ref.dtype)
+        puts.append(pltpu.make_async_copy(
+            ready_ref.at[rows, :], out_ref.at[rows, :], sems.at[half]))
+        puts[-1].start()
+    wait(puts)
 
 
 def routes(left_count, right_count):
     index = lambda i, j: i * right_count + j
-    straight, crossed, partner, along = [], [], [], []
+    straight, crossed, partner, along, onward, relay = [], [], [], [], [], []
+    middle, edge = right_count // 2, right_count - 1
+    via = {middle - 1: edge, middle: 0}
     for i in range(left_count):
         for j in range(right_count):
             step = 1 if j % 2 == 0 else -1
             partner.append((index(i, j + step), index(i, j)))
-            if 0 <= i + step < left_count:
-                straight.append((index(i + step, j), index(i, j)))
-                crossed.append((index(i + step, j + step), index(i, j)))
-            if 0 <= j - step < right_count and 0 <= i + step < left_count:
+            if not 0 <= i + step < left_count:
+                continue
+            straight.append((index(i + step, j), index(i, j)))
+            crossed.append((index(i + step, j + step), index(i, j)))
+            if 0 <= j - step < right_count:
                 along.append((index(i, j), index(i, j - step)))
-    return straight, crossed, partner, along
+                onward.append((index(i, j), index(i, via.get(j, j - step))))
+                if j in via:
+                    relay.append((index(i, via[j]), index(i, j - step)))
+    return straight, crossed, partner, along, onward, relay
 
 
 def shards(left_count, right_count, psi, left_whole, right_whole):
     axes = ("lsec", "rsec")
-    straight, crossed, partner, along = routes(left_count, right_count)
+    straight, crossed, partner, along, onward, relay = routes(left_count, right_count)
     rows, columns = psi.shape
     channels = left_whole.shape[0]
     charged_count, local_rest = channels // period, channels // 2 - local_first
@@ -238,7 +237,8 @@
         [half_total],
         cost(charged_count, part, rows, columns),
     )(moved, upper, own, total)
-    first_received = lax.ppermute(first, axes, along)
+    first_received = lax.ppermute(first, axes, onward)
+    across = lax.ppermute(give, axes, partner)
 
     second, rest_left, rest_right = call(
         second_kernel,
@@ -248,34 +248,25 @@
         cost(charged_count, part, rows, columns),
     )(moved, lower, own, left_env, right_env, first)
     second_received = lax.ppermute(second, axes, along)
-    across = lax.ppermute(give, axes, partner)
+    relayed = lax.ppermute(first_received, axes, relay)
 
     (total,) = call(
-        rest_kernel,
-        [in_vmem, in_vmem, in_vmem, in_hbm, in_hbm, in_vmem, in_hbm],
+        tail_kernel,
+        [in_vmem] * 7 + [in_hbm, in_hbm, in_vmem, in_hbm],
         [total_shape],
         [lefts(local_rest - 1), rights(local_rest - 1), sems(2 * local_rest - 2)],
-        cost(local_rest, rows, rows, columns),
-        aliases={5: 0},
-    )(kept, rest_left, rest_right, left_env, right_env, total, second)
-    moved_across, total = lax.optimization_barrier((moved_across, total))
-    out, total = call(
-        late_kernel,
-        [in_vmem] * 6,
-        [pltpu.VMEM((rows, columns), bf16), half_total],
-        [half_total, half_block, pltpu.SemaphoreType.DMA],
-        cost(charged_count, rows, rows, columns),
-        out_specs=[in_hbm, in_vmem],
-    )(moved_across, upper, lower, across, total, first_received)
+        cost(local_rest + charged_count, rows, rows, columns),
+        aliases={9: 0},
+    )(kept, moved_across, rest_left, rest_right, upper, lower, across, left_env, right_env, total,
+      second)
     (out,) = call(
-        finish_kernel,
-        [in_vmem, in_vmem, in_hbm],
+        functools.partial(finish_kernel, right_count),
+        [in_vmem] * 4,
         [pltpu.VMEM((rows, columns), bf16)],
-        [half_block, pltpu.SemaphoreType.DMA],
+        [pltpu.VMEM((rows, columns), bf16), sems(2)],
         None,
-        aliases={2: 0},
         out_specs=[in_hbm],
-    )(total, second_received, out)
+    )(total, first_received, relayed, second_received)
     return out
 
 

time: 49.5 us -> 68.1 us (1.38)
  the two profiles are of different devices: /device:TPU:19 before, /device:TPU:0 now
where the time goes in v7:
time: 68.1 us; the launch traced here: 67.6 us
  Pallas kernels  32.2 us (47%)
  waiting for transfers between devices  23.3 us (34%)
  starting transfers between devices  11.8 us (17%)
    ppermute x1, waiting for transfers between devices, shards(): moved = lax.ppermute(psi, axes, straight)  17.7 us
    pallas_call x1, Pallas kernels, shards(): call(tail_kernel, [in_vmem] * 7 + [in_hbm, in_hbm, in_vmem, in_hbm], [tot...  12.9 us
    pallas_call x1, Pallas kernels, shards(): call(local_kernel, [in_smem, in_hbm, in_hbm, in_hbm], [total_shape, pltpu...  11.3 us
    ppermute x1, starting transfers between devices, shards(): moved_across = lax.ppermute(kept, axes, crossed)  6.49 us
    ppermute x1, waiting for transfers between devices, shards(): first_received = lax.ppermute(first, axes, onward)  5.62 us
    pallas_call x1, Pallas kernels, shards(): call(second_kernel, [in_vmem, in_vmem, in_vmem, in_hbm, in_hbm, in_hbm],...  3.45 us
    pallas_call x1, Pallas kernels, shards(): call(first_kernel, [in_vmem, in_vmem, in_vmem, in_hbm], [half_block], [ha...  3.42 us
    ppermute x1, starting transfers between devices, shards(): relayed = lax.ppermute(first_received, axes, relay)  1.49 us
  transfers between devices with their start and end apart: 6, of which 2 were waited for; matrix products, arithmetic and copies ran while one was open for 0% of the time, Pallas kernels for 29%

profile of v7, /device:TPU:0, one launch (start us, length us, event | category | flops | bytes accessed | tf_op | source)
XLA Modules:
  0.0 67.6 jit_solution(9175818228002065898)
XLA Ops:
  0.0 0.0 copy-start
  0.0 11.3 %shard_map.37 = (f32[1024,512]{1,0:T(8,128)S(1)}, bf16[1024,512]{1,0:T(8,128)(2,1)S(1)}, bf16[4,512,1024]{2,1,0:T(8,128)(2,1)S(1)}, bf16[4,512,1024]{2,1,0:T(8,1...) custom-call(s32[1]{0:T(128)} %bitcast.charged_ref, bf16[1024,512]{1,0:T(8,128)(2,1)} %whole_ref.1, ...), custom_call_target="tpu_custom_call" | custom-call | flops 8053063680 | bytes 13107200 | tf_op jit(solution)/shard_map/pallas_call | solution.py:222
  11.3 0.6 collective-permute-start.2
  11.9 0.0 copy-done
  11.9 1.3 %collective-permute-start.1 = (bf16[1024,512]{1,0:T(8,128)(2,1)S(1)}, bf16[1024,512]{1,0:T(8,128)(2,1)S(1)}, u32[]{:S(2)}, u32[]{:S(2)}) collective-permute-start(bf16[1024,512]{1,0:T(8,128)(2,1)S(1)} %copy-done), channel_id=1, source_target_pairs={{8,0},{10,2},{12,4},{14,6},{16,8},{1,9},{18,10},{3,11},{20,12},{5,... | collective-permute-start | bytes 3145736 | tf_op jit(solution)/shard_map/ppermute | solution.py:220
  13.2 6.5 %collective-permute-start = (bf16[1024,512]{1,0:T(8,128)(2,1)S(1)}, bf16[1024,512]{1,0:T(8,128)(2,1)S(1)}, u32[]{:S(2)}, u32[]{:S(2)}) collective-permute-start(bf16[1024,512]{1,0:T(8,128)(2,1)S(1)} %get-tuple-element.16.psi_ref), channel_id=1, source_target_pairs={{9,0},{11,2},{13,4},{15,6},{17,8},{0,9},{19,10},{2,11},{21,12},{4,... | collective-permute-start | bytes 3145736 | tf_op jit(solution)/shard_map/ppermute | solution.py:231
  19.7 17.7 %collective-permute-done.1.psi_ref = bf16[1024,512]{1,0:T(8,128)(2,1)S(1)} collective-permute-done((bf16[1024,512]{1,0:T(8,128)(2,1)S(1)}, bf16[1024,512]{1,0:T(8,128)(2,1)S(1)}, u32[]{:S(2)}, u32[]{:S(2)}) %collective-permute-start.1) | collective-permute-done | bytes 1048608 | tf_op jit(solution)/shard_map/ppermute | solution.py:220
  37.4 3.4 %shard_map.38.after_ref = bf16[512,512]{1,0:T(8,128)(2,1)S(1)} custom-call(bf16[1024,512]{1,0:T(8,128)(2,1)S(1)} %collective-permute-done.1.psi_ref, bf16[4,512,1024]{2,1,0:T(8,128)(2,1)S(1)} %get-tuple-element.21.lefts_ref.upper_ref, bf16[4,512,512]{2,1,0:T(8,128)(2,1)S(1)} %get-tuple-element.20.rights_ref, ...), custom_call_target="tpu_custom_call" | custom-call | flops 3221225472 | bytes 6291456 | tf_op jit(solution)/shard_map/pallas_call | solution.py:233
  40.8 1.3 %collective-permute-start.3 = (bf16[512,512]{1,0:T(8,128)(2,1)S(1)}, bf16[512,512]{1,0:T(8,128)(2,1)S(1)}, u32[]{:S(2)}, u32[]{:S(2)}) collective-permute-start(bf16[512,512]{1,0:T(8,128)(2,1)S(1)} %shard_map.38.after_ref), channel_id=1, source_target_pairs={{2,1},{4,0},{6,5},{9,10},{10,9},{11,15},{12,8},{13,14},{14,13},{17... | collective-permute-start | bytes 1572872 | tf_op jit(solution)/shard_map/ppermute | solution.py:240
  42.1 3.4 %shard_map.39 = (bf16[512,512]{1,0:T(8,128)(2,1)S(1)}, bf16[1,1024,1024]{2,1,0:T(8,128)(2,1)S(1)}, bf16[1,512,512]{2,1,0:T(8,128)(2,1)S(1)}) custom-call(bf16[1024,512]{1,0:T(8,128)(2,1)S(1)} %collective-permute-done.1.psi_ref, bf16[4,512,1024]{2,1,0:T(8,128)(2,1)S(1)} %get-tuple-element.19.lefts_ref.lower_ref, ...), custom_call_target="tpu_custom_call" | custom-call | flops 3221225472 | bytes 6291456 | tf_op jit(solution)/shard_map/pallas_call | solution.py:243
  45.5 0.7 %collective-permute-start.5 = (bf16[512,512]{1,0:T(8,128)(2,1)S(1)}, bf16[512,512]{1,0:T(8,128)(2,1)S(1)}, u32[]{:S(2)}, u32[]{:S(2)}) collective-permute-start(bf16[512,512]{1,0:T(8,128)(2,1)S(1)} %get-tuple-element.26.after_ref), channel_id=1, source_target_pairs={{2,1},{4,3},{6,5},{9,10},{10,9},{11,12},{12,11},{13,14},{14,13},{1... | collective-permute-start | bytes 1572872 | tf_op jit(solution)/shard_map/ppermute | solution.py:250
  46.2 5.6 %collective-permute-done.3.first_ref = bf16[512,512]{1,0:T(8,128)(2,1)S(1)} collective-permute-done((bf16[512,512]{1,0:T(8,128)(2,1)S(1)}, bf16[512,512]{1,0:T(8,128)(2,1)S(1)}, u32[]{:S(2)}, u32[]{:S(2)}) %collective-permute-start.3) | collective-permute-done | bytes 524320 | tf_op jit(solution)/shard_map/ppermute | solution.py:240
  51.9 1.5 %collective-permute-start.4 = (bf16[512,512]{1,0:T(8,128)(2,1)S(1)}, bf16[512,512]{1,0:T(8,128)(2,1)S(1)}, u32[]{:S(2)}, u32[]{:S(2)}) collective-permute-start(bf16[512,512]{1,0:T(8,128)(2,1)S(1)} %collective-permute-done.3.first_ref), channel_id=1, source_target_pairs={{0,3},{15,12},{8,11},{23,20},{16,19},{31,28}} | collective-permute-start | bytes 1572872 | tf_op jit(solution)/shard_map/ppermute | solution.py:251
  53.4 0.0 collective-permute-done.moved_ref
  53.4 0.0 collective-permute-done.2.across_ref
  53.4 12.9 %shard_map.40.total_ref = f32[1024,512]{1,0:T(8,128)S(1)} custom-call(bf16[1024,512]{1,0:T(8,128)(2,1)S(1)} %get-tuple-element.16.psi_ref, bf16[1024,512]{1,0:T(8,128)(2,1)S(1)} %collective-permute-done.moved_ref, bf16[1,1024,1024]{2,1,0:T(8,128)(2,1)S(1)} %get-tuple-element.23.left0_ref, ...), custom_call_target="tpu_custom_call", output_to_operand_aliasing={{}: (9, {})} | custom-call | flops 11274289152 | bytes 18350080 | tf_op jit(solution)/shard_map/pallas_call | solution.py:253
  66.3 0.0 collective-permute-done.5.second_ref
  66.3 0.0 collective-permute-done.4.relay_ref
  66.3 1.1 %shard_map.41 = bf16[1024,512]{1,0:T(8,128)(2,1)} custom-call(f32[1024,512]{1,0:T(8,128)S(1)} %shard_map.40.total_ref, bf16[512,512]{1,0:T(8,128)(2,1)S(1)} %collective-permute-done.3.first_ref, bf16[512,512]{1,0:T(8,128)(2,1)S(1)} %collective-permute-done.4.relay_ref, bf16[512,512]{1,0:T(8,128)(2,1)S(1)} %collective-permute-done.5.second_ref), custom_call_target="tpu_custom_call" | custom-call | tf_op jit(solution)/shard_map/pallas_call | solution.py:262
Async XLA Ops:
  0.0 11.9 %copy-start = (bf16[1024,512]{1,0:T(8,128)(2,1)S(1)}, bf16[1024,512]{1,0:T(8,128)(2,1)}, u32[]{:S(2)}) copy-start(bf16[1024,512]{1,0:T(8,128)(2,1)} %whole_ref.1) | copy-start | bytes 3145732
  11.3 42.1 %collective-permute-start.2 = (bf16[4,512,512]{2,1,0:T(8,128)(2,1)S(1)}, bf16[4,512,512]{2,1,0:T(8,128)(2,1)S(1)}, u32[]{:S(2)}, u32[]{:S(2)}) collective-permute-start(bf16[4,512,512]{2,1,0:T(8,128)(2,1)S(1)} %get-tuple-element.25), channel_id=1, source_target_pairs={{1,0},{0,1},{3,2},{2,3},{5,4},{4,5},{7,6},{6,7},{9,8},{8,9},{11,10... | collective-permute-start | bytes 6291464 | tf_op jit(solution)/shard_map/ppermute | solution.py:241
  11.9 25.5 %collective-permute-start.1 = (bf16[1024,512]{1,0:T(8,128)(2,1)S(1)}, bf16[1024,512]{1,0:T(8,128)(2,1)S(1)}, u32[]{:S(2)}, u32[]{:S(2)}) collective-permute-start(bf16[1024,512]{1,0:T(8,128)(2,1)S(1)} %copy-done), channel_id=1, source_target_pairs={{8,0},{10,2},{12,4},{14,6},{16,8},{1,9},{18,10},{3,11},{20,12},{5,... | collective-permute-start | bytes 3145736 | tf_op jit(solution)/shard_map/ppermute | solution.py:220
  13.2 40.2 %collective-permute-start = (bf16[1024,512]{1,0:T(8,128)(2,1)S(1)}, bf16[1024,512]{1,0:T(8,128)(2,1)S(1)}, u32[]{:S(2)}, u32[]{:S(2)}) collective-permute-start(bf16[1024,512]{1,0:T(8,128)(2,1)S(1)} %get-tuple-element.16.psi_ref), channel_id=1, source_target_pairs={{9,0},{11,2},{13,4},{15,6},{17,8},{0,9},{19,10},{2,11},{21,12},{4,... | collective-permute-start | bytes 3145736 | tf_op jit(solution)/shard_map/ppermute | solution.py:231
  40.8 11.1 %collective-permute-start.3 = (bf16[512,512]{1,0:T(8,128)(2,1)S(1)}, bf16[512,512]{1,0:T(8,128)(2,1)S(1)}, u32[]{:S(2)}, u32[]{:S(2)}) collective-permute-start(bf16[512,512]{1,0:T(8,128)(2,1)S(1)} %shard_map.38.after_ref), channel_id=1, source_target_pairs={{2,1},{4,0},{6,5},{9,10},{10,9},{11,15},{12,8},{13,14},{14,13},{17... | collective-permute-start | bytes 1572872 | tf_op jit(solution)/shard_map/ppermute | solution.py:240
  45.5 20.8 %collective-permute-start.5 = (bf16[512,512]{1,0:T(8,128)(2,1)S(1)}, bf16[512,512]{1,0:T(8,128)(2,1)S(1)}, u32[]{:S(2)}, u32[]{:S(2)}) collective-permute-start(bf16[512,512]{1,0:T(8,128)(2,1)S(1)} %get-tuple-element.26.after_ref), channel_id=1, source_target_pairs={{2,1},{4,3},{6,5},{9,10},{10,9},{11,12},{12,11},{13,14},{14,13},{1... | collective-permute-start | bytes 1572872 | tf_op jit(solution)/shard_map/ppermute | solution.py:250
  51.9 14.5 %collective-permute-start.4 = (bf16[512,512]{1,0:T(8,128)(2,1)S(1)}, bf16[512,512]{1,0:T(8,128)(2,1)S(1)}, u32[]{:S(2)}, u32[]{:S(2)}) collective-permute-start(bf16[512,512]{1,0:T(8,128)(2,1)S(1)} %collective-permute-done.3.first_ref), channel_id=1, source_target_pairs={{0,3},{15,12},{8,11},{23,20},{16,19},{31,28}} | collective-permute-start | bytes 1572872 | tf_op jit(solution)/shard_map/ppermute | solution.py:251

commit v8 on v7

--- a/solution.py
+++ b/solution.py
@@ -10,7 +10,6 @@
 
 channel_shifts = (0, 1, -1, 0)
 period = len(channel_shifts)
-local_first = 5
 in_vmem = pl.BlockSpec(memory_space=pltpu.VMEM)
 in_smem = pl.BlockSpec(memory_space=pltpu.SMEM)
 in_hbm = pl.BlockSpec(memory_space=pl.ANY)
@@ -110,38 +109,71 @@
             term_ref[...] = total.astype(term_ref.dtype)
 
 
-def first_kernel(psi_ref, lefts_ref, rights_ref, after_ref, term_ref, total_ref):
-    del after_ref
-    early_term(psi_ref, lefts_ref, rights_ref, term_ref, total_ref)
-
-
-def second_kernel(psi_ref, lefts_ref, rights_ref, left_ref, right_ref, after_ref,
-                  term_ref, next_left_ref, next_right_ref, total_ref, sems):
-    del after_ref
+def at_edge(right_count):
+    sector = lax.axis_index("rsec")
+    return (sector == 0) | (sector == right_count - 1)
+
+
+def early_or_local(edge, step, kept_ref, psi_ref, lefts_ref, rights_ref, left_ref, right_ref,
+                   term_ref, total_ref, work_ref, spare_left_ref, spare_right_ref, sems):
+    @pl.when(edge)
+    def _():
+        wait(Fetch(sems).start(*local_blocks(
+            left_ref, right_ref, spare_left_ref, spare_right_ref, step, 0)))
+        total_ref[...] += contract(spare_left_ref[0], kept_ref[...], spare_right_ref[0])
+
+    @pl.when(jnp.logical_not(edge))
+    def _():
+        early_term(psi_ref, lefts_ref, rights_ref, term_ref, work_ref)
+
+
+def first_kernel(right_count, step, kept_ref, psi_ref, lefts_ref, rights_ref, left_ref,
+                 right_ref, start_ref, term_ref, total_ref, work_ref, spare_left_ref,
+                 spare_right_ref, sems):
+    del start_ref
+    early_or_local(at_edge(right_count), step, kept_ref, psi_ref, lefts_ref, rights_ref,
+                   left_ref, right_ref, term_ref, total_ref, work_ref, spare_left_ref,
+                   spare_right_ref, sems)
+
+
+def second_kernel(right_count, step, next_step, kept_ref, psi_ref, lefts_ref, rights_ref,
+                  left_ref, right_ref, start_ref, after_ref, term_ref, total_ref, next_left_ref,
+                  next_right_ref, work_ref, spare_left_ref, spare_right_ref, sems, next_sems):
+    del start_ref, after_ref
+    coming = Fetch(next_sems).start(*local_blocks(
+        left_ref, right_ref, next_left_ref, next_right_ref, next_step, 0))
+    early_or_local(at_edge(right_count), step, kept_ref, psi_ref, lefts_ref, rights_ref,
+                   left_ref, right_ref, term_ref, total_ref, work_ref, spare_left_ref,
+                   spare_right_ref, sems)
+    wait(coming)
+
+
+def rest_kernel(next_step, psi_ref, left0_ref, right0_ref, left_ref, right_ref, start_ref,
+                after_ref, total_ref, next_left_ref, next_right_ref, sems):
+    del start_ref, after_ref
     coming = Fetch(sems).start(*local_blocks(
-        left_ref, right_ref, next_left_ref, next_right_ref, local_first, 0))
-    early_term(psi_ref, lefts_ref, rights_ref, term_ref, total_ref)
+        left_ref, right_ref, next_left_ref, next_right_ref, next_step, 0))
+    total_ref[...] += contract(left0_ref[0], psi_ref[...], right0_ref[0])
     wait(coming)
 
 
-def tail_kernel(psi_ref, moved_ref, left0_ref, right0_ref, upper_ref, lower_ref, across_ref,
-                left_ref, right_ref, start_ref, after_ref, total_ref, lefts_ref, rights_ref, sems):
-    del after_ref
-    fetch = Fetch(sems)
-    count = lefts_ref.shape[0]
-    coming = [
-        fetch.start(*local_blocks(
-            left_ref, right_ref, lefts_ref, rights_ref, local_first + 1 + slot, slot))
-        for slot in range(count)
-    ]
-    total_ref[...] = start_ref[...] + contract(left0_ref[0], psi_ref[...], right0_ref[0])
-    for slot in range(count):
-        wait(coming[slot])
-        total_ref[...] += contract(lefts_ref[slot], psi_ref[...], rights_ref[slot])
+def tail_kernel(right_count, step, psi_ref, moved_ref, left0_ref, right0_ref, upper_ref,
+                lower_ref, across_ref, left_ref, right_ref, start_ref, after_ref, total_ref,
+                spare_left_ref, spare_right_ref, sems):
+    del start_ref, after_ref
+
+    @pl.when(jnp.logical_not(at_edge(right_count)))
+    def _():
+        coming = Fetch(sems).start(*local_blocks(
+            left_ref, right_ref, spare_left_ref, spare_right_ref, step, 0))
+        total_ref[...] += contract(left0_ref[0], psi_ref[...], right0_ref[0])
+        wait(coming)
+        total_ref[...] += contract(spare_left_ref[0], psi_ref[...], spare_right_ref[0])
+
     part = upper_ref.shape[1]
-    for step in range(across_ref.shape[0]):
+    for index in range(across_ref.shape[0]):
         for rows, side_ref in ((slice(0, part), upper_ref), (slice(part, None), lower_ref)):
-            total_ref[rows, :] += contract(side_ref[step], moved_ref[...], across_ref[step])
+            total_ref[rows, :] += contract(side_ref[index], moved_ref[...], across_ref[index])
 
 
 def finish_kernel(right_count, total_ref, first_ref, relay_ref, second_ref, out_ref, ready_ref,
@@ -189,7 +221,8 @@
     straight, crossed, partner, along, onward, relay = routes(left_count, right_count)
     rows, columns = psi.shape
     channels = left_whole.shape[0]
-    charged_count, local_rest = channels // period, channels // 2 - local_first
+    charged_count = channels // period
+    local_first = channels // 2 - 3
     part = rows // 2
     f32, bf16 = jnp.float32, jnp.bfloat16
     lefts = lambda count: pltpu.VMEM((count, rows, rows), bf16)
@@ -230,32 +263,42 @@
 
     moved_across = lax.ppermute(kept, axes, crossed)
     moved, total = lax.optimization_barrier((moved, total))
-    (first,) = call(
-        first_kernel,
-        [in_vmem, in_vmem, in_vmem, in_hbm],
-        [half_block],
-        [half_total],
+    first, total = call(
+        functools.partial(first_kernel, right_count, local_first + 2),
+        [in_vmem] * 4 + [in_hbm, in_hbm, in_vmem],
+        [half_block, total_shape],
+        [half_total, lefts(1), rights(1), sems(2)],
         cost(charged_count, part, rows, columns),
-    )(moved, upper, own, total)
+        aliases={6: 1},
+    )(kept, moved, upper, own, left_env, right_env, total)
     first_received = lax.ppermute(first, axes, onward)
+    second, total, rest_left, rest_right = call(
+        functools.partial(second_kernel, right_count, local_first + 1, local_first),
+        [in_vmem] * 4 + [in_hbm, in_hbm, in_vmem, in_hbm],
+        [half_block, total_shape, lefts(1), rights(1)],
+        [half_total, lefts(1), rights(1), sems(2), sems(2)],
+        cost(charged_count, part, rows, columns),
+        aliases={6: 1},
+    )(kept, moved, lower, own, left_env, right_env, total, first)
+    second_received = lax.ppermute(second, axes, along)
     across = lax.ppermute(give, axes, partner)
-
-    second, rest_left, rest_right = call(
-        second_kernel,
-        [in_vmem, in_vmem, in_vmem, in_hbm, in_hbm, in_hbm],
-        [half_block, lefts(1), rights(1)],
-        [half_total, sems(2)],
-        cost(charged_count, part, rows, columns),
-    )(moved, lower, own, left_env, right_env, first)
-    second_received = lax.ppermute(second, axes, along)
+    total, rest_left, rest_right = call(
+        functools.partial(rest_kernel, local_first + 1),
+        [in_vmem, in_vmem, in_vmem, in_hbm, in_hbm, in_vmem, in_hbm],
+        [total_shape, lefts(1), rights(1)],
+        [sems(2)],
+        cost(1, rows, rows, columns),
+        aliases={5: 0},
+    )(kept, rest_left, rest_right, left_env, right_env, total, second)
+    first_received, total = lax.optimization_barrier((first_received, total))
     relayed = lax.ppermute(first_received, axes, relay)
 
     (total,) = call(
-        tail_kernel,
+        functools.partial(tail_kernel, right_count, local_first + 2),
         [in_vmem] * 7 + [in_hbm, in_hbm, in_vmem, in_hbm],
         [total_shape],
-        [lefts(local_rest - 1), rights(local_rest - 1), sems(2 * local_rest - 2)],
-        cost(local_rest + charged_count, rows, rows, columns),
+        [lefts(1), rights(1), sems(2)],
+        cost(2 + charged_count, rows, rows, columns),
         aliases={9: 0},
     )(kept, moved_across, rest_left, rest_right, upper, lower, across, left_env, right_env, total,
       second)

time: 68.1 us -> 66.4 us (0.975)
  the two profiles are of different devices: /device:TPU:0 before, /device:TPU:19 now
where the time goes in v8:
time: 66.4 us; the launch traced here: 66.1 us
  Pallas kernels  32.2 us (48%)
  waiting for transfers between devices  19.2 us (29%)
  starting transfers between devices  14.5 us (22%)
    ppermute x1, waiting for transfers between devices, shards(): moved = lax.ppermute(psi, axes, straight)  19.2 us
    pallas_call x1, Pallas kernels, shards(): call(local_kernel, [in_smem, in_hbm, in_hbm, in_hbm], [total_shape, pltpu...  11.3 us
    pallas_call x1, Pallas kernels, shards(): call(functools.partial(tail_kernel, right_count, local_first + 2), [in_vm...  10.8 us
    ppermute x1, starting transfers between devices, shards(): second_received = lax.ppermute(second, axes, along)  4.15 us
    pallas_call x1, Pallas kernels, shards(): call(functools.partial(second_kernel, right_count, local_first + 1, local...  3.66 us
    pallas_call x1, Pallas kernels, shards(): call(functools.partial(first_kernel, right_count, local_first + 2), [in_v...  3.44 us
    ppermute x1, starting transfers between devices, shards(): first_received = lax.ppermute(first, axes, onward)  3.22 us
    ppermute x1, starting transfers between devices, shards(): moved = lax.ppermute(psi, axes, straight)  3.19 us
  transfers between devices with their start and end apart: 6, of which 1 were waited for; matrix products, arithmetic and copies ran while one was open for 0% of the time, Pallas kernels for 30%

profile of v8, /device:TPU:19, one launch (start us, length us, event | category | flops | bytes accessed | tf_op | source)
XLA Modules:
  0.0 66.1 jit_solution(10771634220115111099)
XLA Ops:
  0.0 0.0 copy-start
  0.0 11.3 %shard_map.37 = (f32[1024,512]{1,0:T(8,128)S(1)}, bf16[1024,512]{1,0:T(8,128)(2,1)S(1)}, bf16[4,512,1024]{2,1,0:T(8,128)(2,1)S(1)}, bf16[4,512,1024]{2,1,0:T(8,1...) custom-call(s32[1]{0:T(128)} %bitcast.charged_ref, bf16[1024,512]{1,0:T(8,128)(2,1)} %whole_ref.1, ...), custom_call_target="tpu_custom_call" | custom-call | flops 8053063680 | bytes 13107200 | tf_op jit(solution)/shard_map/pallas_call | solution.py:255
  11.4 0.7 %collective-permute-start.2 = (bf16[4,512,512]{2,1,0:T(8,128)(2,1)S(1)}, bf16[4,512,512]{2,1,0:T(8,128)(2,1)S(1)}, u32[]{:S(2)}, u32[]{:S(2)}) collective-permute-start(bf16[4,512,512]{2,1,0:T(8,128)(2,1)S(1)} %get-tuple-element.39), channel_id=1, source_target_pairs={{1,0},{0,1},{3,2},{2,3},{5,4},{4,5},{7,6},{6,7},{9,8},{8,9},{11,10... | collective-permute-start | bytes 6291464 | tf_op jit(solution)/shard_map/ppermute | solution.py:284
  12.1 0.0 copy-done
  12.1 3.2 %collective-permute-start.1 = (bf16[1024,512]{1,0:T(8,128)(2,1)S(1)}, bf16[1024,512]{1,0:T(8,128)(2,1)S(1)}, u32[]{:S(2)}, u32[]{:S(2)}) collective-permute-start(bf16[1024,512]{1,0:T(8,128)(2,1)S(1)} %copy-done), channel_id=1, source_target_pairs={{8,0},{10,2},{12,4},{14,6},{16,8},{1,9},{18,10},{3,11},{20,12},{5,... | collective-permute-start | bytes 3145736 | tf_op jit(solution)/shard_map/ppermute | solution.py:253
  15.3 1.9 %collective-permute-start = (bf16[1024,512]{1,0:T(8,128)(2,1)S(1)}, bf16[1024,512]{1,0:T(8,128)(2,1)S(1)}, u32[]{:S(2)}, u32[]{:S(2)}) collective-permute-start(bf16[1024,512]{1,0:T(8,128)(2,1)S(1)} %get-tuple-element.24.kept_ref.psi_ref), channel_id=1, source_target_pairs={{9,0},{11,2},{13,4},{15,6},{17,8},{0,9},{19,10},{2,11},{21,12},{4,... | collective-permute-start | bytes 3145736 | tf_op jit(solution)/shard_map/ppermute | solution.py:264
  17.2 19.2 %collective-permute-done.1.psi_ref = bf16[1024,512]{1,0:T(8,128)(2,1)S(1)} collective-permute-done((bf16[1024,512]{1,0:T(8,128)(2,1)S(1)}, bf16[1024,512]{1,0:T(8,128)(2,1)S(1)}, u32[]{:S(2)}, u32[]{:S(2)}) %collective-permute-start.1) | collective-permute-done | bytes 1048608 | tf_op jit(solution)/shard_map/ppermute | solution.py:253
  36.4 3.4 %shard_map.38 = (bf16[512,512]{1,0:T(8,128)(2,1)S(1)}, f32[1024,512]{1,0:T(8,128)S(1)}) custom-call(bf16[1024,512]{1,0:T(8,128)(2,1)S(1)} %get-tuple-element.24.kept_ref.psi_ref, bf16[1024,512]{1,0:T(8,128)(2,1)S(1)} %collective-permute-done.1.psi_ref, ...), custom_call_target="tpu_custom_call", output_to_operand_aliasing={{1}: (6, {})} | custom-call | flops 3221225472 | bytes 6291456 | tf_op jit(solution)/shard_map/pallas_call | solution.py:266
  39.8 3.2 %collective-permute-start.3 = (bf16[512,512]{1,0:T(8,128)(2,1)S(1)}, bf16[512,512]{1,0:T(8,128)(2,1)S(1)}, u32[]{:S(2)}, u32[]{:S(2)}) collective-permute-start(bf16[512,512]{1,0:T(8,128)(2,1)S(1)} %get-tuple-element.32.after_ref), channel_id=1, source_target_pairs={{2,1},{4,0},{6,5},{9,10},{10,9},{11,15},{12,8},{13,14},{14,13},{17... | collective-permute-start | bytes 1572872 | tf_op jit(solution)/shard_map/ppermute | solution.py:274
  43.1 3.7 %shard_map.39 = (bf16[512,512]{1,0:T(8,128)(2,1)S(1)}, f32[1024,512]{1,0:T(8,128)S(1)}, bf16[1,1024,1024]{2,1,0:T(8,128)(2,1)S(1)}, bf16[1,512,512]{2,1,0:T(8,128)(2,1)S(1)}) custom-call(bf16[1024,512]{1,0:T(8,128)(2,1)S(1)} %get-tuple-element.24.kept_ref.psi_ref, ...), custom_call_target="tpu_custom_call", output_to_operand_aliasing={{1}: (6, {})} | custom-call | flops 3221225472 | bytes 6291456 | tf_op jit(solution)/shard_map/pallas_call | solution.py:275
  46.7 4.1 %collective-permute-start.5 = (bf16[512,512]{1,0:T(8,128)(2,1)S(1)}, bf16[512,512]{1,0:T(8,128)(2,1)S(1)}, u32[]{:S(2)}, u32[]{:S(2)}) collective-permute-start(bf16[512,512]{1,0:T(8,128)(2,1)S(1)} %get-tuple-element.36.after_ref), channel_id=1, source_target_pairs={{2,1},{4,3},{6,5},{9,10},{10,9},{11,12},{12,11},{13,14},{14,13},{1... | collective-permute-start | bytes 1572872 | tf_op jit(solution)/shard_map/ppermute | solution.py:283
  50.9 1.8 %shard_map.40 = (f32[1024,512]{1,0:T(8,128)S(1)}, bf16[1,1024,1024]{2,1,0:T(8,128)(2,1)S(1)}, bf16[1,512,512]{2,1,0:T(8,128)(2,1)S(1)}) custom-call(bf16[1024,512]{1,0:T(8,128)(2,1)S(1)} %get-tuple-element.24.kept_ref.psi_ref, bf16[1,1024,1024]{2,1,0:T(8,128)(2,1)S(1)} %get-tuple-element.33.left0_ref, ...), custom_call_target="tpu_custom_call", output_to_operand_aliasing={{0}: (5, {})} | custom-call | flops 1610612736 | bytes 2621440 | tf_op jit(solution)/shard_map/pallas_call | solution.py:285
  52.7 0.0 collective-permute-done.3.first_ref
  52.7 1.3 %collective-permute-start.4 = (bf16[512,512]{1,0:T(8,128)(2,1)S(1)}, bf16[512,512]{1,0:T(8,128)(2,1)S(1)}, u32[]{:S(2)}, u32[]{:S(2)}) collective-permute-start(bf16[512,512]{1,0:T(8,128)(2,1)S(1)} %collective-permute-done.3.first_ref), channel_id=1, source_target_pairs={{0,3},{15,12},{8,11},{23,20},{16,19},{31,28}} | collective-permute-start | bytes 1572872 | tf_op jit(solution)/shard_map/ppermute | solution.py:294
  54.0 0.0 collective-permute-done.moved_ref
  54.0 0.0 collective-permute-done.2.across_ref
  54.0 10.8 %shard_map.41.total_ref = f32[1024,512]{1,0:T(8,128)S(1)} custom-call(bf16[1024,512]{1,0:T(8,128)(2,1)S(1)} %get-tuple-element.24.kept_ref.psi_ref, bf16[1024,512]{1,0:T(8,128)(2,1)S(1)} %collective-permute-done.moved_ref, bf16[1,1024,1024]{2,1,0:T(8,128)(2,1)S(1)} %get-tuple-element.37.left0_ref, ...), custom_call_target="tpu_custom_call", output_to_operand_aliasing={{}: (9, {})} | custom-call | flops 9663676416 | bytes 15728640 | tf_op jit(solution)/shard_map/pallas_call | solution.py:296
  64.9 0.0 collective-permute-done.5.second_ref
  64.9 0.0 collective-permute-done.4.relay_ref
  64.9 1.1 %shard_map.42 = bf16[1024,512]{1,0:T(8,128)(2,1)} custom-call(f32[1024,512]{1,0:T(8,128)S(1)} %shard_map.41.total_ref, bf16[512,512]{1,0:T(8,128)(2,1)S(1)} %collective-permute-done.3.first_ref, bf16[512,512]{1,0:T(8,128)(2,1)S(1)} %collective-permute-done.4.relay_ref, bf16[512,512]{1,0:T(8,128)(2,1)S(1)} %collective-permute-done.5.second_ref), custom_call_target="tpu_custom_call" | custom-call | tf_op jit(solution)/shard_map/pallas_call | solution.py:305
Async XLA Ops:
  0.0 12.1 %copy-start = (bf16[1024,512]{1,0:T(8,128)(2,1)S(1)}, bf16[1024,512]{1,0:T(8,128)(2,1)}, u32[]{:S(2)}) copy-start(bf16[1024,512]{1,0:T(8,128)(2,1)} %whole_ref.1) | copy-start | bytes 3145732
  11.4 42.7 %collective-permute-start.2 = (bf16[4,512,512]{2,1,0:T(8,128)(2,1)S(1)}, bf16[4,512,512]{2,1,0:T(8,128)(2,1)S(1)}, u32[]{:S(2)}, u32[]{:S(2)}) collective-permute-start(bf16[4,512,512]{2,1,0:T(8,128)(2,1)S(1)} %get-tuple-element.39), channel_id=1, source_target_pairs={{1,0},{0,1},{3,2},{2,3},{5,4},{4,5},{7,6},{6,7},{9,8},{8,9},{11,10... | collective-permute-start | bytes 6291464 | tf_op jit(solution)/shard_map/ppermute | solution.py:284
  12.1 24.3 %collective-permute-start.1 = (bf16[1024,512]{1,0:T(8,128)(2,1)S(1)}, bf16[1024,512]{1,0:T(8,128)(2,1)S(1)}, u32[]{:S(2)}, u32[]{:S(2)}) collective-permute-start(bf16[1024,512]{1,0:T(8,128)(2,1)S(1)} %copy-done), channel_id=1, source_target_pairs={{8,0},{10,2},{12,4},{14,6},{16,8},{1,9},{18,10},{3,11},{20,12},{5,... | collective-permute-start | bytes 3145736 | tf_op jit(solution)/shard_map/ppermute | solution.py:253
  15.3 38.7 %collective-permute-start = (bf16[1024,512]{1,0:T(8,128)(2,1)S(1)}, bf16[1024,512]{1,0:T(8,128)(2,1)S(1)}, u32[]{:S(2)}, u32[]{:S(2)}) collective-permute-start(bf16[1024,512]{1,0:T(8,128)(2,1)S(1)} %get-tuple-element.24.kept_ref.psi_ref), channel_id=1, source_target_pairs={{9,0},{11,2},{13,4},{15,6},{17,8},{0,9},{19,10},{2,11},{21,12},{4,... | collective-permute-start | bytes 3145736 | tf_op jit(solution)/shard_map/ppermute | solution.py:264
  39.8 12.9 %collective-permute-start.3 = (bf16[512,512]{1,0:T(8,128)(2,1)S(1)}, bf16[512,512]{1,0:T(8,128)(2,1)S(1)}, u32[]{:S(2)}, u32[]{:S(2)}) collective-permute-start(bf16[512,512]{1,0:T(8,128)(2,1)S(1)} %get-tuple-element.32.after_ref), channel_id=1, source_target_pairs={{2,1},{4,0},{6,5},{9,10},{10,9},{11,15},{12,8},{13,14},{14,13},{17... | collective-permute-start | bytes 1572872 | tf_op jit(solution)/shard_map/ppermute | solution.py:274
  46.7 18.1 %collective-permute-start.5 = (bf16[512,512]{1,0:T(8,128)(2,1)S(1)}, bf16[512,512]{1,0:T(8,128)(2,1)S(1)}, u32[]{:S(2)}, u32[]{:S(2)}) collective-permute-start(bf16[512,512]{1,0:T(8,128)(2,1)S(1)} %get-tuple-element.36.after_ref), channel_id=1, source_target_pairs={{2,1},{4,3},{6,5},{9,10},{10,9},{11,12},{12,11},{13,14},{14,13},{1... | collective-permute-start | bytes 1572872 | tf_op jit(solution)/shard_map/ppermute | solution.py:283
  52.7 12.1 %collective-permute-start.4 = (bf16[512,512]{1,0:T(8,128)(2,1)S(1)}, bf16[512,512]{1,0:T(8,128)(2,1)S(1)}, u32[]{:S(2)}, u32[]{:S(2)}) collective-permute-start(bf16[512,512]{1,0:T(8,128)(2,1)S(1)} %collective-permute-done.3.first_ref), channel_id=1, source_target_pairs={{0,3},{15,12},{8,11},{23,20},{16,19},{31,28}} | collective-permute-start | bytes 1572872 | tf_op jit(solution)/shard_map/ppermute | solution.py:294

commit v9 on v8

--- a/solution.py
+++ b/solution.py
@@ -114,26 +114,41 @@
     return (sector == 0) | (sector == right_count - 1)
 
 
-def early_or_local(edge, step, kept_ref, psi_ref, lefts_ref, rights_ref, left_ref, right_ref,
-                   term_ref, total_ref, work_ref, spare_left_ref, spare_right_ref, sems):
-    @pl.when(edge)
-    def _():
-        wait(Fetch(sems).start(*local_blocks(
-            left_ref, right_ref, spare_left_ref, spare_right_ref, step, 0)))
+def early_or_local(early, local, step, kept_ref, psi_ref, lefts_ref, rights_ref, left_ref,
+                   right_ref, term_ref, total_ref, work_ref, spare_left_ref, spare_right_ref,
+                   sems):
+    copies = [
+        pltpu.make_async_copy(source, target, sems.at[index])
+        for index, (source, target) in enumerate(local_blocks(
+            left_ref, right_ref, spare_left_ref, spare_right_ref, step, 0))
+    ]
+
+    @pl.when(local)
+    def _():
+        for copy in copies:
+            copy.start()
+
+    @pl.when(early)
+    def _():
+        early_term(psi_ref, lefts_ref, rights_ref, term_ref, work_ref)
+
+    @pl.when(local)
+    def _():
+        wait(copies)
         total_ref[...] += contract(spare_left_ref[0], kept_ref[...], spare_right_ref[0])
 
-    @pl.when(jnp.logical_not(edge))
-    def _():
-        early_term(psi_ref, lefts_ref, rights_ref, term_ref, work_ref)
+
+def takes_more(right_count):
+    return at_edge(right_count) | (lax.rem(lax.axis_index("rsec"), 2) == 1)
 
 
 def first_kernel(right_count, step, kept_ref, psi_ref, lefts_ref, rights_ref, left_ref,
                  right_ref, start_ref, term_ref, total_ref, work_ref, spare_left_ref,
                  spare_right_ref, sems):
     del start_ref
-    early_or_local(at_edge(right_count), step, kept_ref, psi_ref, lefts_ref, rights_ref,
-                   left_ref, right_ref, term_ref, total_ref, work_ref, spare_left_ref,
-                   spare_right_ref, sems)
+    early_or_local(jnp.logical_not(at_edge(right_count)), takes_more(right_count), step, kept_ref,
+                   psi_ref, lefts_ref, rights_ref, left_ref, right_ref, term_ref, total_ref,
+                   work_ref, spare_left_ref, spare_right_ref, sems)
 
 
 def second_kernel(right_count, step, next_step, kept_ref, psi_ref, lefts_ref, rights_ref,
@@ -142,7 +157,8 @@
     del start_ref, after_ref
     coming = Fetch(next_sems).start(*local_blocks(
         left_ref, right_ref, next_left_ref, next_right_ref, next_step, 0))
-    early_or_local(at_edge(right_count), step, kept_ref, psi_ref, lefts_ref, rights_ref,
+    edge = at_edge(right_count)
+    early_or_local(jnp.logical_not(edge), edge, step, kept_ref, psi_ref, lefts_ref, rights_ref,
                    left_ref, right_ref, term_ref, total_ref, work_ref, spare_left_ref,
                    spare_right_ref, sems)
     wait(coming)
@@ -157,19 +173,33 @@
     wait(coming)
 
 
-def tail_kernel(right_count, step, psi_ref, moved_ref, left0_ref, right0_ref, upper_ref,
-                lower_ref, across_ref, left_ref, right_ref, start_ref, after_ref, total_ref,
-                spare_left_ref, spare_right_ref, sems):
+def tail_kernel(right_count, step, psi_ref, left0_ref, right0_ref, left_ref, right_ref,
+                start_ref, after_ref, total_ref, spare_left_ref, spare_right_ref, sems):
     del start_ref, after_ref
+    more = jnp.logical_not(takes_more(right_count))
+    copies = [
+        pltpu.make_async_copy(source, target, sems.at[index])
+        for index, (source, target) in enumerate(local_blocks(
+            left_ref, right_ref, spare_left_ref, spare_right_ref, step, 0))
+    ]
+
+    @pl.when(more)
+    def _():
+        for copy in copies:
+            copy.start()
 
     @pl.when(jnp.logical_not(at_edge(right_count)))
     def _():
-        coming = Fetch(sems).start(*local_blocks(
-            left_ref, right_ref, spare_left_ref, spare_right_ref, step, 0))
         total_ref[...] += contract(left0_ref[0], psi_ref[...], right0_ref[0])
-        wait(coming)
+
+    @pl.when(more)
+    def _():
+        wait(copies)
         total_ref[...] += contract(spare_left_ref[0], psi_ref[...], spare_right_ref[0])
 
+
+def late_kernel(moved_ref, upper_ref, lower_ref, across_ref, start_ref, total_ref):
+    del start_ref
     part = upper_ref.shape[1]
     for index in range(across_ref.shape[0]):
         for rows, side_ref in ((slice(0, part), upper_ref), (slice(part, None), lower_ref)):
@@ -295,13 +325,21 @@
 
     (total,) = call(
         functools.partial(tail_kernel, right_count, local_first + 2),
-        [in_vmem] * 7 + [in_hbm, in_hbm, in_vmem, in_hbm],
+        [in_vmem] * 3 + [in_hbm, in_hbm, in_vmem, in_hbm],
         [total_shape],
         [lefts(1), rights(1), sems(2)],
-        cost(2 + charged_count, rows, rows, columns),
-        aliases={9: 0},
-    )(kept, moved_across, rest_left, rest_right, upper, lower, across, left_env, right_env, total,
-      second)
+        cost(2, rows, rows, columns),
+        aliases={5: 0},
+    )(kept, rest_left, rest_right, left_env, right_env, total, second)
+    moved_across, across, total = lax.optimization_barrier((moved_across, across, total))
+    (total,) = call(
+        late_kernel,
+        [in_vmem] * 5,
+        [total_shape],
+        [],
+        cost(charged_count, rows, rows, columns),
+        aliases={4: 0},
+    )(moved_across, upper, lower, across, total)
     (out,) = call(
         functools.partial(finish_kernel, right_count),
         [in_vmem] * 4,

time: 66.4 us -> 45.8 us (0.69)
  the two profiles are of different devices: /device:TPU:19 before, /device:TPU:12 now
where the time goes in v9:
time: 45.8 us; the launch traced here: 45.6 us
  Pallas kernels  31.5 us (69%)
  starting transfers between devices  13.2 us (29%)
  waiting for transfers between devices  0.58 us (1%)
    pallas_call x1, Pallas kernels, shards(): call(local_kernel, [in_smem, in_hbm, in_hbm, in_hbm], [total_shape, pltpu...  11.3 us
    pallas_call x1, Pallas kernels, shards(): call(late_kernel, [in_vmem] * 5, [total_shape], [], cost(charged_count, r...  6.67 us
    pallas_call x1, Pallas kernels, shards(): call(functools.partial(tail_kernel, right_count, local_first + 2), [in_vm...  3.63 us
    pallas_call x1, Pallas kernels, shards(): call(functools.partial(second_kernel, right_count, local_first + 1, local...  3.49 us
    pallas_call x1, Pallas kernels, shards(): call(functools.partial(first_kernel, right_count, local_first + 2), [in_v...  3.46 us
    ppermute x1, starting transfers between devices, shards(): second_received = lax.ppermute(second, axes, along)  3.28 us
    ppermute x1, starting transfers between devices, shards(): moved_across = lax.ppermute(kept, axes, crossed)  3.1 us
    ppermute x1, starting transfers between devices, shards(): first_received = lax.ppermute(first, axes, onward)  2.48 us
  transfers between devices with their start and end apart: 6, of which 2 were waited for; matrix products, arithmetic and copies ran while one was open for 0% of the time, Pallas kernels for 67%

profile of v9, /device:TPU:12, one launch (start us, length us, event | category | flops | bytes accessed | tf_op | source)
XLA Modules:
  0.0 45.6 jit_solution(10631258822325927186)
XLA Ops:
  0.0 2.3 %collective-permute-start.2 = (bf16[1024,512]{1,0:T(8,128)(2,1)}, bf16[1024,512]{1,0:T(8,128)(2,1)S(1)}, u32[]{:S(2)}, u32[]{:S(2)}) collective-permute-start(bf16[1024,512]{1,0:T(8,128)(2,1)} %whole_ref.1), channel_id=1, source_target_pairs={{8,0},{10,2},{12,4},{14,6},{16,8},{1,9},{18,10},{3,11},{20,12},{5,... | collective-permute-start | bytes 3145736 | tf_op jit(solution)/shard_map/ppermute | solution.py:283
  2.4 11.3 %shard_map.37 = (f32[1024,512]{1,0:T(8,128)S(1)}, bf16[1024,512]{1,0:T(8,128)(2,1)S(1)}, bf16[4,512,1024]{2,1,0:T(8,128)(2,1)S(1)}, bf16[4,512,1024]{2,1,0:T(8,1...) custom-call(s32[1]{0:T(128)} %bitcast.charged_ref, bf16[1024,512]{1,0:T(8,128)(2,1)} %whole_ref.1, ...), custom_call_target="tpu_custom_call" | custom-call | flops 8053063680 | bytes 13107200 | tf_op jit(solution)/shard_map/pallas_call | solution.py:285
  13.6 0.8 %collective-permute-start.1 = (bf16[4,512,512]{2,1,0:T(8,128)(2,1)S(1)}, bf16[4,512,512]{2,1,0:T(8,128)(2,1)S(1)}, u32[]{:S(2)}, u32[]{:S(2)}) collective-permute-start(bf16[4,512,512]{2,1,0:T(8,128)(2,1)S(1)} %get-tuple-element.28), channel_id=1, source_target_pairs={{1,0},{0,1},{3,2},{2,3},{5,4},{4,5},{7,6},{6,7},{9,8},{8,9},{11,10... | collective-permute-start | bytes 6291464 | tf_op jit(solution)/shard_map/ppermute | solution.py:314
  14.4 3.1 %collective-permute-start = (bf16[1024,512]{1,0:T(8,128)(2,1)S(1)}, bf16[1024,512]{1,0:T(8,128)(2,1)S(1)}, u32[]{:S(2)}, u32[]{:S(2)}) collective-permute-start(bf16[1024,512]{1,0:T(8,128)(2,1)S(1)} %get-tuple-element.27.kept_ref.psi_ref), channel_id=1, source_target_pairs={{9,0},{11,2},{13,4},{15,6},{17,8},{0,9},{19,10},{2,11},{21,12},{4,... | collective-permute-start | bytes 3145736 | tf_op jit(solution)/shard_map/ppermute | solution.py:294
  17.5 0.0 collective-permute-done.2.psi_ref
  17.5 3.5 %shard_map.38 = (bf16[512,512]{1,0:T(8,128)(2,1)S(1)}, f32[1024,512]{1,0:T(8,128)S(1)}) custom-call(bf16[1024,512]{1,0:T(8,128)(2,1)S(1)} %get-tuple-element.27.kept_ref.psi_ref, bf16[1024,512]{1,0:T(8,128)(2,1)S(1)} %collective-permute-done.2.psi_ref, ...), custom_call_target="tpu_custom_call", output_to_operand_aliasing={{1}: (6, {})} | custom-call | flops 3221225472 | bytes 6291456 | tf_op jit(solution)/shard_map/pallas_call | solution.py:296
  21.0 2.5 %collective-permute-start.3 = (bf16[512,512]{1,0:T(8,128)(2,1)S(1)}, bf16[512,512]{1,0:T(8,128)(2,1)S(1)}, u32[]{:S(2)}, u32[]{:S(2)}) collective-permute-start(bf16[512,512]{1,0:T(8,128)(2,1)S(1)} %get-tuple-element.36.after_ref), channel_id=1, source_target_pairs={{2,1},{4,0},{6,5},{9,10},{10,9},{11,15},{12,8},{13,14},{14,13},{17... | collective-permute-start | bytes 1572872 | tf_op jit(solution)/shard_map/ppermute | solution.py:304
  23.5 3.5 %shard_map.39 = (bf16[512,512]{1,0:T(8,128)(2,1)S(1)}, f32[1024,512]{1,0:T(8,128)S(1)}, bf16[1,1024,1024]{2,1,0:T(8,128)(2,1)S(1)}, bf16[1,512,512]{2,1,0:T(8,128)(2,1)S(1)}) custom-call(bf16[1024,512]{1,0:T(8,128)(2,1)S(1)} %get-tuple-element.27.kept_ref.psi_ref, ...), custom_call_target="tpu_custom_call", output_to_operand_aliasing={{1}: (6, {})} | custom-call | flops 3221225472 | bytes 6291456 | tf_op jit(solution)/shard_map/pallas_call | solution.py:305
  27.0 3.3 %collective-permute-start.5 = (bf16[512,512]{1,0:T(8,128)(2,1)S(1)}, bf16[512,512]{1,0:T(8,128)(2,1)S(1)}, u32[]{:S(2)}, u32[]{:S(2)}) collective-permute-start(bf16[512,512]{1,0:T(8,128)(2,1)S(1)} %get-tuple-element.40.after_ref), channel_id=1, source_target_pairs={{2,1},{4,3},{6,5},{9,10},{10,9},{11,12},{12,11},{13,14},{14,13},{1... | collective-permute-start | bytes 1572872 | tf_op jit(solution)/shard_map/ppermute | solution.py:313
  30.2 1.8 %shard_map.40 = (f32[1024,512]{1,0:T(8,128)S(1)}, bf16[1,1024,1024]{2,1,0:T(8,128)(2,1)S(1)}, bf16[1,512,512]{2,1,0:T(8,128)(2,1)S(1)}) custom-call(bf16[1024,512]{1,0:T(8,128)(2,1)S(1)} %get-tuple-element.27.kept_ref.psi_ref, bf16[1,1024,1024]{2,1,0:T(8,128)(2,1)S(1)} %get-tuple-element.37.left0_ref, ...), custom_call_target="tpu_custom_call", output_to_operand_aliasing={{0}: (5, {})} | custom-call | flops 1610612736 | bytes 2621440 | tf_op jit(solution)/shard_map/pallas_call | solution.py:315
  32.1 0.0 collective-permute-done.3.first_ref
  32.1 1.3 %collective-permute-start.4 = (bf16[512,512]{1,0:T(8,128)(2,1)S(1)}, bf16[512,512]{1,0:T(8,128)(2,1)S(1)}, u32[]{:S(2)}, u32[]{:S(2)}) collective-permute-start(bf16[512,512]{1,0:T(8,128)(2,1)S(1)} %collective-permute-done.3.first_ref), channel_id=1, source_target_pairs={{0,3},{15,12},{8,11},{23,20},{16,19},{31,28}} | collective-permute-start | bytes 1572872 | tf_op jit(solution)/shard_map/ppermute | solution.py:324
  33.4 3.6 %shard_map.41.start_ref = f32[1024,512]{1,0:T(8,128)S(1)} custom-call(bf16[1024,512]{1,0:T(8,128)(2,1)S(1)} %get-tuple-element.27.kept_ref.psi_ref, bf16[1,1024,1024]{2,1,0:T(8,128)(2,1)S(1)} %get-tuple-element.41.left0_ref, bf16[1,512,512]{2,1,0:T(8,128)(2,1)S(1)} %get-tuple-element.42.right0_ref, ...), custom_call_target="tpu_custom_call", output_to_operand_aliasing={{}: (5, {})} | custom-call | flops 3221225472 | bytes 5242880 | tf_op jit(solution)/shard_map/pallas_call | solution.py:326
  37.0 0.0 collective-permute-done.moved_ref
  37.0 0.0 collective-permute-done.1.across_ref
  37.0 6.7 %shard_map.42.total_ref = f32[1024,512]{1,0:T(8,128)S(1)} custom-call(bf16[1024,512]{1,0:T(8,128)(2,1)S(1)} %collective-permute-done.moved_ref, bf16[4,512,1024]{2,1,0:T(8,128)(2,1)S(1)} %get-tuple-element.33.lefts_ref.upper_ref, bf16[4,512,1024]{2,1,0:T(8,128)(2,1)S(1)} %get-tuple-element.31.lefts_ref.lower_ref, ...), custom_call_target="tpu_custom_call", output_to_operand_aliasing={{}: (4, {})} | custom-call | flops 6442450944 | bytes 10485760 | tf_op jit(solution)/shard_map/pallas_call | solution.py:335
  43.7 0.1 collective-permute-done.5.second_ref
  43.9 0.4 collective-permute-done.4.relay_ref
  44.3 1.1 %shard_map.43 = bf16[1024,512]{1,0:T(8,128)(2,1)} custom-call(f32[1024,512]{1,0:T(8,128)S(1)} %shard_map.42.total_ref, bf16[512,512]{1,0:T(8,128)(2,1)S(1)} %collective-permute-done.3.first_ref, bf16[512,512]{1,0:T(8,128)(2,1)S(1)} %collective-permute-done.4.relay_ref, bf16[512,512]{1,0:T(8,128)(2,1)S(1)} %collective-permute-done.5.second_ref), custom_call_target="tpu_custom_call" | custom-call | tf_op jit(solution)/shard_map/pallas_call | solution.py:343
Async XLA Ops:
  0.0 17.5 %collective-permute-start.2 = (bf16[1024,512]{1,0:T(8,128)(2,1)}, bf16[1024,512]{1,0:T(8,128)(2,1)S(1)}, u32[]{:S(2)}, u32[]{:S(2)}) collective-permute-start(bf16[1024,512]{1,0:T(8,128)(2,1)} %whole_ref.1), channel_id=1, source_target_pairs={{8,0},{10,2},{12,4},{14,6},{16,8},{1,9},{18,10},{3,11},{20,12},{5,... | collective-permute-start | bytes 3145736 | tf_op jit(solution)/shard_map/ppermute | solution.py:283
  13.6 23.4 %collective-permute-start.1 = (bf16[4,512,512]{2,1,0:T(8,128)(2,1)S(1)}, bf16[4,512,512]{2,1,0:T(8,128)(2,1)S(1)}, u32[]{:S(2)}, u32[]{:S(2)}) collective-permute-start(bf16[4,512,512]{2,1,0:T(8,128)(2,1)S(1)} %get-tuple-element.28), channel_id=1, source_target_pairs={{1,0},{0,1},{3,2},{2,3},{5,4},{4,5},{7,6},{6,7},{9,8},{8,9},{11,10... | collective-permute-start | bytes 6291464 | tf_op jit(solution)/shard_map/ppermute | solution.py:314
  14.4 22.6 %collective-permute-start = (bf16[1024,512]{1,0:T(8,128)(2,1)S(1)}, bf16[1024,512]{1,0:T(8,128)(2,1)S(1)}, u32[]{:S(2)}, u32[]{:S(2)}) collective-permute-start(bf16[1024,512]{1,0:T(8,128)(2,1)S(1)} %get-tuple-element.27.kept_ref.psi_ref), channel_id=1, source_target_pairs={{9,0},{11,2},{13,4},{15,6},{17,8},{0,9},{19,10},{2,11},{21,12},{4,... | collective-permute-start | bytes 3145736 | tf_op jit(solution)/shard_map/ppermute | solution.py:294
  21.0 11.1 %collective-permute-start.3 = (bf16[512,512]{1,0:T(8,128)(2,1)S(1)}, bf16[512,512]{1,0:T(8,128)(2,1)S(1)}, u32[]{:S(2)}, u32[]{:S(2)}) collective-permute-start(bf16[512,512]{1,0:T(8,128)(2,1)S(1)} %get-tuple-element.36.after_ref), channel_id=1, source_target_pairs={{2,1},{4,0},{6,5},{9,10},{10,9},{11,15},{12,8},{13,14},{14,13},{17... | collective-permute-start | bytes 1572872 | tf_op jit(solution)/shard_map/ppermute | solution.py:304
  27.0 16.9 %collective-permute-start.5 = (bf16[512,512]{1,0:T(8,128)(2,1)S(1)}, bf16[512,512]{1,0:T(8,128)(2,1)S(1)}, u32[]{:S(2)}, u32[]{:S(2)}) collective-permute-start(bf16[512,512]{1,0:T(8,128)(2,1)S(1)} %get-tuple-element.40.after_ref), channel_id=1, source_target_pairs={{2,1},{4,3},{6,5},{9,10},{10,9},{11,12},{12,11},{13,14},{14,13},{1... | collective-permute-start | bytes 1572872 | tf_op jit(solution)/shard_map/ppermute | solution.py:313
  32.1 12.2 %collective-permute-start.4 = (bf16[512,512]{1,0:T(8,128)(2,1)S(1)}, bf16[512,512]{1,0:T(8,128)(2,1)S(1)}, u32[]{:S(2)}, u32[]{:S(2)}) collective-permute-start(bf16[512,512]{1,0:T(8,128)(2,1)S(1)} %collective-permute-done.3.first_ref), channel_id=1, source_target_pairs={{0,3},{15,12},{8,11},{23,20},{16,19},{31,28}} | collective-permute-start | bytes 1572872 | tf_op jit(solution)/shard_map/ppermute | solution.py:324

commit v10 on v9

--- a/solution.py
+++ b/solution.py
@@ -74,8 +74,18 @@
     ]
 
 
-def local_kernel(charged_ref, whole_ref, left_ref, right_ref, total_ref, psi_ref, next_left_ref,
-                 lower_ref, next_right_ref, give_ref, lefts_ref, rights_ref, sems):
+def spare_copies(left_ref, right_ref, left_target, right_target, step, half, sems):
+    channel, part = local_channel(step), left_target.shape[0]
+    rows = pl.ds(half * part, part)
+    return [
+        pltpu.make_async_copy(left_ref.at[channel, rows, :], left_target, sems.at[0]),
+        pltpu.make_async_copy(right_ref.at[channel], right_target, sems.at[1]),
+    ]
+
+
+def local_kernel(right_count, spare_step, charged_ref, whole_ref, left_ref, right_ref, total_ref, psi_ref, next_left_ref,
+                 lower_ref, next_right_ref, give_ref, lefts_ref, rights_ref, spare_left_ref,
+                 spare_right_ref, sems, spare_sems):
     charged = charged_ref[0]
     fetch = Fetch(sems)
     steps = lefts_ref.shape[0]
@@ -84,17 +94,33 @@
     )
     coming = {0: fetch.start((whole_ref, psi_ref)) + bring(0)}
     last = []
+    more = jnp.logical_not(takes_more(right_count))
+    part = spare_left_ref.shape[0]
+    spare = spare_copies(left_ref, right_ref, spare_left_ref, spare_right_ref, spare_step, 0,
+                         spare_sems)
     for step in range(steps):
         wait(coming[step])
-        for more in range(1, steps) if step == 0 else ():
-            coming[more] = bring(more)
+        for later in range(1, steps) if step == 0 else ():
+            coming[later] = bring(later)
         if step == 1:
             last += fetch.start(*right_blocks(right_ref, next_right_ref, charged))
             last += fetch.start(*half_blocks(left_ref, next_left_ref, charged, 0))
             last += fetch.start(*half_blocks(left_ref, lower_ref, charged, 1))
             last += fetch.start(*right_blocks(right_ref, give_ref, period - 1 - charged))
+        if step == 2:
+            @pl.when(more)
+            def _():
+                for copy in spare:
+                    copy.start()
+
         term = contract(lefts_ref[step], psi_ref[...], rights_ref[step])
         total_ref[...] = total_ref[...] + term if step else term
+
+    @pl.when(more)
+    def _():
+        wait(spare)
+        total_ref[:part, :] += contract(spare_left_ref[...], psi_ref[...], spare_right_ref[...])
+
     wait(last)
 
 
@@ -177,15 +203,12 @@
                 start_ref, after_ref, total_ref, spare_left_ref, spare_right_ref, sems):
     del start_ref, after_ref
     more = jnp.logical_not(takes_more(right_count))
-    copies = [
-        pltpu.make_async_copy(source, target, sems.at[index])
-        for index, (source, target) in enumerate(local_blocks(
-            left_ref, right_ref, spare_left_ref, spare_right_ref, step, 0))
-    ]
+    part = spare_left_ref.shape[0]
+    spare = spare_copies(left_ref, right_ref, spare_left_ref, spare_right_ref, step, 1, sems)
 
     @pl.when(more)
     def _():
-        for copy in copies:
+        for copy in spare:
             copy.start()
 
     @pl.when(jnp.logical_not(at_edge(right_count)))
@@ -194,8 +217,8 @@
 
     @pl.when(more)
     def _():
-        wait(copies)
-        total_ref[...] += contract(spare_left_ref[0], psi_ref[...], spare_right_ref[0])
+        wait(spare)
+        total_ref[part:, :] += contract(spare_left_ref[...], psi_ref[...], spare_right_ref[...])
 
 
 def late_kernel(moved_ref, upper_ref, lower_ref, across_ref, start_ref, total_ref):
@@ -213,15 +236,21 @@
     middle = right_count // 2
     inner = (sector == middle - 1) | (sector == middle)
     relayed = inner | (sector == 0) | (sector == right_count - 1)
-    first = jnp.where(relayed, relay_ref[...], first_ref[...])
-    puts = []
-    for half, received in enumerate((first, second_ref[...])):
-        rows = pl.ds(half * part, part)
-        total = total_ref[rows, :] + received.astype(jnp.float32)
-        ready_ref[rows, :] = total.astype(ready_ref.dtype)
+    puts, step = [], part // 2
+
+    def put(offset, rows, received):
+        target = pl.ds(offset + rows.start, step)
+        total = total_ref[target, :] + received.astype(jnp.float32)
+        ready_ref[target, :] = total.astype(ready_ref.dtype)
         puts.append(pltpu.make_async_copy(
-            ready_ref.at[rows, :], out_ref.at[rows, :], sems.at[half]))
+            ready_ref.at[target, :], out_ref.at[target, :], sems.at[len(puts)]))
         puts[-1].start()
+
+    pieces = [slice(0, step), slice(step, part)]
+    for rows in pieces:
+        put(part, rows, second_ref[rows, :])
+    for rows in pieces:
+        put(0, rows, jnp.where(relayed, relay_ref[rows, :], first_ref[rows, :]))
     wait(puts)
 
 
@@ -277,17 +306,18 @@
     left_env = pltpu.with_memory_space_constraint(left_whole, pltpu.HBM)
     right_env = pltpu.with_memory_space_constraint(right_whole, pltpu.HBM)
     total_shape = pltpu.VMEM((rows, columns), f32)
+    spare = [pltpu.VMEM((part, rows), bf16), pltpu.VMEM((columns, columns), bf16)]
     half_total = pltpu.VMEM((part, columns), f32)
     half_block = pltpu.VMEM((part, columns), bf16)
 
     moved = lax.ppermute(psi, axes, straight)
 
     total, kept, upper, lower, own, give = call(
-        local_kernel,
+        functools.partial(local_kernel, right_count, local_first + 2),
         [in_smem, in_hbm, in_hbm, in_hbm],
         [total_shape, pltpu.VMEM((rows, columns), bf16), halves, halves, rights(charged_count), rights(charged_count)],
-        [lefts(local_first), rights(local_first),
-         sems(2 * local_first + 1 + 4 * charged_count)],
+        [lefts(local_first), rights(local_first), *spare,
+         sems(2 * local_first + 1 + 4 * charged_count), sems(2)],
         cost(local_first, rows, rows, columns),
     )(charged, pltpu.with_memory_space_constraint(psi, pltpu.HBM), left_env, right_env)
 
@@ -327,7 +357,7 @@
         functools.partial(tail_kernel, right_count, local_first + 2),
         [in_vmem] * 3 + [in_hbm, in_hbm, in_vmem, in_hbm],
         [total_shape],
-        [lefts(1), rights(1), sems(2)],
+        [*spare, sems(2)],
         cost(2, rows, rows, columns),
         aliases={5: 0},
     )(kept, rest_left, rest_right, left_env, right_env, total, second)
@@ -344,7 +374,7 @@
         functools.partial(finish_kernel, right_count),
         [in_vmem] * 4,
         [pltpu.VMEM((rows, columns), bf16)],
-        [pltpu.VMEM((rows, columns), bf16), sems(2)],
+        [pltpu.VMEM((rows, columns), bf16), sems(4)],
         None,
         out_specs=[in_hbm],
     )(total, first_received, relayed, second_received)

time: 45.8 us -> 46.8 us (1.022)
  the two profiles are of different devices: /device:TPU:12 before, /device:TPU:20 now
where the time goes in v10:
time: 46.8 us; the launch traced here: 46.5 us
  Pallas kernels  31.7 us (68%)
  starting transfers between devices  12.3 us (26%)
  waiting for transfers between devices  2.15 us (5%)
    pallas_call x1, Pallas kernels, shards(): call(functools.partial(local_kernel, right_count, local_first + 2), [in_s...  12.3 us
    pallas_call x1, Pallas kernels, shards(): call(late_kernel, [in_vmem] * 5, [total_shape], [], cost(charged_count, r...  6.67 us
    pallas_call x1, Pallas kernels, shards(): call(functools.partial(second_kernel, right_count, local_first + 1, local...  3.67 us
    ppermute x1, starting transfers between devices, shards(): moved_across = lax.ppermute(kept, axes, crossed)  3.63 us
    ppermute x1, starting transfers between devices, shards(): second_received = lax.ppermute(second, axes, along)  3.5 us
    pallas_call x1, Pallas kernels, shards(): call(functools.partial(first_kernel, right_count, local_first + 2), [in_v...  3.46 us
    pallas_call x1, Pallas kernels, shards(): call(functools.partial(tail_kernel, right_count, local_first + 2), [in_vm...  2.82 us
    ppermute x1, starting transfers between devices, shards(): moved = lax.ppermute(psi, axes, straight)  2.35 us
  transfers between devices with their start and end apart: 6, of which 1 were waited for; matrix products, arithmetic and copies ran while one was open for 0% of the time, Pallas kernels for 66%

profile of v10, /device:TPU:20, one launch (start us, length us, event | category | flops | bytes accessed | tf_op | source)
XLA Modules:
  0.0 46.5 jit_solution(297843515770964789)
XLA Ops:
  0.0 2.3 %collective-permute-start.2 = (bf16[1024,512]{1,0:T(8,128)(2,1)}, bf16[1024,512]{1,0:T(8,128)(2,1)S(1)}, u32[]{:S(2)}, u32[]{:S(2)}) collective-permute-start(bf16[1024,512]{1,0:T(8,128)(2,1)} %whole_ref.1), channel_id=1, source_target_pairs={{8,0},{10,2},{12,4},{14,6},{16,8},{1,9},{18,10},{3,11},{20,12},{5,... | collective-permute-start | bytes 3145736 | tf_op jit(solution)/shard_map/ppermute | solution.py:313
  2.4 12.3 %shard_map.37 = (f32[1024,512]{1,0:T(8,128)S(1)}, bf16[1024,512]{1,0:T(8,128)(2,1)S(1)}, bf16[4,512,1024]{2,1,0:T(8,128)(2,1)S(1)}, bf16[4,512,1024]{2,1,0:T(8,1...) custom-call(s32[1]{0:T(128)} %bitcast.charged_ref, bf16[1024,512]{1,0:T(8,128)(2,1)} %whole_ref.1, ...), custom_call_target="tpu_custom_call" | custom-call | flops 8053063680 | bytes 13107200 | tf_op jit(solution)/shard_map/pallas_call | solution.py:315
  14.6 0.1 collective-permute-start.1
  14.7 3.6 %collective-permute-start = (bf16[1024,512]{1,0:T(8,128)(2,1)S(1)}, bf16[1024,512]{1,0:T(8,128)(2,1)S(1)}, u32[]{:S(2)}, u32[]{:S(2)}) collective-permute-start(bf16[1024,512]{1,0:T(8,128)(2,1)S(1)} %get-tuple-element.27.kept_ref.psi_ref), channel_id=1, source_target_pairs={{9,0},{11,2},{13,4},{15,6},{17,8},{0,9},{19,10},{2,11},{21,12},{4,... | collective-permute-start | bytes 3145736 | tf_op jit(solution)/shard_map/ppermute | solution.py:324
  18.4 0.0 collective-permute-done.2.psi_ref
  18.4 3.5 %shard_map.38 = (bf16[512,512]{1,0:T(8,128)(2,1)S(1)}, f32[1024,512]{1,0:T(8,128)S(1)}) custom-call(bf16[1024,512]{1,0:T(8,128)(2,1)S(1)} %get-tuple-element.27.kept_ref.psi_ref, bf16[1024,512]{1,0:T(8,128)(2,1)S(1)} %collective-permute-done.2.psi_ref, ...), custom_call_target="tpu_custom_call", output_to_operand_aliasing={{1}: (6, {})} | custom-call | flops 3221225472 | bytes 6291456 | tf_op jit(solution)/shard_map/pallas_call | solution.py:326
  21.8 1.5 %collective-permute-start.3 = (bf16[512,512]{1,0:T(8,128)(2,1)S(1)}, bf16[512,512]{1,0:T(8,128)(2,1)S(1)}, u32[]{:S(2)}, u32[]{:S(2)}) collective-permute-start(bf16[512,512]{1,0:T(8,128)(2,1)S(1)} %get-tuple-element.36.after_ref), channel_id=1, source_target_pairs={{2,1},{4,0},{6,5},{9,10},{10,9},{11,15},{12,8},{13,14},{14,13},{17... | collective-permute-start | bytes 1572872 | tf_op jit(solution)/shard_map/ppermute | solution.py:334
  23.3 3.7 %shard_map.39 = (bf16[512,512]{1,0:T(8,128)(2,1)S(1)}, f32[1024,512]{1,0:T(8,128)S(1)}, bf16[1,1024,1024]{2,1,0:T(8,128)(2,1)S(1)}, bf16[1,512,512]{2,1,0:T(8,128)(2,1)S(1)}) custom-call(bf16[1024,512]{1,0:T(8,128)(2,1)S(1)} %get-tuple-element.27.kept_ref.psi_ref, ...), custom_call_target="tpu_custom_call", output_to_operand_aliasing={{1}: (6, {})} | custom-call | flops 3221225472 | bytes 6291456 | tf_op jit(solution)/shard_map/pallas_call | solution.py:335
  27.0 3.5 %collective-permute-start.5 = (bf16[512,512]{1,0:T(8,128)(2,1)S(1)}, bf16[512,512]{1,0:T(8,128)(2,1)S(1)}, u32[]{:S(2)}, u32[]{:S(2)}) collective-permute-start(bf16[512,512]{1,0:T(8,128)(2,1)S(1)} %get-tuple-element.40.after_ref), channel_id=1, source_target_pairs={{2,1},{4,3},{6,5},{9,10},{10,9},{11,12},{12,11},{13,14},{14,13},{1... | collective-permute-start | bytes 1572872 | tf_op jit(solution)/shard_map/ppermute | solution.py:343
  30.5 1.8 %shard_map.40 = (f32[1024,512]{1,0:T(8,128)S(1)}, bf16[1,1024,1024]{2,1,0:T(8,128)(2,1)S(1)}, bf16[1,512,512]{2,1,0:T(8,128)(2,1)S(1)}) custom-call(bf16[1024,512]{1,0:T(8,128)(2,1)S(1)} %get-tuple-element.27.kept_ref.psi_ref, bf16[1,1024,1024]{2,1,0:T(8,128)(2,1)S(1)} %get-tuple-element.37.left0_ref, ...), custom_call_target="tpu_custom_call", output_to_operand_aliasing={{0}: (5, {})} | custom-call | flops 1610612736 | bytes 2621440 | tf_op jit(solution)/shard_map/pallas_call | solution.py:345
  32.4 0.0 collective-permute-done.3.first_ref
  32.4 1.3 %collective-permute-start.4 = (bf16[512,512]{1,0:T(8,128)(2,1)S(1)}, bf16[512,512]{1,0:T(8,128)(2,1)S(1)}, u32[]{:S(2)}, u32[]{:S(2)}) collective-permute-start(bf16[512,512]{1,0:T(8,128)(2,1)S(1)} %collective-permute-done.3.first_ref), channel_id=1, source_target_pairs={{0,3},{15,12},{8,11},{23,20},{16,19},{31,28}} | collective-permute-start | bytes 1572872 | tf_op jit(solution)/shard_map/ppermute | solution.py:354
  33.7 2.8 %shard_map.41.start_ref = f32[1024,512]{1,0:T(8,128)S(1)} custom-call(bf16[1024,512]{1,0:T(8,128)(2,1)S(1)} %get-tuple-element.27.kept_ref.psi_ref, bf16[1,1024,1024]{2,1,0:T(8,128)(2,1)S(1)} %get-tuple-element.41.left0_ref, bf16[1,512,512]{2,1,0:T(8,128)(2,1)S(1)} %get-tuple-element.42.right0_ref, ...), custom_call_target="tpu_custom_call", output_to_operand_aliasing={{}: (5, {})} | custom-call | flops 3221225472 | bytes 5242880 | tf_op jit(solution)/shard_map/pallas_call | solution.py:356
  36.5 0.0 collective-permute-done.moved_ref
  36.5 0.0 collective-permute-done.1.across_ref
  36.5 6.7 %shard_map.42.total_ref = f32[1024,512]{1,0:T(8,128)S(1)} custom-call(bf16[1024,512]{1,0:T(8,128)(2,1)S(1)} %collective-permute-done.moved_ref, bf16[4,512,1024]{2,1,0:T(8,128)(2,1)S(1)} %get-tuple-element.33.lefts_ref.upper_ref, bf16[4,512,1024]{2,1,0:T(8,128)(2,1)S(1)} %get-tuple-element.31.lefts_ref.lower_ref, ...), custom_call_target="tpu_custom_call", output_to_operand_aliasing={{}: (4, {})} | custom-call | flops 6442450944 | bytes 10485760 | tf_op jit(solution)/shard_map/pallas_call | solution.py:365
  43.2 0.0 collective-permute-done.5.second_ref
  43.2 2.1 %collective-permute-done.4.relay_ref = bf16[512,512]{1,0:T(8,128)(2,1)S(1)} collective-permute-done((bf16[512,512]{1,0:T(8,128)(2,1)S(1)}, bf16[512,512]{1,0:T(8,128)(2,1)S(1)}, u32[]{:S(2)}, u32[]{:S(2)}) %collective-permute-start.4) | collective-permute-done | bytes 524320 | tf_op jit(solution)/shard_map/ppermute | solution.py:354
  45.3 1.0 %shard_map.43 = bf16[1024,512]{1,0:T(8,128)(2,1)} custom-call(f32[1024,512]{1,0:T(8,128)S(1)} %shard_map.42.total_ref, bf16[512,512]{1,0:T(8,128)(2,1)S(1)} %collective-permute-done.3.first_ref, bf16[512,512]{1,0:T(8,128)(2,1)S(1)} %collective-permute-done.4.relay_ref, bf16[512,512]{1,0:T(8,128)(2,1)S(1)} %collective-permute-done.5.second_ref), custom_call_target="tpu_custom_call" | custom-call | tf_op jit(solution)/shard_map/pallas_call | solution.py:373
Async XLA Ops:
  0.0 18.4 %collective-permute-start.2 = (bf16[1024,512]{1,0:T(8,128)(2,1)}, bf16[1024,512]{1,0:T(8,128)(2,1)S(1)}, u32[]{:S(2)}, u32[]{:S(2)}) collective-permute-start(bf16[1024,512]{1,0:T(8,128)(2,1)} %whole_ref.1), channel_id=1, source_target_pairs={{8,0},{10,2},{12,4},{14,6},{16,8},{1,9},{18,10},{3,11},{20,12},{5,... | collective-permute-start | bytes 3145736 | tf_op jit(solution)/shard_map/ppermute | solution.py:313
  14.6 21.9 %collective-permute-start.1 = (bf16[4,512,512]{2,1,0:T(8,128)(2,1)S(1)}, bf16[4,512,512]{2,1,0:T(8,128)(2,1)S(1)}, u32[]{:S(2)}, u32[]{:S(2)}) collective-permute-start(bf16[4,512,512]{2,1,0:T(8,128)(2,1)S(1)} %get-tuple-element.28), channel_id=1, source_target_pairs={{1,0},{0,1},{3,2},{2,3},{5,4},{4,5},{7,6},{6,7},{9,8},{8,9},{11,10... | collective-permute-start | bytes 6291464 | tf_op jit(solution)/shard_map/ppermute | solution.py:344
  14.7 21.8 %collective-permute-start = (bf16[1024,512]{1,0:T(8,128)(2,1)S(1)}, bf16[1024,512]{1,0:T(8,128)(2,1)S(1)}, u32[]{:S(2)}, u32[]{:S(2)}) collective-permute-start(bf16[1024,512]{1,0:T(8,128)(2,1)S(1)} %get-tuple-element.27.kept_ref.psi_ref), channel_id=1, source_target_pairs={{9,0},{11,2},{13,4},{15,6},{17,8},{0,9},{19,10},{2,11},{21,12},{4,... | collective-permute-start | bytes 3145736 | tf_op jit(solution)/shard_map/ppermute | solution.py:324
  21.8 10.5 %collective-permute-start.3 = (bf16[512,512]{1,0:T(8,128)(2,1)S(1)}, bf16[512,512]{1,0:T(8,128)(2,1)S(1)}, u32[]{:S(2)}, u32[]{:S(2)}) collective-permute-start(bf16[512,512]{1,0:T(8,128)(2,1)S(1)} %get-tuple-element.36.after_ref), channel_id=1, source_target_pairs={{2,1},{4,0},{6,5},{9,10},{10,9},{11,15},{12,8},{13,14},{14,13},{17... | collective-permute-start | bytes 1572872 | tf_op jit(solution)/shard_map/ppermute | solution.py:334
  27.0 16.2 %collective-permute-start.5 = (bf16[512,512]{1,0:T(8,128)(2,1)S(1)}, bf16[512,512]{1,0:T(8,128)(2,1)S(1)}, u32[]{:S(2)}, u32[]{:S(2)}) collective-permute-start(bf16[512,512]{1,0:T(8,128)(2,1)S(1)} %get-tuple-element.40.after_ref), channel_id=1, source_target_pairs={{2,1},{4,3},{6,5},{9,10},{10,9},{11,12},{12,11},{13,14},{14,13},{1... | collective-permute-start | bytes 1572872 | tf_op jit(solution)/shard_map/ppermute | solution.py:343
  32.4 13.0 %collective-permute-start.4 = (bf16[512,512]{1,0:T(8,128)(2,1)S(1)}, bf16[512,512]{1,0:T(8,128)(2,1)S(1)}, u32[]{:S(2)}, u32[]{:S(2)}) collective-permute-start(bf16[512,512]{1,0:T(8,128)(2,1)S(1)} %collective-permute-done.3.first_ref), channel_id=1, source_target_pairs={{0,3},{15,12},{8,11},{23,20},{16,19},{31,28}} | collective-permute-start | bytes 1572872 | tf_op jit(solution)/shard_map/ppermute | solution.py:354

commit v11 on v10

--- a/solution.py
+++ b/solution.py
@@ -140,7 +140,7 @@
     return (sector == 0) | (sector == right_count - 1)
 
 
-def early_or_local(early, local, step, kept_ref, psi_ref, lefts_ref, rights_ref, left_ref,
+def early_or_local(early, local, whole, step, kept_ref, psi_ref, lefts_ref, rights_ref, left_ref,
                    right_ref, term_ref, total_ref, work_ref, spare_left_ref, spare_right_ref,
                    sems):
     copies = [
@@ -158,10 +158,18 @@
     def _():
         early_term(psi_ref, lefts_ref, rights_ref, term_ref, work_ref)
 
+    part = term_ref.shape[0]
+
     @pl.when(local)
     def _():
         wait(copies)
-        total_ref[...] += contract(spare_left_ref[0], kept_ref[...], spare_right_ref[0])
+        total_ref[:part, :] += contract(
+            spare_left_ref[0, :part, :], kept_ref[...], spare_right_ref[0])
+
+    @pl.when(whole)
+    def _():
+        total_ref[part:, :] += contract(
+            spare_left_ref[0, part:, :], kept_ref[...], spare_right_ref[0])
 
 
 def takes_more(right_count):
@@ -172,9 +180,10 @@
                  right_ref, start_ref, term_ref, total_ref, work_ref, spare_left_ref,
                  spare_right_ref, sems):
     del start_ref
-    early_or_local(jnp.logical_not(at_edge(right_count)), takes_more(right_count), step, kept_ref,
-                   psi_ref, lefts_ref, rights_ref, left_ref, right_ref, term_ref, total_ref,
-                   work_ref, spare_left_ref, spare_right_ref, sems)
+    edge = at_edge(right_count)
+    early_or_local(jnp.logical_not(edge), takes_more(right_count), edge, step, kept_ref, psi_ref,
+                   lefts_ref, rights_ref, left_ref, right_ref, term_ref, total_ref, work_ref,
+                   spare_left_ref, spare_right_ref, sems)
 
 
 def second_kernel(right_count, step, next_step, kept_ref, psi_ref, lefts_ref, rights_ref,
@@ -184,7 +193,7 @@
     coming = Fetch(next_sems).start(*local_blocks(
         left_ref, right_ref, next_left_ref, next_right_ref, next_step, 0))
     edge = at_edge(right_count)
-    early_or_local(jnp.logical_not(edge), edge, step, kept_ref, psi_ref, lefts_ref, rights_ref,
+    early_or_local(jnp.logical_not(edge), edge, edge, step, kept_ref, psi_ref, lefts_ref, rights_ref,
                    left_ref, right_ref, term_ref, total_ref, work_ref, spare_left_ref,
                    spare_right_ref, sems)
     wait(coming)
@@ -202,21 +211,14 @@
 def tail_kernel(right_count, step, psi_ref, left0_ref, right0_ref, left_ref, right_ref,
                 start_ref, after_ref, total_ref, spare_left_ref, spare_right_ref, sems):
     del start_ref, after_ref
-    more = jnp.logical_not(takes_more(right_count))
     part = spare_left_ref.shape[0]
     spare = spare_copies(left_ref, right_ref, spare_left_ref, spare_right_ref, step, 1, sems)
 
-    @pl.when(more)
+    @pl.when(jnp.logical_not(at_edge(right_count)))
     def _():
         for copy in spare:
             copy.start()
-
-    @pl.when(jnp.logical_not(at_edge(right_count)))
-    def _():
         total_ref[...] += contract(left0_ref[0], psi_ref[...], right0_ref[0])
-
-    @pl.when(more)
-    def _():
         wait(spare)
         total_ref[part:, :] += contract(spare_left_ref[...], psi_ref[...], spare_right_ref[...])
 
@@ -342,6 +344,7 @@
     )(kept, moved, lower, own, left_env, right_env, total, first)
     second_received = lax.ppermute(second, axes, along)
     across = lax.ppermute(give, axes, partner)
+    relayed = lax.ppermute(first_received, axes, relay)
     total, rest_left, rest_right = call(
         functools.partial(rest_kernel, local_first + 1),
         [in_vmem, in_vmem, in_vmem, in_hbm, in_hbm, in_vmem, in_hbm],
@@ -350,8 +353,6 @@
         cost(1, rows, rows, columns),
         aliases={5: 0},
     )(kept, rest_left, rest_right, left_env, right_env, total, second)
-    first_received, total = lax.optimization_barrier((first_received, total))
-    relayed = lax.ppermute(first_received, axes, relay)
 
     (total,) = call(
         functools.partial(tail_kernel, right_count, local_first + 2),

time: 46.8 us -> 47.5 us (1.015)
  the two profiles are of different devices: /device:TPU:20 before, /device:TPU:11 now
where the time goes in v11:
time: 47.5 us; the launch traced here: 47.3 us
  Pallas kernels  31.6 us (67%)
  starting transfers between devices  12.8 us (27%)
  waiting for transfers between devices  2.51 us (5%)
    pallas_call x1, Pallas kernels, shards(): call(functools.partial(local_kernel, right_count, local_first + 2), [in_s...  11.3 us
    pallas_call x1, Pallas kernels, shards(): call(late_kernel, [in_vmem] * 5, [total_shape], [], cost(charged_count, r...  6.67 us
    pallas_call x1, Pallas kernels, shards(): call(functools.partial(first_kernel, right_count, local_first + 2), [in_v...  4.45 us
    pallas_call x1, Pallas kernels, shards(): call(functools.partial(second_kernel, right_count, local_first + 1, local...  3.67 us
    ppermute x1, starting transfers between devices, shards(): moved = lax.ppermute(psi, axes, straight)  3.19 us
    ppermute x1, starting transfers between devices, shards(): second_received = lax.ppermute(second, axes, along)  3.16 us
    pallas_call x1, Pallas kernels, shards(): call(functools.partial(tail_kernel, right_count, local_first + 2), [in_vm...  2.7 us
    ppermute x1, starting transfers between devices, shards(): first_received = lax.ppermute(first, axes, onward)  2.4 us
  transfers between devices with their start and end apart: 6, of which 2 were waited for; matrix products, arithmetic and copies ran while one was open for 0% of the time, Pallas kernels for 65%

profile of v11, /device:TPU:11, one launch (start us, length us, event | category | flops | bytes accessed | tf_op | source)
XLA Modules:
  0.0 47.3 jit_solution(5300872725470819920)
XLA Ops:
  0.0 3.2 %collective-permute-start.2 = (bf16[1024,512]{1,0:T(8,128)(2,1)}, bf16[1024,512]{1,0:T(8,128)(2,1)S(1)}, u32[]{:S(2)}, u32[]{:S(2)}) collective-permute-start(bf16[1024,512]{1,0:T(8,128)(2,1)} %whole_ref.1), channel_id=1, source_target_pairs={{8,0},{10,2},{12,4},{14,6},{16,8},{1,9},{18,10},{3,11},{20,12},{5,... | collective-permute-start | bytes 3145736 | tf_op jit(solution)/shard_map/ppermute | solution.py:315
  3.2 11.3 %shard_map.37 = (f32[1024,512]{1,0:T(8,128)S(1)}, bf16[1024,512]{1,0:T(8,128)(2,1)S(1)}, bf16[4,512,1024]{2,1,0:T(8,128)(2,1)S(1)}, bf16[4,512,1024]{2,1,0:T(8,1...) custom-call(s32[1]{0:T(128)} %bitcast.charged_ref, bf16[1024,512]{1,0:T(8,128)(2,1)} %whole_ref.1, ...), custom_call_target="tpu_custom_call" | custom-call | flops 8053063680 | bytes 13107200 | tf_op jit(solution)/shard_map/pallas_call | solution.py:317
  14.5 0.9 %collective-permute-start.1 = (bf16[4,512,512]{2,1,0:T(8,128)(2,1)S(1)}, bf16[4,512,512]{2,1,0:T(8,128)(2,1)S(1)}, u32[]{:S(2)}, u32[]{:S(2)}) collective-permute-start(bf16[4,512,512]{2,1,0:T(8,128)(2,1)S(1)} %get-tuple-element.26), channel_id=1, source_target_pairs={{1,0},{0,1},{3,2},{2,3},{5,4},{4,5},{7,6},{6,7},{9,8},{8,9},{11,10... | collective-permute-start | bytes 6291464 | tf_op jit(solution)/shard_map/ppermute | solution.py:346
  15.4 1.9 %collective-permute-start = (bf16[1024,512]{1,0:T(8,128)(2,1)S(1)}, bf16[1024,512]{1,0:T(8,128)(2,1)S(1)}, u32[]{:S(2)}, u32[]{:S(2)}) collective-permute-start(bf16[1024,512]{1,0:T(8,128)(2,1)S(1)} %get-tuple-element.25.kept_ref.psi_ref), channel_id=1, source_target_pairs={{9,0},{11,2},{13,4},{15,6},{17,8},{0,9},{19,10},{2,11},{21,12},{4,... | collective-permute-start | bytes 3145736 | tf_op jit(solution)/shard_map/ppermute | solution.py:326
  17.3 0.0 collective-permute-done.2.psi_ref
  17.3 4.5 %shard_map.38 = (bf16[512,512]{1,0:T(8,128)(2,1)S(1)}, f32[1024,512]{1,0:T(8,128)S(1)}) custom-call(bf16[1024,512]{1,0:T(8,128)(2,1)S(1)} %get-tuple-element.25.kept_ref.psi_ref, bf16[1024,512]{1,0:T(8,128)(2,1)S(1)} %collective-permute-done.2.psi_ref, ...), custom_call_target="tpu_custom_call", output_to_operand_aliasing={{1}: (6, {})} | custom-call | flops 3221225472 | bytes 6291456 | tf_op jit(solution)/shard_map/pallas_call | solution.py:328
  21.8 2.4 %collective-permute-start.3 = (bf16[512,512]{1,0:T(8,128)(2,1)S(1)}, bf16[512,512]{1,0:T(8,128)(2,1)S(1)}, u32[]{:S(2)}, u32[]{:S(2)}) collective-permute-start(bf16[512,512]{1,0:T(8,128)(2,1)S(1)} %get-tuple-element.34.after_ref), channel_id=1, source_target_pairs={{2,1},{4,0},{6,5},{9,10},{10,9},{11,15},{12,8},{13,14},{14,13},{17... | collective-permute-start | bytes 1572872 | tf_op jit(solution)/shard_map/ppermute | solution.py:336
  24.2 3.7 %shard_map.39 = (bf16[512,512]{1,0:T(8,128)(2,1)S(1)}, f32[1024,512]{1,0:T(8,128)S(1)}, bf16[1,1024,1024]{2,1,0:T(8,128)(2,1)S(1)}, bf16[1,512,512]{2,1,0:T(8,128)(2,1)S(1)}) custom-call(bf16[1024,512]{1,0:T(8,128)(2,1)S(1)} %get-tuple-element.25.kept_ref.psi_ref, ...), custom_call_target="tpu_custom_call", output_to_operand_aliasing={{1}: (6, {})} | custom-call | flops 3221225472 | bytes 6291456 | tf_op jit(solution)/shard_map/pallas_call | solution.py:337
  27.8 3.2 %collective-permute-start.5 = (bf16[512,512]{1,0:T(8,128)(2,1)S(1)}, bf16[512,512]{1,0:T(8,128)(2,1)S(1)}, u32[]{:S(2)}, u32[]{:S(2)}) collective-permute-start(bf16[512,512]{1,0:T(8,128)(2,1)S(1)} %get-tuple-element.38.after_ref), channel_id=1, source_target_pairs={{2,1},{4,3},{6,5},{9,10},{10,9},{11,12},{12,11},{13,14},{14,13},{1... | collective-permute-start | bytes 1572872 | tf_op jit(solution)/shard_map/ppermute | solution.py:345
  31.0 1.8 %shard_map.40 = (f32[1024,512]{1,0:T(8,128)S(1)}, bf16[1,1024,1024]{2,1,0:T(8,128)(2,1)S(1)}, bf16[1,512,512]{2,1,0:T(8,128)(2,1)S(1)}) custom-call(bf16[1024,512]{1,0:T(8,128)(2,1)S(1)} %get-tuple-element.25.kept_ref.psi_ref, bf16[1,1024,1024]{2,1,0:T(8,128)(2,1)S(1)} %get-tuple-element.35.left0_ref, ...), custom_call_target="tpu_custom_call", output_to_operand_aliasing={{0}: (5, {})} | custom-call | flops 1610612736 | bytes 2621440 | tf_op jit(solution)/shard_map/pallas_call | solution.py:348
  32.8 2.7 %shard_map.41.start_ref = f32[1024,512]{1,0:T(8,128)S(1)} custom-call(bf16[1024,512]{1,0:T(8,128)(2,1)S(1)} %get-tuple-element.25.kept_ref.psi_ref, bf16[1,1024,1024]{2,1,0:T(8,128)(2,1)S(1)} %get-tuple-element.39.left0_ref, bf16[1,512,512]{2,1,0:T(8,128)(2,1)S(1)} %get-tuple-element.40.right0_ref, ...), custom_call_target="tpu_custom_call", output_to_operand_aliasing={{}: (5, {})} | custom-call | flops 3221225472 | bytes 5242880 | tf_op jit(solution)/shard_map/pallas_call | solution.py:357
  35.6 0.0 collective-permute-done.3.first_ref
  35.6 1.3 %collective-permute-start.4 = (bf16[512,512]{1,0:T(8,128)(2,1)S(1)}, bf16[512,512]{1,0:T(8,128)(2,1)S(1)}, u32[]{:S(2)}, u32[]{:S(2)}) collective-permute-start(bf16[512,512]{1,0:T(8,128)(2,1)S(1)} %collective-permute-done.3.first_ref), channel_id=1, source_target_pairs={{0,3},{15,12},{8,11},{23,20},{16,19},{31,28}} | collective-permute-start | bytes 1572872 | tf_op jit(solution)/shard_map/ppermute | solution.py:347
  36.9 0.0 collective-permute-done.moved_ref
  36.9 0.0 collective-permute-done.1.across_ref
  36.9 6.7 %shard_map.42.total_ref = f32[1024,512]{1,0:T(8,128)S(1)} custom-call(bf16[1024,512]{1,0:T(8,128)(2,1)S(1)} %collective-permute-done.moved_ref, bf16[4,512,1024]{2,1,0:T(8,128)(2,1)S(1)} %get-tuple-element.31.lefts_ref.upper_ref, bf16[4,512,1024]{2,1,0:T(8,128)(2,1)S(1)} %get-tuple-element.29.lefts_ref.lower_ref, ...), custom_call_target="tpu_custom_call", output_to_operand_aliasing={{}: (4, {})} | custom-call | flops 6442450944 | bytes 10485760 | tf_op jit(solution)/shard_map/pallas_call | solution.py:366
  43.6 0.9 %collective-permute-done.5.second_ref = bf16[512,512]{1,0:T(8,128)(2,1)S(1)} collective-permute-done((bf16[512,512]{1,0:T(8,128)(2,1)S(1)}, bf16[512,512]{1,0:T(8,128)(2,1)S(1)}, u32[]{:S(2)}, u32[]{:S(2)}) %collective-permute-start.5) | collective-permute-done | bytes 524320 | tf_op jit(solution)/shard_map/ppermute | solution.py:345
  44.5 1.6 %collective-permute-done.4.relay_ref = bf16[512,512]{1,0:T(8,128)(2,1)S(1)} collective-permute-done((bf16[512,512]{1,0:T(8,128)(2,1)S(1)}, bf16[512,512]{1,0:T(8,128)(2,1)S(1)}, u32[]{:S(2)}, u32[]{:S(2)}) %collective-permute-start.4) | collective-permute-done | bytes 524320 | tf_op jit(solution)/shard_map/ppermute | solution.py:347
  46.1 1.0 %shard_map.43 = bf16[1024,512]{1,0:T(8,128)(2,1)} custom-call(f32[1024,512]{1,0:T(8,128)S(1)} %shard_map.42.total_ref, bf16[512,512]{1,0:T(8,128)(2,1)S(1)} %collective-permute-done.3.first_ref, bf16[512,512]{1,0:T(8,128)(2,1)S(1)} %collective-permute-done.4.relay_ref, bf16[512,512]{1,0:T(8,128)(2,1)S(1)} %collective-permute-done.5.second_ref), custom_call_target="tpu_custom_call" | custom-call | tf_op jit(solution)/shard_map/pallas_call | solution.py:374
Async XLA Ops:
  0.0 17.3 %collective-permute-start.2 = (bf16[1024,512]{1,0:T(8,128)(2,1)}, bf16[1024,512]{1,0:T(8,128)(2,1)S(1)}, u32[]{:S(2)}, u32[]{:S(2)}) collective-permute-start(bf16[1024,512]{1,0:T(8,128)(2,1)} %whole_ref.1), channel_id=1, source_target_pairs={{8,0},{10,2},{12,4},{14,6},{16,8},{1,9},{18,10},{3,11},{20,12},{5,... | collective-permute-start | bytes 3145736 | tf_op jit(solution)/shard_map/ppermute | solution.py:315
  14.5 22.4 %collective-permute-start.1 = (bf16[4,512,512]{2,1,0:T(8,128)(2,1)S(1)}, bf16[4,512,512]{2,1,0:T(8,128)(2,1)S(1)}, u32[]{:S(2)}, u32[]{:S(2)}) collective-permute-start(bf16[4,512,512]{2,1,0:T(8,128)(2,1)S(1)} %get-tuple-element.26), channel_id=1, source_target_pairs={{1,0},{0,1},{3,2},{2,3},{5,4},{4,5},{7,6},{6,7},{9,8},{8,9},{11,10... | collective-permute-start | bytes 6291464 | tf_op jit(solution)/shard_map/ppermute | solution.py:346
  15.4 21.5 %collective-permute-start = (bf16[1024,512]{1,0:T(8,128)(2,1)S(1)}, bf16[1024,512]{1,0:T(8,128)(2,1)S(1)}, u32[]{:S(2)}, u32[]{:S(2)}) collective-permute-start(bf16[1024,512]{1,0:T(8,128)(2,1)S(1)} %get-tuple-element.25.kept_ref.psi_ref), channel_id=1, source_target_pairs={{9,0},{11,2},{13,4},{15,6},{17,8},{0,9},{19,10},{2,11},{21,12},{4,... | collective-permute-start | bytes 3145736 | tf_op jit(solution)/shard_map/ppermute | solution.py:326
  21.8 13.8 %collective-permute-start.3 = (bf16[512,512]{1,0:T(8,128)(2,1)S(1)}, bf16[512,512]{1,0:T(8,128)(2,1)S(1)}, u32[]{:S(2)}, u32[]{:S(2)}) collective-permute-start(bf16[512,512]{1,0:T(8,128)(2,1)S(1)} %get-tuple-element.34.after_ref), channel_id=1, source_target_pairs={{2,1},{4,0},{6,5},{9,10},{10,9},{11,15},{12,8},{13,14},{14,13},{17... | collective-permute-start | bytes 1572872 | tf_op jit(solution)/shard_map/ppermute | solution.py:336
  27.8 16.6 %collective-permute-start.5 = (bf16[512,512]{1,0:T(8,128)(2,1)S(1)}, bf16[512,512]{1,0:T(8,128)(2,1)S(1)}, u32[]{:S(2)}, u32[]{:S(2)}) collective-permute-start(bf16[512,512]{1,0:T(8,128)(2,1)S(1)} %get-tuple-element.38.after_ref), channel_id=1, source_target_pairs={{2,1},{4,3},{6,5},{9,10},{10,9},{11,12},{12,11},{13,14},{14,13},{1... | collective-permute-start | bytes 1572872 | tf_op jit(solution)/shard_map/ppermute | solution.py:345
  35.6 10.5 %collective-permute-start.4 = (bf16[512,512]{1,0:T(8,128)(2,1)S(1)}, bf16[512,512]{1,0:T(8,128)(2,1)S(1)}, u32[]{:S(2)}, u32[]{:S(2)}) collective-permute-start(bf16[512,512]{1,0:T(8,128)(2,1)S(1)} %collective-permute-done.3.first_ref), channel_id=1, source_target_pairs={{0,3},{15,12},{8,11},{23,20},{16,19},{31,28}} | collective-permute-start | bytes 1572872 | tf_op jit(solution)/shard_map/ppermute | solution.py:347

commit v12 on v10

--- a/solution.py
+++ b/solution.py
@@ -76,7 +76,7 @@
 
 def spare_copies(left_ref, right_ref, left_target, right_target, step, half, sems):
     channel, part = local_channel(step), left_target.shape[0]
-    rows = pl.ds(half * part, part)
+    rows = pl.ds(half * (left_ref.shape[1] - part), part)
     return [
         pltpu.make_async_copy(left_ref.at[channel, rows, :], left_target, sems.at[0]),
         pltpu.make_async_copy(right_ref.at[channel], right_target, sems.at[1]),
@@ -218,7 +218,8 @@
     @pl.when(more)
     def _():
         wait(spare)
-        total_ref[part:, :] += contract(spare_left_ref[...], psi_ref[...], spare_right_ref[...])
+        total_ref[total_ref.shape[0] - part:, :] += contract(
+            spare_left_ref[...], psi_ref[...], spare_right_ref[...])
 
 
 def late_kernel(moved_ref, upper_ref, lower_ref, across_ref, start_ref, total_ref):
@@ -306,7 +307,9 @@
     left_env = pltpu.with_memory_space_constraint(left_whole, pltpu.HBM)
     right_env = pltpu.with_memory_space_constraint(right_whole, pltpu.HBM)
     total_shape = pltpu.VMEM((rows, columns), f32)
-    spare = [pltpu.VMEM((part, rows), bf16), pltpu.VMEM((columns, columns), bf16)]
+    spare_rows = rows * 3 // 8
+    spare = lambda count: [
+        pltpu.VMEM((count, rows), bf16), pltpu.VMEM((columns, columns), bf16)]
     half_total = pltpu.VMEM((part, columns), f32)
     half_block = pltpu.VMEM((part, columns), bf16)
 
@@ -316,7 +319,7 @@
         functools.partial(local_kernel, right_count, local_first + 2),
         [in_smem, in_hbm, in_hbm, in_hbm],
         [total_shape, pltpu.VMEM((rows, columns), bf16), halves, halves, rights(charged_count), rights(charged_count)],
-        [lefts(local_first), rights(local_first), *spare,
+        [lefts(local_first), rights(local_first), *spare(spare_rows),
          sems(2 * local_first + 1 + 4 * charged_count), sems(2)],
         cost(local_first, rows, rows, columns),
     )(charged, pltpu.with_memory_space_constraint(psi, pltpu.HBM), left_env, right_env)
@@ -357,7 +360,7 @@
         functools.partial(tail_kernel, right_count, local_first + 2),
         [in_vmem] * 3 + [in_hbm, in_hbm, in_vmem, in_hbm],
         [total_shape],
-        [*spare, sems(2)],
+        [*spare(rows - spare_rows), sems(2)],
         cost(2, rows, rows, columns),
         aliases={5: 0},
     )(kept, rest_left, rest_right, left_env, right_env, total, second)

time: 46.8 us -> 46.6 us (level)
  no operation moved by 1% of the time
where the time goes in v12:
time: 46.6 us; the launch traced here: 46.4 us
  Pallas kernels  31.8 us (68%)
  starting transfers between devices  12.3 us (26%)
  waiting for transfers between devices  1.95 us (4%)
    pallas_call x1, Pallas kernels, shards(): call(functools.partial(local_kernel, right_count, local_first + 2), [in_s...  12.1 us
    pallas_call x1, Pallas kernels, shards(): call(late_kernel, [in_vmem] * 5, [total_shape], [], cost(charged_count, r...  6.67 us
    pallas_call x1, Pallas kernels, shards(): call(functools.partial(second_kernel, right_count, local_first + 1, local...  3.67 us
    ppermute x1, starting transfers between devices, shards(): moved_across = lax.ppermute(kept, axes, crossed)  3.63 us
    pallas_call x1, Pallas kernels, shards(): call(functools.partial(first_kernel, right_count, local_first + 2), [in_v...  3.46 us
    ppermute x1, starting transfers between devices, shards(): second_received = lax.ppermute(second, axes, along)  3.35 us
    pallas_call x1, Pallas kernels, shards(): call(functools.partial(tail_kernel, right_count, local_first + 2), [in_vm...  3.02 us
    ppermute x1, starting transfers between devices, shards(): moved = lax.ppermute(psi, axes, straight)  2.35 us
  transfers between devices with their start and end apart: 6, of which 1 were waited for; matrix products, arithmetic and copies ran while one was open for 0% of the time, Pallas kernels for 66%

profile of v12, /device:TPU:20, one launch (start us, length us, event | category | flops | bytes accessed | tf_op | source)
XLA Modules:
  0.0 46.4 jit_solution(970485270130869875)
XLA Ops:
  0.0 2.3 %collective-permute-start.2 = (bf16[1024,512]{1,0:T(8,128)(2,1)}, bf16[1024,512]{1,0:T(8,128)(2,1)S(1)}, u32[]{:S(2)}, u32[]{:S(2)}) collective-permute-start(bf16[1024,512]{1,0:T(8,128)(2,1)} %whole_ref.1), channel_id=1, source_target_pairs={{8,0},{10,2},{12,4},{14,6},{16,8},{1,9},{18,10},{3,11},{20,12},{5,... | collective-permute-start | bytes 3145736 | tf_op jit(solution)/shard_map/ppermute | solution.py:316
  2.4 12.1 %shard_map.37 = (f32[1024,512]{1,0:T(8,128)S(1)}, bf16[1024,512]{1,0:T(8,128)(2,1)S(1)}, bf16[4,512,1024]{2,1,0:T(8,128)(2,1)S(1)}, bf16[4,512,1024]{2,1,0:T(8,1...) custom-call(s32[1]{0:T(128)} %bitcast.charged_ref, bf16[1024,512]{1,0:T(8,128)(2,1)} %whole_ref.1, ...), custom_call_target="tpu_custom_call" | custom-call | flops 8053063680 | bytes 13107200 | tf_op jit(solution)/shard_map/pallas_call | solution.py:318
  14.5 0.1 collective-permute-start.1
  14.6 3.6 %collective-permute-start = (bf16[1024,512]{1,0:T(8,128)(2,1)S(1)}, bf16[1024,512]{1,0:T(8,128)(2,1)S(1)}, u32[]{:S(2)}, u32[]{:S(2)}) collective-permute-start(bf16[1024,512]{1,0:T(8,128)(2,1)S(1)} %get-tuple-element.27.kept_ref.psi_ref), channel_id=1, source_target_pairs={{9,0},{11,2},{13,4},{15,6},{17,8},{0,9},{19,10},{2,11},{21,12},{4,... | collective-permute-start | bytes 3145736 | tf_op jit(solution)/shard_map/ppermute | solution.py:327
  18.2 0.0 collective-permute-done.2.psi_ref
  18.2 3.5 %shard_map.38 = (bf16[512,512]{1,0:T(8,128)(2,1)S(1)}, f32[1024,512]{1,0:T(8,128)S(1)}) custom-call(bf16[1024,512]{1,0:T(8,128)(2,1)S(1)} %get-tuple-element.27.kept_ref.psi_ref, bf16[1024,512]{1,0:T(8,128)(2,1)S(1)} %collective-permute-done.2.psi_ref, ...), custom_call_target="tpu_custom_call", output_to_operand_aliasing={{1}: (6, {})} | custom-call | flops 3221225472 | bytes 6291456 | tf_op jit(solution)/shard_map/pallas_call | solution.py:329
  21.7 1.6 %collective-permute-start.3 = (bf16[512,512]{1,0:T(8,128)(2,1)S(1)}, bf16[512,512]{1,0:T(8,128)(2,1)S(1)}, u32[]{:S(2)}, u32[]{:S(2)}) collective-permute-start(bf16[512,512]{1,0:T(8,128)(2,1)S(1)} %get-tuple-element.36.after_ref), channel_id=1, source_target_pairs={{2,1},{4,0},{6,5},{9,10},{10,9},{11,15},{12,8},{13,14},{14,13},{17... | collective-permute-start | bytes 1572872 | tf_op jit(solution)/shard_map/ppermute | solution.py:337
  23.3 3.7 %shard_map.39 = (bf16[512,512]{1,0:T(8,128)(2,1)S(1)}, f32[1024,512]{1,0:T(8,128)S(1)}, bf16[1,1024,1024]{2,1,0:T(8,128)(2,1)S(1)}, bf16[1,512,512]{2,1,0:T(8,128)(2,1)S(1)}) custom-call(bf16[1024,512]{1,0:T(8,128)(2,1)S(1)} %get-tuple-element.27.kept_ref.psi_ref, ...), custom_call_target="tpu_custom_call", output_to_operand_aliasing={{1}: (6, {})} | custom-call | flops 3221225472 | bytes 6291456 | tf_op jit(solution)/shard_map/pallas_call | solution.py:338
  27.0 3.4 %collective-permute-start.5 = (bf16[512,512]{1,0:T(8,128)(2,1)S(1)}, bf16[512,512]{1,0:T(8,128)(2,1)S(1)}, u32[]{:S(2)}, u32[]{:S(2)}) collective-permute-start(bf16[512,512]{1,0:T(8,128)(2,1)S(1)} %get-tuple-element.40.after_ref), channel_id=1, source_target_pairs={{2,1},{4,3},{6,5},{9,10},{10,9},{11,12},{12,11},{13,14},{14,13},{1... | collective-permute-start | bytes 1572872 | tf_op jit(solution)/shard_map/ppermute | solution.py:346
  30.4 1.8 %shard_map.40 = (f32[1024,512]{1,0:T(8,128)S(1)}, bf16[1,1024,1024]{2,1,0:T(8,128)(2,1)S(1)}, bf16[1,512,512]{2,1,0:T(8,128)(2,1)S(1)}) custom-call(bf16[1024,512]{1,0:T(8,128)(2,1)S(1)} %get-tuple-element.27.kept_ref.psi_ref, bf16[1,1024,1024]{2,1,0:T(8,128)(2,1)S(1)} %get-tuple-element.37.left0_ref, ...), custom_call_target="tpu_custom_call", output_to_operand_aliasing={{0}: (5, {})} | custom-call | flops 1610612736 | bytes 2621440 | tf_op jit(solution)/shard_map/pallas_call | solution.py:348
  32.2 0.0 collective-permute-done.3.first_ref
  32.2 1.3 %collective-permute-start.4 = (bf16[512,512]{1,0:T(8,128)(2,1)S(1)}, bf16[512,512]{1,0:T(8,128)(2,1)S(1)}, u32[]{:S(2)}, u32[]{:S(2)}) collective-permute-start(bf16[512,512]{1,0:T(8,128)(2,1)S(1)} %collective-permute-done.3.first_ref), channel_id=1, source_target_pairs={{0,3},{15,12},{8,11},{23,20},{16,19},{31,28}} | collective-permute-start | bytes 1572872 | tf_op jit(solution)/shard_map/ppermute | solution.py:357
  33.5 3.0 %shard_map.41.start_ref = f32[1024,512]{1,0:T(8,128)S(1)} custom-call(bf16[1024,512]{1,0:T(8,128)(2,1)S(1)} %get-tuple-element.27.kept_ref.psi_ref, bf16[1,1024,1024]{2,1,0:T(8,128)(2,1)S(1)} %get-tuple-element.41.left0_ref, bf16[1,512,512]{2,1,0:T(8,128)(2,1)S(1)} %get-tuple-element.42.right0_ref, ...), custom_call_target="tpu_custom_call", output_to_operand_aliasing={{}: (5, {})} | custom-call | flops 3221225472 | bytes 5242880 | tf_op jit(solution)/shard_map/pallas_call | solution.py:359
  36.5 0.0 collective-permute-done.moved_ref
  36.6 0.0 collective-permute-done.1.across_ref
  36.6 6.7 %shard_map.42.total_ref = f32[1024,512]{1,0:T(8,128)S(1)} custom-call(bf16[1024,512]{1,0:T(8,128)(2,1)S(1)} %collective-permute-done.moved_ref, bf16[4,512,1024]{2,1,0:T(8,128)(2,1)S(1)} %get-tuple-element.33.lefts_ref.upper_ref, bf16[4,512,1024]{2,1,0:T(8,128)(2,1)S(1)} %get-tuple-element.31.lefts_ref.lower_ref, ...), custom_call_target="tpu_custom_call", output_to_operand_aliasing={{}: (4, {})} | custom-call | flops 6442450944 | bytes 10485760 | tf_op jit(solution)/shard_map/pallas_call | solution.py:368
  43.2 0.0 collective-permute-done.5.second_ref
  43.3 1.9 %collective-permute-done.4.relay_ref = bf16[512,512]{1,0:T(8,128)(2,1)S(1)} collective-permute-done((bf16[512,512]{1,0:T(8,128)(2,1)S(1)}, bf16[512,512]{1,0:T(8,128)(2,1)S(1)}, u32[]{:S(2)}, u32[]{:S(2)}) %collective-permute-start.4) | collective-permute-done | bytes 524320 | tf_op jit(solution)/shard_map/ppermute | solution.py:357
  45.2 1.0 %shard_map.43 = bf16[1024,512]{1,0:T(8,128)(2,1)} custom-call(f32[1024,512]{1,0:T(8,128)S(1)} %shard_map.42.total_ref, bf16[512,512]{1,0:T(8,128)(2,1)S(1)} %collective-permute-done.3.first_ref, bf16[512,512]{1,0:T(8,128)(2,1)S(1)} %collective-permute-done.4.relay_ref, bf16[512,512]{1,0:T(8,128)(2,1)S(1)} %collective-permute-done.5.second_ref), custom_call_target="tpu_custom_call" | custom-call | tf_op jit(solution)/shard_map/pallas_call | solution.py:376
Async XLA Ops:
  0.0 18.2 %collective-permute-start.2 = (bf16[1024,512]{1,0:T(8,128)(2,1)}, bf16[1024,512]{1,0:T(8,128)(2,1)S(1)}, u32[]{:S(2)}, u32[]{:S(2)}) collective-permute-start(bf16[1024,512]{1,0:T(8,128)(2,1)} %whole_ref.1), channel_id=1, source_target_pairs={{8,0},{10,2},{12,4},{14,6},{16,8},{1,9},{18,10},{3,11},{20,12},{5,... | collective-permute-start | bytes 3145736 | tf_op jit(solution)/shard_map/ppermute | solution.py:316
  14.5 22.1 %collective-permute-start.1 = (bf16[4,512,512]{2,1,0:T(8,128)(2,1)S(1)}, bf16[4,512,512]{2,1,0:T(8,128)(2,1)S(1)}, u32[]{:S(2)}, u32[]{:S(2)}) collective-permute-start(bf16[4,512,512]{2,1,0:T(8,128)(2,1)S(1)} %get-tuple-element.28), channel_id=1, source_target_pairs={{1,0},{0,1},{3,2},{2,3},{5,4},{4,5},{7,6},{6,7},{9,8},{8,9},{11,10... | collective-permute-start | bytes 6291464 | tf_op jit(solution)/shard_map/ppermute | solution.py:347
  14.6 22.0 %collective-permute-start = (bf16[1024,512]{1,0:T(8,128)(2,1)S(1)}, bf16[1024,512]{1,0:T(8,128)(2,1)S(1)}, u32[]{:S(2)}, u32[]{:S(2)}) collective-permute-start(bf16[1024,512]{1,0:T(8,128)(2,1)S(1)} %get-tuple-element.27.kept_ref.psi_ref), channel_id=1, source_target_pairs={{9,0},{11,2},{13,4},{15,6},{17,8},{0,9},{19,10},{2,11},{21,12},{4,... | collective-permute-start | bytes 3145736 | tf_op jit(solution)/shard_map/ppermute | solution.py:327
  21.7 10.5 %collective-permute-start.3 = (bf16[512,512]{1,0:T(8,128)(2,1)S(1)}, bf16[512,512]{1,0:T(8,128)(2,1)S(1)}, u32[]{:S(2)}, u32[]{:S(2)}) collective-permute-start(bf16[512,512]{1,0:T(8,128)(2,1)S(1)} %get-tuple-element.36.after_ref), channel_id=1, source_target_pairs={{2,1},{4,0},{6,5},{9,10},{10,9},{11,15},{12,8},{13,14},{14,13},{17... | collective-permute-start | bytes 1572872 | tf_op jit(solution)/shard_map/ppermute | solution.py:337
  27.0 16.2 %collective-permute-start.5 = (bf16[512,512]{1,0:T(8,128)(2,1)S(1)}, bf16[512,512]{1,0:T(8,128)(2,1)S(1)}, u32[]{:S(2)}, u32[]{:S(2)}) collective-permute-start(bf16[512,512]{1,0:T(8,128)(2,1)S(1)} %get-tuple-element.40.after_ref), channel_id=1, source_target_pairs={{2,1},{4,3},{6,5},{9,10},{10,9},{11,12},{12,11},{13,14},{14,13},{1... | collective-permute-start | bytes 1572872 | tf_op jit(solution)/shard_map/ppermute | solution.py:346
  32.2 13.0 %collective-permute-start.4 = (bf16[512,512]{1,0:T(8,128)(2,1)S(1)}, bf16[512,512]{1,0:T(8,128)(2,1)S(1)}, u32[]{:S(2)}, u32[]{:S(2)}) collective-permute-start(bf16[512,512]{1,0:T(8,128)(2,1)S(1)} %collective-permute-done.3.first_ref), channel_id=1, source_target_pairs={{0,3},{15,12},{8,11},{23,20},{16,19},{31,28}} | collective-permute-start | bytes 1572872 | tf_op jit(solution)/shard_map/ppermute | solution.py:357
